TPU v7x, 32 devices: a whole 2x2x4 slice. The times are simulated.
32 devices in a mesh: scan: 2 (over x), seq: 16 (over z, y, core).
Axes of the slice: x: 2, y: 2, z: 4, core: 2. Of those that a mesh axis runs over, the one named last changes fastest.
Arguments:
- tokens: bfloat16 [8192, 1024], P(('scan', 'seq')), parts along dimension 0, may hold values from -12 to 12
- ln_gain: float32 [1024], replicated, may hold values from 0.1 to 1.9
- w_query: bfloat16 [1024, 1024], P('seq'), may hold values from -2 to 2
- w_key: bfloat16 [1024, 1024], P('seq'), may hold values from -2 to 2
- w_value: bfloat16 [1024, 1024], P('seq'), may hold values from -0.1875 to 0.1875
- w_out: bfloat16 [1024, 1024], P('seq'), may hold values from -0.1875 to 0.1875
- probe_gain: float32 [1024], replicated, may hold values from 0.1 to 1.9
- probe_queries: bfloat16 [256, 1024], replicated, may hold values from -46 to 46
- key_blocks: int32 [64, 8], P('scan'), parts along dimension 0, may hold values from 0 to 31, as said below
- key_counts: int32 [64], P('scan'), parts along dimension 0, may hold values from 1 to 8, as said below
Outputs:
- layer_out: bfloat16 [8192, 1024], P(('scan', 'seq')), parts along dimension 0
- probe_out: float32 [512, 1024], P(('scan', 'seq')), parts along dimension 0
There are 2 independent parts, one for each index of `scan`. A program takes and returns all parts, laid end to end along the dimension named above; an argument that names none is the same for every part. Nothing has to cross between parts.
Inputs may be any that keep to these rules, and one draw needn't show every extreme that they name: `key_blocks`: entry 0 of each query block's list is that block itself; the entries of one list are different blocks. Entries at or after key_counts are ignored. `key_counts`: some block uses all 8 entries in every draw.
All inputs are finite; a program needn't handle non-finite values.
Results may differ from a plain program's by a relative error of at most 0.0061.
Values may be sent and summed in bfloat16 or wider, within the bound.
No kernel may reach another device: no remote copies, remote signals or barrier semaphores. Data moves between devices by JAX's collectives and lax.ppermute only.
A program may use at most 64 MiB of HBM per device.

v0:
```python
import math

import jax
import jax.numpy as jnp
from jax import lax
from jax.sharding import PartitionSpec as P

D = 1024
HEADS = 16
HEAD_DIM = 64
PROBES = 256
BLOCK = 128
MAXK = 8
TOK_DEV = 256


EPS = 1e-05


def layer_norm(values, gain):
    wide = values.astype(jnp.float32)
    center = wide - jnp.mean(wide, axis=-1, keepdims=True)
    spread = jnp.mean(center * center, axis=-1, keepdims=True)
    return (center * lax.rsqrt(spread + EPS) * gain).astype(jnp.bfloat16)


def widen_heads(factor):
    return jnp.repeat(jnp.transpose(factor), HEAD_DIM, axis=1)


def per_device(
    tokens,
    ln_gain,
    w_query,
    w_key,
    w_value,
    w_out,
    probe_gain,
    probe_queries,
    key_blocks,
    key_counts,
):
    scale = 1.0 / math.sqrt(HEAD_DIM)
    ranks = lax.axis_size("seq")
    group = ranks // HEADS
    piece_rows = TOK_DEV // group
    myself = lax.axis_index("seq")
    quarter = myself % group
    normed = layer_norm(tokens, ln_gain)
    columns = normed
    query = jnp.dot(
        columns,
        lax.all_gather(w_query, "seq", axis=0, tiled=True),
        preferred_element_type=jnp.float32,
    )
    keys = jnp.dot(
        columns,
        lax.all_gather(w_key, "seq", axis=0, tiled=True),
        preferred_element_type=jnp.float32,
    )
    values = jnp.dot(
        columns,
        lax.all_gather(w_value, "seq", axis=0, tiled=True),
        preferred_element_type=jnp.float32,
    )
    query = query.astype(jnp.bfloat16)
    pairs = jnp.concatenate(
        [
            keys.astype(jnp.bfloat16).reshape(TOK_DEV, HEADS, HEAD_DIM),
            values.astype(jnp.bfloat16).reshape(TOK_DEV, HEADS, HEAD_DIM),
        ],
        axis=2,
    )
    query_send = jnp.transpose(
        query.reshape(group, piece_rows, HEADS, HEAD_DIM), (2, 0, 1, 3)
    ).reshape(ranks, piece_rows * HEAD_DIM)
    pair_send = jnp.repeat(
        jnp.transpose(pairs, (1, 0, 2)).reshape(HEADS, TOK_DEV * 2 * HEAD_DIM), group, axis=0
    )
    query_got, pair_got = (
        lax.all_to_all(query_send, "seq", split_axis=0, concat_axis=0, tiled=True),
        lax.all_to_all(pair_send, "seq", split_axis=0, concat_axis=0, tiled=True),
    )
    pair_all = pair_got.reshape(ranks * TOK_DEV, 2 * HEAD_DIM)
    blocks_total = ranks * TOK_DEV // BLOCK
    pair_grid = pair_all.reshape(blocks_total, BLOCK, 2 * HEAD_DIM)
    unit = min(piece_rows, BLOCK)
    per_piece = piece_rows // unit
    units = ranks * per_piece
    unit_ids = jnp.arange(units, dtype=jnp.int32)
    starts = unit_ids // per_piece * TOK_DEV + quarter * piece_rows + unit_ids % per_piece * unit
    block_ids = starts // BLOCK
    unit_lists = key_blocks[block_ids]
    unit_counts = key_counts[block_ids]
    per_batch = min(units, max(1, 1024 // unit))
    batches = units // per_batch
    query_units = query_got.reshape(batches, per_batch, unit, HEAD_DIM)
    slot_of = jnp.arange(MAXK * BLOCK, dtype=jnp.int32) // BLOCK

    def attend_batch(operands):
        batch_query, batch_lists, batch_counts = operands
        picked = pair_grid[batch_lists].reshape(per_batch, MAXK * BLOCK, 2 * HEAD_DIM)
        batch_keys = picked[:, :, :HEAD_DIM]
        batch_values = picked[:, :, HEAD_DIM:]
        scores = (
            jnp.einsum("uqd,ukd->uqk", batch_query, batch_keys, preferred_element_type=jnp.float32)
            * scale
        )
        valid = slot_of[None, :] < batch_counts[:, None]
        scores = jnp.where(valid[:, None, :], scores, -jnp.inf)
        top = jnp.max(scores, axis=-1, keepdims=True)
        weights = jnp.exp(scores - top)
        total = jnp.sum(weights, axis=-1, keepdims=True)
        mixed = jnp.einsum(
            "uqk,ukd->uqd",
            weights.astype(jnp.bfloat16),
            batch_values,
            preferred_element_type=jnp.float32,
        )
        return (mixed / total).astype(jnp.bfloat16)

    attended_heads = lax.map(
        attend_batch,
        (
            query_units,
            unit_lists.reshape(batches, per_batch, MAXK),
            unit_counts.reshape(batches, per_batch),
        ),
    )
    returned = lax.all_to_all(
        attended_heads.reshape(ranks, piece_rows * HEAD_DIM),
        "seq",
        split_axis=0,
        concat_axis=0,
        tiled=True,
    )
    attended = jnp.transpose(
        returned.reshape(HEADS, group, piece_rows, HEAD_DIM), (1, 2, 0, 3)
    ).reshape(TOK_DEV, D)
    columns = attended
    projected = jnp.dot(
        columns,
        lax.all_gather(w_out, "seq", axis=0, tiled=True),
        preferred_element_type=jnp.float32,
    )
    layer_out = (tokens.astype(jnp.float32) + projected).astype(jnp.bfloat16)
    pooled = layer_norm(layer_out, probe_gain)
    pooled_heads = pooled.reshape(TOK_DEV, HEADS, HEAD_DIM)
    probe_heads = probe_queries.reshape(PROBES, HEADS, HEAD_DIM)
    probe_scores = (
        jnp.einsum("phd,nhd->hpn", probe_heads, pooled_heads, preferred_element_type=jnp.float32)
        * scale
    )
    pooled_wide = pooled_heads.astype(jnp.float32)
    own_top = jnp.max(probe_scores, axis=-1)
    top = lax.pmax(own_top, "seq")
    weights = jnp.exp(probe_scores - top[:, :, None])
    own_total = jnp.sum(weights, axis=-1)
    own_acc = jnp.einsum(
        "hpn,nhd->phd", weights, pooled_wide, precision=lax.Precision.HIGHEST
    ).reshape(PROBES, D)
    total, accum = lax.psum((own_total, own_acc), "seq")
    probe_all = accum / widen_heads(total)
    share = PROBES // ranks
    probe_out = lax.dynamic_slice_in_dim(probe_all, myself * share, share, 0)
    return (layer_out, probe_out)


def solution(mesh):
    return jax.shard_map(
        per_device,
        mesh=mesh,
        in_specs=(
            P(("scan", "seq"), None),
            P(),
            P("seq", None),
            P("seq", None),
            P("seq", None),
            P("seq", None),
            P(),
            P(),
            P("scan", None),
            P("scan"),
        ),
        out_specs=(P(("scan", "seq"), None), P(("scan", "seq"), None)),
        check_vma=False,
    )
```

profile of v0, /device:TPU:0, one launch (start us, length us, event | category | flops | bytes accessed | tf_op | source)
XLA Modules:
  0.0 426.0 jit_solution(11318317714799748280)
XLA Ops:
  7.2 0.7 all-gather.5.cloned.1.call-update
  8.0 0.7 all-gather.7.cloned.1.call-update
  8.7 0.7 all-gather.9.cloned.1.call-update
  9.4 1.2 convert_reduce_fusion
  10.6 1.3 fusion.54
  11.9 42.4 %all-gather.5.cloned.1.call-done = bf16[1024,1024]{1,0:T(8,128)(2,1)} async-done(((bf16[64,1024]{1,0:T(8,128)(2,1)}), bf16[1024,1024]{1,0:T(8,128)(2,1)}) %all-gather.5.cloned.1.call-update) | async-done | bytes 2097168 | tf_op jit(solution)/shard_map/all_gather | solution.py:53
  54.3 2.5 convolution_convert_fusion.2
  57.6 0.7 all_to_all.24
  58.7 3.8 reduce.3
  62.6 1.2 reshape.298
  63.8 4.4 %all-to-all-start = ((bf16[16,2,8192]{2,1,0:T(2,128)(2,1)}), bf16[16,2,8192]{2,1,0:T(2,128)(2,1)}, u32[]{:S(2)}, u32[]{:S(2)}) async-start(bf16[16,2,8192]{2,1,0:T(2,128)(2,1)} %reshape.298), calls=%async_computation | async-start | bytes 1048576 | tf_op jit(solution)/shard_map/all_to_all | solution.py:81
  68.2 30.9 %all-gather.7.cloned.1.call-done = bf16[1024,1024]{1,0:T(8,128)(2,1)} async-done(((bf16[64,1024]{1,0:T(8,128)(2,1)}), bf16[1024,1024]{1,0:T(8,128)(2,1)}) %all-gather.7.cloned.1.call-update) | async-done | bytes 2097168 | tf_op jit(solution)/shard_map/all_gather | solution.py:58
  99.1 2.4 convolution_convert_fusion.1
  101.7 39.8 %all-gather.9.cloned.1.call-done = bf16[1024,1024]{1,0:T(8,128)(2,1)} async-done(((bf16[64,1024]{1,0:T(8,128)(2,1)}), bf16[1024,1024]{1,0:T(8,128)(2,1)}) %all-gather.9.cloned.1.call-update) | async-done | bytes 2097168 | tf_op jit(solution)/shard_map/all_gather | solution.py:63
  141.5 2.4 convolution_convert_fusion
  144.1 0.7 copy.59
  145.3 7.2 %reduce.4 = bf16[16,32768]{1,0:T(8,128)(2,1)S(1)} reduce(bf16[16,1,32768]{2,1,0:T(2,128)(2,1)S(1)} %all_to_all.25, bf16[]{:T(256)} %broadcast.287), dimensions={1}, to_apply=%all_to_all.25.reduce_sub_computation | reduce | bytes 2097154 | tf_op jit(solution)/shard_map/all_to_all | solution.py:82
  152.6 1.6 reshape.300
  154.2 3.7 all-to-all-start.1
  158.5 0.6 gather_fusion.2
  159.1 0.7 gather_fusion.1
  159.9 2.6 reshape.299
  162.5 3.3 reduce
  165.8 1.1 reshape.255
  167.0 1.1 copy.61
  168.1 15.3 %all-to-all-done.1 = bf16[16,2,16384]{2,1,0:T(2,128)(2,1)S(1)} async-done(((bf16[16,2,16384]{2,1,0:T(2,128)(2,1)}), bf16[16,2,16384]{2,1,0:T(2,128)(2,1)S(1)}, u32[]{:S(2)}, u32[]{:S(2)}) %all-to-all-start.1) | async-done | bytes 1048608 | tf_op jit(solution)/shard_map/all_to_all | solution.py:82
  183.4 1.0 reshape.301
  184.5 6.7 %reduce.1 = bf16[16,32768]{1,0:T(8,128)(2,1)S(1)} reduce(bf16[16,1,32768]{2,1,0:T(2,128)(2,1)S(1)} %reshape.301, bf16[]{:T(256)} %constant.115), dimensions={1}, to_apply=%all_to_all.21.reduce_sub_computation | reduce | bytes 2097154 | tf_op jit(solution)/shard_map/all_to_all | solution.py:82
  191.2 0.5 reshape_reshape.3
  191.7 27.2 %while.11 = (s32[]{:T(128)}, bf16[4,8,128,64]{2,3,1,0:T(8,128)(2,1)}, s32[4,8]{1,0:T(4,128)S(1)}, bf16[4,8,128,64]{2,3,1,0:T(8,128)(2,1)}, s32[4,8,8]{2,1,0:T(8,...) while((s32[]{:T(128)}, bf16[4,8,128,64]{2,3,1,0:T(8,128)(2,1)}, s32[4,8]{1,0:T(4,128)S(1)}, ...), condition=%wide.region_5.6_spmd.clone, body=%wide.region_2.5_spmd.clone.sunk | while | flops 280116416 | bytes 21301940 | solution.py:122
  192.0 1.0 gather_fusion
  193.1 1.8 fusion.85
  194.8 1.1 fusion.86
  195.9 2.7 fusion.87
  198.7 1.0 gather_fusion
  199.8 1.8 fusion.85
  201.6 1.1 fusion.86
  202.7 2.7 fusion.87
  205.5 1.0 gather_fusion
  206.6 1.8 fusion.85
  208.3 1.1 fusion.86
  209.4 2.7 fusion.87
  212.2 1.0 gather_fusion
  213.3 1.8 fusion.85
  215.1 1.1 fusion.86
  216.2 2.7 fusion.87
  218.9 1.6 copy.62
  220.5 0.7 all_to_all.26
  221.2 3.8 reduce.5
  225.0 1.2 reshape.302
  226.2 8.5 %all-to-all-start.2 = ((bf16[16,2,8192]{2,1,0:T(2,128)(2,1)}), bf16[16,2,8192]{2,1,0:T(2,128)(2,1)S(1)}, u32[]{:S(2)}, u32[]{:S(2)}) async-start(bf16[16,2,8192]{2,1,0:T(2,128)(2,1)} %reshape.302), calls=%async_computation.2 | async-start | bytes 1048576 | tf_op jit(solution)/shard_map/all_to_all | solution.py:130
  235.0 14.2 %all-to-all-done.2 = bf16[16,2,8192]{2,1,0:T(2,128)(2,1)S(1)} async-done(((bf16[16,2,8192]{2,1,0:T(2,128)(2,1)}), bf16[16,2,8192]{2,1,0:T(2,128)(2,1)S(1)}, u32[]{:S(2)}, u32[]{:S(2)}) %all-to-all-start.2) | async-done | bytes 524320 | tf_op jit(solution)/shard_map/all_to_all | solution.py:130
  249.2 0.7 reshape.303
  249.9 3.3 reduce.2
  253.2 1.1 reshape.259
  254.8 2.4 convert_reduce_fusion.1
  258.0 2.7 bitcast_reduce_fusion
  260.7 60.1 %pmax.7 = f32[16,256]{1,0:T(8,128)S(1)} all-reduce(f32[16,256]{1,0:T(8,128)S(1)} %get-tuple-element.94), channel_id=1, replica_groups=mesh['scan'=2,'seq'=16] {'seq'}, use_global_device_ids=true, to_apply=%region_9.10 | all-reduce | flops 4096 | bytes 32768 | tf_op jit(solution)/shard_map/pmax | solution.py:156
  320.8 5.4 %fusion.45 = f32[16,64,256]{2,1,0:T(8,128)} fusion(bf16[256,16,64]{0,2,1:T(8,128)(2,1)S(1)} %bitcast.70, f32[16,256,256]{2,1,0:T(8,128)} %get-tuple-element.95, f32[16,256]{1,0:T(8,128)S(1)} %pmax.7), kind=kOutput, calls=%fused_computation.42 | convolution fusion | flops 807403520 | bytes 5783552 | tf_op jit(solution)/shard_map/hpn,nhd->phd/dot_general | solution.py:159
  326.3 2.9 fusion.44
  329.2 58.0 %psum.15 = f32[256,16]{0,1:T(8,128)S(1)} all-reduce(f32[256,16]{0,1:T(8,128)S(1)} %bitcast.80), channel_id=1, replica_groups=mesh['scan'=2,'seq'=16] {'seq'}, use_global_device_ids=true, to_apply=%region_12.13 | all-reduce | flops 4096 | bytes 32768 | tf_op jit(solution)/shard_map/psum | solution.py:162
  387.3 29.7 %all-reduce.2.cloned.1.call-done = f32[256,1024]{0,1:T(8,128)} async-done(((f32[256,1024]{0,1:T(8,128)}), f32[256,1024]{0,1:T(8,128)}) %all-reduce.2.cloned.1.call-update) | async-done | bytes 1048592 | tf_op jit(solution)/shard_map/psum | solution.py:162
  417.0 1.4 dynamic-slice_divide_fusion
  418.4 0.8 copy.68
  (71 shorter events, 5.3 us)
Async XLA Ops:
  7.2 152.0 %copy-start = (s32[32]{0:T(128)S(1)}, s32[32]{0:T(128)}, u32[]{:S(2)}) copy-start(s32[32]{0:T(128)} %param.21) | copy-start | bytes 388
  7.2 47.1 %all-gather.5.cloned.1.call-start = ((), (), s32[]{:S(2)}) async-start(), calls=%async_computation.3 | async-start | bytes 2228224 | tf_op jit(solution)/shard_map/all_gather | solution.py:53
  7.9 91.2 %all-gather.7.cloned.1.call-start = ((), (), s32[]{:S(2)}) async-start(), calls=%async_computation.4 | async-start | bytes 2228224 | tf_op jit(solution)/shard_map/all_gather | solution.py:58
  8.7 132.8 %all-gather.9.cloned.1.call-start = ((), (), s32[]{:S(2)}) async-start(), calls=%async_computation.5 | async-start | bytes 2228224 | tf_op jit(solution)/shard_map/all_gather | solution.py:63
  56.9 42.3 %copy-start.1 = (bf16[256,1024]{1,0:T(8,128)(2,1)S(1)}, bf16[256,1024]{1,0:T(8,128)(2,1)}, u32[]{:S(2)}) copy-start(bf16[256,1024]{1,0:T(8,128)(2,1)} %param.12) | copy-start | bytes 1572868
  56.9 42.2 %copy-start.7 = (f32[1024]{0:T(1024)S(1)}, f32[1024]{0:T(1024)}, u32[]{:S(2)}) copy-start(f32[1024]{0:T(1024)} %param.13) | copy-start | bytes 12292
  63.8 90.4 %all-to-all-start = ((bf16[16,2,8192]{2,1,0:T(2,128)(2,1)}), bf16[16,2,8192]{2,1,0:T(2,128)(2,1)}, u32[]{:S(2)}, u32[]{:S(2)}) async-start(bf16[16,2,8192]{2,1,0:T(2,128)(2,1)} %reshape.298), calls=%async_computation | async-start | bytes 1048576 | tf_op jit(solution)/shard_map/all_to_all | solution.py:81
  145.3 13.1 %copy-start.6 = (s32[32,8]{0,1:T(8,128)S(1)}, s32[32,8]{0,1:T(8,128)}, u32[]{:S(2)}) copy-start(s32[32,8]{0,1:T(8,128)} %param.20) | copy-start | bytes 3076
  154.2 29.3 %all-to-all-start.1 = ((bf16[16,2,16384]{2,1,0:T(2,128)(2,1)}), bf16[16,2,16384]{2,1,0:T(2,128)(2,1)S(1)}, u32[]{:S(2)}, u32[]{:S(2)}) async-start(bf16[16,2,16384]{2,1,0:T(2,128)(2,1)} %reshape.300), calls=%async_computation.1 | async-start | bytes 2097152 | tf_op jit(solution)/shard_map/all_to_all | solution.py:82
  157.8 96.9 %all-gather.11.cloned.1.call-start = ((), (), s32[]{:S(2)}) async-start(), calls=%async_computation.6 | async-start | bytes 2228224 | tf_op jit(solution)/shard_map/all_gather | solution.py:143
  218.9 15.9 %copy-start.4 = (bf16[256,1024]{1,0:T(8,128)(2,1)S(1)}, bf16[256,1024]{1,0:T(8,128)(2,1)}, u32[]{:S(2)}) copy-start(bf16[256,1024]{1,0:T(8,128)(2,1)} %param.19) | copy-start | bytes 1572868
  226.2 28.6 %copy-start.2 = (bf16[256,1024]{1,0:T(8,128)(2,1)S(1)}, bf16[256,1024]{1,0:T(8,128)(2,1)}, u32[]{:S(2)}) copy-start(bf16[256,1024]{1,0:T(8,128)(2,1)} %param.12) | copy-start | bytes 1572868
  226.2 23.0 %all-to-all-start.2 = ((bf16[16,2,8192]{2,1,0:T(2,128)(2,1)}), bf16[16,2,8192]{2,1,0:T(2,128)(2,1)S(1)}, u32[]{:S(2)}, u32[]{:S(2)}) async-start(bf16[16,2,8192]{2,1,0:T(2,128)(2,1)} %reshape.302), calls=%async_computation.2 | async-start | bytes 1048576 | tf_op jit(solution)/shard_map/all_to_all | solution.py:130
  234.7 182.2 %all-reduce.2.cloned.1.call-start = ((), (), s32[]{:S(2)}) async-start(), calls=%async_computation.7 | async-start | bytes 2097152 | tf_op jit(solution)/shard_map/psum | solution.py:162
  249.9 7.6 %copy-start.5 = (f32[1024]{0:T(1024)S(1)}, f32[1024]{0:T(1024)}, u32[]{:S(2)}) copy-start(f32[1024]{0:T(1024)} %param.18) | copy-start | bytes 12292
  257.2 69.1 %copy-start.3 = (bf16[256,1024]{1,0:T(8,128)(2,1)}, bf16[256,1024]{1,0:T(8,128)(2,1)S(1)}, u32[]{:S(2)}) copy-start(bf16[256,1024]{1,0:T(8,128)(2,1)S(1)} %get-tuple-element.93) | copy-start | bytes 1572868
Sparse Core Ops, SparseCore 0:
  10.2 44.0 all-gather.4
  56.5 42.5 all-gather.6
  101.3 40.1 all-gather.8
  160.5 48.5 all-gather.10
  326.4 90.4 all-reduce.1
where the time goes:
time: 432 us; the launch traced here: 426 us
  waiting for transfers between devices  175 us (41%)
  blocking collectives  118 us (27%)
  other arithmetic  40.5 us (9%)
  matrix products  35.7 us (8%)
  local copies, waits for them, and re-layouts  25.2 us (6%)
  starting transfers between devices  16.8 us (4%)
  between operations  14.4 us (3%)
    pmax x1, blocking collectives, per_device(): top = lax.pmax(own_top, 'seq')  60.1 us
    psum x1, blocking collectives, per_device(): total, accum = lax.psum((own_total, own_acc), 'seq')  58 us
    all_gather x1, waiting for transfers between devices, per_device(): lax.all_gather(w_query, 'seq', axis=0, tiled=True)  42.4 us
    all_gather x1, waiting for transfers between devices, per_device(): lax.all_gather(w_value, 'seq', axis=0, tiled=True)  39.8 us
    all_gather x1, waiting for transfers between devices, per_device(): lax.all_gather(w_key, 'seq', axis=0, tiled=True)  30.9 us
    psum x1, waiting for transfers between devices, per_device(): total, accum = lax.psum((own_total, own_acc), 'seq')  29.7 us
    all_to_all x1, waiting for transfers between devices, per_device(): lax.all_to_all(pair_send, 'seq', split_axis=0, concat_axis=0, tiled=True)  15.3 us
    all_to_all x1, waiting for transfers between devices, per_device(): lax.all_to_all(attended_heads.reshape(ranks, piece_rows * HEAD_DIM), 'seq...  14.2 us
  transfers between devices with their start and end apart: 8, of which 6 were waited for; matrix products, arithmetic and copies ran while one was open for 20% of the time, Pallas kernels for 0%

commit v1 on v0

v1 whole, which is shorter than its diff:
```python
import functools
import math

import jax
import jax.numpy as jnp
from jax import lax
from jax.experimental import pallas as pl
from jax.experimental.pallas import tpu as pltpu
from jax.sharding import PartitionSpec as P

D = 1024
HEADS = 16
HEAD_DIM = 64
PROBES = 256
BLOCK = 128
MAXK = 8
TOK_DEV = 256
STATS = 128
EPS = 1e-05
SCALE = 1.0 / math.sqrt(HEAD_DIM)
EXP2_SCALE = SCALE / math.log(2.0)
BF16 = jnp.bfloat16
F32 = jnp.float32
NT = (((1,), (1,)), ((), ()))
VMEM_BYTES = 40 * 1024 * 1024


def whole():
    return pl.BlockSpec(memory_space=pltpu.VMEM)


def scalars():
    return pl.BlockSpec(memory_space=pltpu.SMEM)


def params():
    return pltpu.CompilerParams(vmem_limit_bytes=VMEM_BYTES)


def layer_norm(values, gain):
    wide = values.astype(F32)
    center = wide - jnp.mean(wide, axis=-1, keepdims=True)
    spread = jnp.mean(center * center, axis=-1, keepdims=True)
    return (center * lax.rsqrt(spread + EPS) * gain).astype(BF16)


def head_masked(block, heads):
    if heads == 1:
        return block
    lanes = lax.broadcasted_iota(jnp.int32, block.shape, 1) // HEAD_DIM
    zero = jnp.zeros_like(block)
    return jnp.concatenate([jnp.where(lanes == h, block, zero) for h in range(heads)], axis=0)


def project_kernel(count, width, *refs):
    inputs, (gain_ref, weight_ref, query_ref, pair_ref) = refs[:count], refs[count:]
    at = 0
    for ref in inputs:
        rows = ref.shape[0]
        normed = layer_norm(ref[...], gain_ref[...])
        result = jnp.dot(normed, weight_ref[...], preferred_element_type=F32)
        query_ref[at : at + rows, :] = result[:, :width].astype(BF16)
        pair_ref[at : at + rows, :] = result[:, width:].astype(BF16)
        at += rows


def project(pieces, gain, weight, width):
    rows = sum(p.shape[0] for p in pieces)
    return pl.pallas_call(
        functools.partial(project_kernel, len(pieces), width),
        out_shape=(
            jax.ShapeDtypeStruct((rows, width), BF16),
            jax.ShapeDtypeStruct((rows, 2 * width), BF16),
        ),
        in_specs=[whole()] * (len(pieces) + 2),
        out_specs=(whole(), whole()),
        compiler_params=params(),
        name="project",
    )(*pieces, gain, weight)


def attend_kernel(chips, group, heads, sizes, place_ref, lists_ref, counts_ref, *refs):
    n = len(sizes)
    width = heads * HEAD_DIM
    queries, own, other = refs[:n], refs[n : 2 * n], refs[2 * n : 3 * n]
    outs = refs[3 * n : 3 * n + chips]
    q_all, k_all, vt_all, mixed = refs[3 * n + chips :]
    chip, core, member = place_ref[0], place_ref[1], place_ref[2]
    blocks = TOK_DEV // BLOCK
    piece = TOK_DEV // group
    shard = 0
    for i, size in enumerate(sizes):
        for t in range(size):
            owner = place_ref[3 + shard]
            shard += 1
            for u in range(blocks):
                lo = t * TOK_DEV + u * BLOCK
                q_all[owner * blocks + u] = queries[i][lo : lo + BLOCK, :]
                for ref, side in ((own, core), (other, 1 - core)):
                    block = (owner * 2 + side) * blocks + u
                    pair = ref[i][lo : lo + BLOCK, :]
                    k_all[block] = pair[:, :width]
                    vt_all[block] = jnp.transpose(pair[:, width:].astype(F32)).astype(BF16)
    per_piece = piece // BLOCK

    def one_unit(index, carry):
        step = index // per_piece
        part = index % per_piece
        target = lax.bitwise_xor(chip, step)
        within = member * per_piece + part
        block = (target * 2 + core) * blocks + within
        count = counts_ref[block]
        for used in range(1, MAXK + 1):

            @pl.when(count == used)
            def _(used=used):
                picked = [lists_ref[block, s] for s in range(used)]
                stacked = head_masked(q_all[target * blocks + within], heads)
                keys = jnp.concatenate([k_all[p] for p in picked], axis=0)
                scores = lax.dot_general(keys, stacked, NT, preferred_element_type=F32)
                top = jnp.max(scores, axis=0, keepdims=True)
                weights = jnp.exp2((scores - top) * EXP2_SCALE)
                total = jnp.sum(weights, axis=0, keepdims=True)
                values = jnp.concatenate([vt_all[p] for p in picked], axis=1)
                full = jnp.dot(values, weights.astype(BF16), preferred_element_type=F32)
                full = full / total
                result = jnp.concatenate(
                    [
                        full[h * HEAD_DIM : (h + 1) * HEAD_DIM, h * BLOCK : (h + 1) * BLOCK]
                        for h in range(heads)
                    ],
                    axis=0,
                )
                mixed[index] = jnp.transpose(result).astype(BF16)

        return carry

    lax.fori_loop(0, chips * per_piece, one_unit, 0)
    for k in range(chips):
        for part in range(per_piece):
            outs[k][part * BLOCK : (part + 1) * BLOCK, :] = mixed[k * per_piece + part]


def attend(place, lists, counts, queries, own, other, chips, group, heads):
    sizes = tuple(q.shape[0] // TOK_DEV for q in queries)
    width = heads * HEAD_DIM
    piece = TOK_DEV // group
    blocks = TOK_DEV // BLOCK
    n = len(sizes)
    return pl.pallas_call(
        functools.partial(attend_kernel, chips, group, heads, sizes),
        out_shape=[jax.ShapeDtypeStruct((piece, width), BF16)] * chips,
        in_specs=[scalars()] * 3 + [whole()] * (3 * n),
        out_specs=[whole()] * chips,
        scratch_shapes=[
            pltpu.VMEM((chips * blocks, BLOCK, width), BF16),
            pltpu.VMEM((2 * chips * blocks, BLOCK, width), BF16),
            pltpu.VMEM((2 * chips * blocks, width, BLOCK), BF16),
            pltpu.VMEM((chips * (piece // BLOCK), BLOCK, width), BF16),
        ],
        compiler_params=params(),
        name="attend",
    )(place, lists, counts, *queries, *own, *other)


def tail_kernel(chips, group, heads, split, place_ref, *refs):
    width = heads * HEAD_DIM
    sets = HEADS // heads
    piece = TOK_DEV // group
    got = refs[:chips]
    weight_ref, tokens_ref, gain_ref, probe_ref, layer_ref = refs[chips : chips + 5]
    part_refs, (stage,) = refs[chips + 5 : -1], refs[-1:]
    chip, core = place_ref[0], place_ref[1]
    for k in range(chips):
        source = lax.bitwise_xor(chip, k)
        if group == 1:
            stage[source] = got[k][...]
        else:
            stage[source // group, pl.ds(pl.multiple_of(source % group * piece, piece), piece), :] = got[k][...]
    attended = jnp.concatenate([stage[s] for s in range(sets)], axis=1)
    projected = jnp.dot(attended, weight_ref[...], preferred_element_type=F32)
    layer = (tokens_ref[...].astype(F32) + projected).astype(BF16)
    layer_ref[...] = layer
    pooled = layer_norm(layer, gain_ref[...])
    rows = []

    def emit(lo, value):
        hi = lo + value.shape[1]
        if not split:
            part_refs[0][:, lo:hi] = value.astype(BF16)
            return
        share = PROBES // (2 * chips)
        shaped = value.reshape(chips, 2, share, value.shape[1])
        first, second = shaped[:, 0], shaped[:, 1]
        mine = jnp.where(core == 0, first, second)
        theirs = jnp.where(core == 0, second, first)
        part_refs[0][:, lo:hi] = mine.reshape(chips * share, -1).astype(BF16)
        part_refs[1][:, lo:hi] = theirs.reshape(chips * share, -1).astype(BF16)

    for pair in range(HEADS // 2):
        lo = pair * 2 * HEAD_DIM
        own = pooled[:, lo : lo + 2 * HEAD_DIM]
        stacked = head_masked(probe_ref[:, lo : lo + 2 * HEAD_DIM], 2)
        scores = lax.dot_general(own, stacked, NT, preferred_element_type=F32)
        top = jnp.max(scores, axis=0, keepdims=True)
        weights = jnp.exp2((scores - top) * EXP2_SCALE)
        total = jnp.sum(weights, axis=0, keepdims=True)
        flipped = jnp.transpose(own.astype(F32)).astype(BF16)
        full = jnp.dot(flipped, weights.astype(BF16), preferred_element_type=F32) / total
        result = jnp.concatenate([full[:HEAD_DIM, :PROBES], full[HEAD_DIM:, PROBES:]], axis=0)
        emit(lo, jnp.transpose(result))
        logs = top * SCALE + jnp.log(total)
        rows += [logs[:, :PROBES], logs[:, PROBES:]]
    logs = jnp.concatenate(rows, axis=0)
    high = logs.astype(BF16).astype(F32)
    middle = (logs - high).astype(BF16).astype(F32)
    low = logs - high - middle
    rest = jnp.zeros((STATS - 3 * HEADS, PROBES), F32)
    emit(D, jnp.transpose(jnp.concatenate([high, middle, low, rest], axis=0)))


def tail(place, got, weight, tokens, gain, probes, chips, group, heads, split):
    width = heads * HEAD_DIM
    rows = PROBES // 2 if split else PROBES
    return pl.pallas_call(
        functools.partial(tail_kernel, chips, group, heads, split),
        out_shape=[jax.ShapeDtypeStruct((TOK_DEV, D), BF16)]
        + [jax.ShapeDtypeStruct((rows, D + STATS), BF16)] * (2 if split else 1),
        in_specs=[scalars()] + [whole()] * (chips + 4),
        out_specs=[whole()] * (3 if split else 2),
        scratch_shapes=[pltpu.VMEM((HEADS // heads, TOK_DEV, width), BF16)],
        compiler_params=params(),
        name="tail",
    )(place, *got, weight, tokens, gain, probes)


def read_logs(block):
    pick = lax.broadcasted_iota(jnp.int32, (STATS, STATS), 0)
    head = lax.broadcasted_iota(jnp.int32, (STATS, STATS), 1)
    gather = ((pick < 3 * HEADS) & (pick % HEADS == head)).astype(BF16)
    return jnp.dot(block, gather, preferred_element_type=F32)


def spread_heads(factors):
    row = lax.broadcasted_iota(jnp.int32, (STATS, D), 0)
    lane = lax.broadcasted_iota(jnp.int32, (STATS, D), 1)
    widen = (lane // HEAD_DIM == row).astype(F32)
    return jnp.dot(factors, widen, preferred_element_type=F32, precision=lax.Precision.HIGHEST)


def blend(blocks):
    logs = [read_logs(b[:, D:]) for b in blocks]
    top = functools.reduce(jnp.maximum, logs)
    shares = [jnp.exp(one - top) for one in logs]
    total = functools.reduce(jnp.add, shares)
    rows = blocks[0].shape[0]
    wide = spread_heads(jnp.concatenate([s / total for s in shares], axis=0))
    value = 0.0
    for i, b in enumerate(blocks):
        value = value + wide[i * rows : (i + 1) * rows] * b[:, :D].astype(F32)
    return value, top + jnp.log(total)


def pair_kernel(chips, place_ref, mine_ref, got_ref, *outs_and_stage):
    outs, stage = outs_and_stage[:-1], outs_and_stage[-1]
    value, logs = blend([mine_ref[...], got_ref[...]])
    high = logs.astype(BF16).astype(F32)
    middle = (logs - high).astype(BF16).astype(F32)
    low = logs - high - middle
    rest = jnp.zeros((value.shape[0], STATS - 3 * HEADS), F32)
    packed = jnp.concatenate(
        [value, high[:, :HEADS], middle[:, :HEADS], low[:, :HEADS], rest], axis=1
    ).astype(BF16)
    share = value.shape[0] // chips
    stage[...] = packed.reshape(chips, share, D + STATS)
    for k in range(chips):
        outs[k][...] = stage[lax.bitwise_xor(place_ref[0], k)]


def pair_up(place, mine, got, chips):
    share = mine.shape[0] // chips
    return pl.pallas_call(
        functools.partial(pair_kernel, chips),
        out_shape=[jax.ShapeDtypeStruct((share, D + STATS), BF16)] * chips,
        in_specs=[scalars(), whole(), whole()],
        out_specs=[whole()] * chips,
        scratch_shapes=[pltpu.VMEM((chips, share, D + STATS), BF16)],
        compiler_params=params(),
        name="pair_up",
    )(place, mine, got)


def last_kernel(*refs):
    refs[-1][...] = blend([r[...] for r in refs[:-1]])[0]


def join(parts):
    return pl.pallas_call(
        last_kernel,
        out_shape=jax.ShapeDtypeStruct((parts[0].shape[0], D), F32),
        in_specs=[whole()] * len(parts),
        out_specs=whole(),
        compiler_params=params(),
        name="join",
    )(*parts)


def per_device(
    tokens,
    ln_gain,
    w_query,
    w_key,
    w_value,
    w_out,
    probe_gain,
    probe_queries,
    key_blocks,
    key_counts,
):
    ranks = lax.axis_size("seq")
    chips = ranks // 2
    heads = max(1, HEADS // chips)
    group = max(1, chips // HEADS)
    sets = HEADS // heads
    width = heads * HEAD_DIM
    myself = lax.axis_index("seq")
    chip, core = myself // 2, myself % 2
    order = list(range(0, chips, 2)) + list(range(chips - 1, 0, -2))
    swap = [(i, i ^ 1) for i in range(ranks)]
    same_core = [[2 * c + k for c in range(chips)] for k in range(2)]

    def around(shift):
        return [
            (order[i] * 2 + k, order[(i + shift) % chips] * 2 + k)
            for i in range(chips)
            for k in range(2)
        ]

    def across(k):
        return [(2 * c + q, 2 * (c ^ k) + q) for c in range(chips) for q in range(2)]

    depth = w_query.shape[0]
    cut = jnp.stack([w_query, w_key, w_value]).reshape(3, depth, sets, width)
    cut = jnp.transpose(cut, (2, 1, 0, 3)).reshape(sets, depth, 3 * width)
    if group > 1:
        cut = jnp.repeat(cut, group, axis=0)
    here = lax.all_to_all(
        cut, "seq", split_axis=0, concat_axis=0, tiled=True, axis_index_groups=same_core
    )
    there = lax.ppermute(here, "seq", swap)
    even = jnp.where(core == 0, here, there)
    odd = jnp.where(core == 0, there, here)
    weight = jnp.stack([even, odd], axis=1).reshape(D, 3 * width)
    out_weight = lax.all_gather(w_out, "seq", axis=0, tiled=True)

    gain = ln_gain.reshape(1, D)
    steps = [[tokens]]
    forward = backward = tokens
    for s in range(1, chips // 2):
        forward = lax.ppermute(forward, "seq", around(1))
        backward = lax.ppermute(backward, "seq", around(-1))
        steps.append([forward, backward])
    half = TOK_DEV // 2
    steps.append(
        [
            lax.ppermute(forward[:half], "seq", around(1)),
            lax.ppermute(backward[half:], "seq", around(-1)),
        ]
    )
    queries, own, other = [], [], []
    for pieces in steps:
        query, pair = project(pieces, gain, weight, width)
        queries.append(query)
        own.append(pair)
        other.append(lax.ppermute(pair, "seq", swap))

    position = jnp.array([order.index(c) for c in range(chips)], jnp.int32)[chip]
    offsets = [0]
    for s in range(1, chips // 2):
        offsets += [-s, s]
    offsets.append(chips // 2)
    owners = jnp.array(order, jnp.int32)[(position + jnp.array(offsets, jnp.int32)) % chips]
    place = jnp.concatenate([jnp.stack([chip, core, chip % group]), owners]).astype(jnp.int32)

    attended = attend(place, key_blocks, key_counts, queries, own, other, chips, group, heads)
    got = [attended[0]] + [lax.ppermute(attended[k], "seq", across(k)) for k in range(1, chips)]

    share = PROBES // ranks
    split = share % 16 == 0
    layer_out, *parts = tail(
        place,
        got,
        out_weight,
        tokens,
        probe_gain.reshape(1, D),
        probe_queries,
        chips,
        group,
        heads,
        split,
    )
    if split:
        mine, theirs = parts
        pieces = pair_up(place, mine, lax.ppermute(theirs, "seq", swap), chips)
        joined = [pieces[0]] + [
            lax.ppermute(pieces[k], "seq", across(k)) for k in range(1, chips)
        ]
        return layer_out, join(joined)
    rows = lax.all_to_all(
        parts[0].reshape(ranks, share, D + STATS), "seq", split_axis=0, concat_axis=0, tiled=True
    ).astype(F32)
    logs = rows[:, :, D : D + 3 * HEADS].reshape(ranks, share, 3, HEADS).sum(axis=2)
    factors = jnp.exp(logs - jnp.max(logs, axis=0, keepdims=True))
    factors = factors / jnp.sum(factors, axis=0, keepdims=True)
    probe_out = jnp.sum(jnp.repeat(factors, HEAD_DIM, axis=2) * rows[:, :, :D], axis=0)
    return layer_out, probe_out


def solution(mesh):
    return jax.shard_map(
        per_device,
        mesh=mesh,
        in_specs=(
            P(("scan", "seq"), None),
            P(),
            P("seq", None),
            P("seq", None),
            P("seq", None),
            P("seq", None),
            P(),
            P(),
            P("scan", None),
            P("scan"),
        ),
        out_specs=(P(("scan", "seq"), None), P(("scan", "seq"), None)),
        check_vma=False,
    )
```

time: 432 us -> 147 us (0.34); the launches traced: 426 us -> 146 us
  waiting for transfers between devices: 175 us -> 43.2 us
  blocking collectives: 118 us -> 0 us
  other arithmetic: 40.5 us -> 2.81 us
  matrix products: 35.7 us -> 0 us
  starting transfers between devices: 16.8 us -> 49.3 us
  Pallas kernels: 0 us -> 24.6 us
  local copies, waits for them, and re-layouts: 25.2 us -> 11.4 us
    all_gather x4 -> x1, waiting for transfers between devices: 113 us -> 0.01 us  [per_device(): out_weight = lax.all_gather(w_out, 'seq', axis=0, tiled=True)]
    pmax x1 -> x0, blocking collectives: 60.1 us -> none  [per_device(): top = lax.pmax(own_top, 'seq')]
    psum x1 -> x0, blocking collectives: 58 us -> none  [per_device(): total, accum = lax.psum((own_total, own_acc), 'seq')]
    ppermute x0 -> x29, starting transfers between devices: none -> 43 us  [the longest x3 14 us: per_device(): forward = lax.ppermute(forward, 'seq', around(1))]
    dot_general x14 -> x0, matrix products: 35.7 us -> none  [the longest x4 10.9 us: attend_batch(): jnp.einsum('uqk,ukd->uqd', weights.astype(jnp.bfloat16), batch_values, pr...]
    ppermute x0 -> x29, waiting for transfers between devices: none -> 31.1 us  [the longest x3 18.6 us: per_device(): forward = lax.ppermute(forward, 'seq', around(1))]
    psum x1 -> x0, waiting for transfers between devices: 29.7 us -> none  [per_device(): total, accum = lax.psum((own_total, own_acc), 'seq')]
    all_to_all x6 -> x0, other arithmetic: 28.2 us -> none  [the longest x2 13.9 us: per_device(): lax.all_to_all(pair_send, 'seq', split_axis=0, concat_axis=0, tiled=True)]
  transfers between devices with their start and end apart: 8 -> 31, of which waited for: 6 -> 12; matrix products, arithmetic and copies ran while one was open for 20% -> 6% of each run, Pallas kernels for 0% -> 12%
where the time goes in v1:
time: 147 us; the launch traced here: 146 us
  starting transfers between devices  49.3 us (34%)
  waiting for transfers between devices  43.2 us (29%)
  Pallas kernels  24.6 us (17%)
  between operations  14.3 us (10%)
  local copies, waits for them, and re-layouts  11.4 us (8%)
  other arithmetic  2.81 us (2%)
    ppermute x3, waiting for transfers between devices, per_device(): forward = lax.ppermute(forward, 'seq', around(1))  18.6 us
    ppermute x3, starting transfers between devices, per_device(): forward = lax.ppermute(forward, 'seq', around(1))  14 us
    ppermute x7, starting transfers between devices, per_device(): lax.ppermute(pieces[k], 'seq', across(k))  12.5 us
    pallas_call x1, Pallas kernels, attend(): pl.pallas_call(functools.partial(attend_kernel, chips, group, heads, size...  11.9 us
    ppermute x7, starting transfers between devices, per_device(): lax.ppermute(attended[k], 'seq', across(k))  11.6 us
    all_to_all x1, waiting for transfers between devices, per_device(): lax.all_to_all(cut, 'seq', split_axis=0, concat_axis=0, tiled=True, axis_...  11.4 us
    unnamed x36, local copies, waits for them, and re-layouts  8.32 us
    all_to_all x1, starting transfers between devices, per_device(): lax.all_to_all(cut, 'seq', split_axis=0, concat_axis=0, tiled=True, axis_...  6.27 us
  transfers between devices with their start and end apart: 31, of which 12 were waited for; matrix products, arithmetic and copies ran while one was open for 6% of the time, Pallas kernels for 12%

profile of v1, /device:TPU:0, one launch (start us, length us, event | category | flops | bytes accessed | tf_op | source)
XLA Modules:
  0.0 145.7 jit_solution(3020026316857857020)
XLA Ops:
  7.2 0.7 all-gather.2.cloned.1.call-update
  7.9 3.1 %collective-permute-start.1 = (bf16[256,1024]{1,0:T(8,128)(2,1)}, bf16[256,1024]{1,0:T(8,128)(2,1)S(1)}, u32[]{:S(2)}, u32[]{:S(2)}) collective-permute-start(bf16[256,1024]{1,0:T(8,128)(2,1)} %refs_9_.1), channel_id=1, source_target_pairs={{0,4},{1,5},{4,8},{5,9},{8,12},{9,13},{12,14},{13,15},{14,10},{15,... | collective-permute-start | bytes 1572872 | tf_op jit(solution)/shard_map/ppermute | solution.py:360
  11.0 0.9 copy.25
  11.9 0.2 copy.20
  12.1 0.9 copy.24
  13.1 0.2 copy.19
  13.3 0.9 copy.23
  14.2 0.2 copy.18
  14.4 0.9 maximum_bitcast_fusion
  15.3 1.1 reshape.24
  16.4 6.3 %all-to-all-start = ((bf16[8,64,384]{2,1,0:T(8,128)(2,1)}), bf16[8,64,384]{2,1,0:T(8,128)(2,1)S(1)}, u32[]{:S(2)}, u32[]{:S(2)}) async-start(bf16[8,64,384]{2,1,0:T(8,128)(2,1)} %reshape.24), calls=%async_computation | async-start | bytes 786432 | tf_op jit(solution)/shard_map/all_to_all | solution.py:347
  22.7 2.0 %collective-permute-done.1.refs_0_ = bf16[256,1024]{1,0:T(8,128)(2,1)S(1)} collective-permute-done((bf16[256,1024]{1,0:T(8,128)(2,1)}, bf16[256,1024]{1,0:T(8,128)(2,1)S(1)}, u32[]{:S(2)}, u32[]{:S(2)}) %collective-permute-start.1) | collective-permute-done | bytes 524320 | tf_op jit(solution)/shard_map/ppermute | solution.py:360
  24.7 2.8 %collective-permute-start.3 = (bf16[256,1024]{1,0:T(8,128)(2,1)S(1)}, bf16[256,1024]{1,0:T(8,128)(2,1)S(1)}, u32[]{:S(2)}, u32[]{:S(2)}) collective-permute-start(bf16[256,1024]{1,0:T(8,128)(2,1)S(1)} %collective-permute-done.1.refs_0_), channel_id=1, source_target_pairs={{0,4},{1,5},{4,8},{5,9},{8,12},{9,13},{12,14},{13,15},{14,10},{15,... | collective-permute-start | bytes 1572872 | tf_op jit(solution)/shard_map/ppermute | solution.py:360
  27.5 0.2 collective-permute-start.4
  27.7 11.4 %all-to-all-done = bf16[8,64,384]{2,1,0:T(8,128)(2,1)S(1)} async-done(((bf16[8,64,384]{2,1,0:T(8,128)(2,1)}), bf16[8,64,384]{2,1,0:T(8,128)(2,1)S(1)}, u32[]{:S(2)}, u32[]{:S(2)}) %all-to-all-start) | async-done | bytes 393248 | tf_op jit(solution)/shard_map/all_to_all | solution.py:347
  39.1 9.0 %collective-permute-done.3.refs_0_ = bf16[256,1024]{1,0:T(8,128)(2,1)S(1)} collective-permute-done((bf16[256,1024]{1,0:T(8,128)(2,1)S(1)}, bf16[256,1024]{1,0:T(8,128)(2,1)S(1)}, u32[]{:S(2)}, u32[]{:S(2)}) %collective-permute-start.3) | collective-permute-done | bytes 524320 | tf_op jit(solution)/shard_map/ppermute | solution.py:360
  48.2 8.1 %collective-permute-start.5 = (bf16[256,1024]{1,0:T(8,128)(2,1)S(1)}, bf16[256,1024]{1,0:T(8,128)(2,1)S(1)}, u32[]{:S(2)}, u32[]{:S(2)}) collective-permute-start(bf16[256,1024]{1,0:T(8,128)(2,1)S(1)} %collective-permute-done.3.refs_0_), channel_id=1, source_target_pairs={{0,4},{1,5},{4,8},{5,9},{8,12},{9,13},{12,14},{13,15},{14,10},{15,... | collective-permute-start | bytes 1572872 | tf_op jit(solution)/shard_map/ppermute | solution.py:360
  56.3 0.6 dynamic_slice.3
  56.9 1.1 select_bitcast_fusion.1
  58.0 7.6 %collective-permute-done.5.refs_0_ = bf16[256,1024]{1,0:T(8,128)(2,1)S(1)} collective-permute-done((bf16[256,1024]{1,0:T(8,128)(2,1)S(1)}, bf16[256,1024]{1,0:T(8,128)(2,1)S(1)}, u32[]{:S(2)}, u32[]{:S(2)}) %collective-permute-start.5) | collective-permute-done | bytes 524320 | tf_op jit(solution)/shard_map/ppermute | solution.py:360
  65.5 2.8 %collective-permute-start.7 = (bf16[128,1024]{1,0:T(8,128)(2,1)S(1)}, bf16[128,1024]{1,0:T(8,128)(2,1)S(1)}, u32[]{:S(2)}, u32[]{:S(2)}) collective-permute-start(bf16[128,1024]{1,0:T(8,128)(2,1)S(1)} %slice.10), channel_id=1, source_target_pairs={{0,4},{1,5},{4,8},{5,9},{8,12},{9,13},{12,14},{13,15},{14,10},{15,... | collective-permute-start | bytes 786440 | tf_op jit(solution)/shard_map/ppermute | solution.py:366
  68.3 0.4 collective-permute-done.6.refs_1_
  68.7 0.6 collective-permute-start.8
  69.4 0.1 pad_maximum_fusion
  69.5 1.1 project.6
  70.8 1.1 project.7
  72.0 0.6 collective-permute-start.11
  72.5 1.1 project.8
  73.8 0.7 compare_select_fusion
  74.4 0.7 project.5
  75.2 0.6 copy-done.6
  75.8 0.5 collective-permute-start.9
  76.3 0.7 project.9
  77.1 0.6 copy-done.8
  77.8 0.6 gather_fusion
  78.5 0.5 collective-permute-done.13.refs_14_
  79.0 0.9 copy-done.4
  79.9 0.8 copy-done.7
  80.8 0.8 copy-done.9
  81.6 11.9 %attend.1 = (bf16[256,128]{1,0:T(8,128)(2,1)S(1)}, bf16[256,128]{1,0:T(8,128)(2,1)S(1)}, bf16[256,128]{1,0:T(8,128)(2,1)S(1)}, bf16[256,128]{1,0:T(8,128)(2,1)S(...) custom-call(s32[11]{0:T(128)S(1)} %pad_add_fusion.place_ref, ...), custom_call_target="tpu_custom_call" | custom-call | tf_op jit(solution)/shard_map/attend/pallas_call | solution.py:150
  93.5 2.1 %collective-permute-start.14 = (bf16[256,128]{1,0:T(8,128)(2,1)S(1)}, bf16[256,128]{1,0:T(8,128)(2,1)S(1)}, u32[]{:S(2)}, u32[]{:S(2)}) collective-permute-start(bf16[256,128]{1,0:T(8,128)(2,1)S(1)} %get-tuple-element.42), channel_id=1, source_target_pairs={{0,2},{1,3},{2,0},{3,1},{4,6},{5,7},{6,4},{7,5},{8,10},{9,11},{10,... | collective-permute-start | bytes 196616 | tf_op jit(solution)/shard_map/ppermute | solution.py:386
  95.6 1.9 %collective-permute-start.15 = (bf16[256,128]{1,0:T(8,128)(2,1)S(1)}, bf16[256,128]{1,0:T(8,128)(2,1)S(1)}, u32[]{:S(2)}, u32[]{:S(2)}) collective-permute-start(bf16[256,128]{1,0:T(8,128)(2,1)S(1)} %get-tuple-element.43), channel_id=1, source_target_pairs={{0,4},{1,5},{2,6},{3,7},{4,0},{5,1},{6,2},{7,3},{8,12},{9,13},{10,... | collective-permute-start | bytes 196616 | tf_op jit(solution)/shard_map/ppermute | solution.py:386
  97.4 2.6 %collective-permute-start.17 = (bf16[256,128]{1,0:T(8,128)(2,1)S(1)}, bf16[256,128]{1,0:T(8,128)(2,1)S(1)}, u32[]{:S(2)}, u32[]{:S(2)}) collective-permute-start(bf16[256,128]{1,0:T(8,128)(2,1)S(1)} %get-tuple-element.45), channel_id=1, source_target_pairs={{0,8},{1,9},{2,10},{3,11},{4,12},{5,13},{6,14},{7,15},{8,0},{9,1},... | collective-permute-start | bytes 196616 | tf_op jit(solution)/shard_map/ppermute | solution.py:386
  100.1 1.4 collective-permute-start.18
  101.4 1.3 collective-permute-start.19
  102.7 2.4 %collective-permute-start.20 = (bf16[256,128]{1,0:T(8,128)(2,1)S(1)}, bf16[256,128]{1,0:T(8,128)(2,1)S(1)}, u32[]{:S(2)}, u32[]{:S(2)}) collective-permute-start(bf16[256,128]{1,0:T(8,128)(2,1)S(1)} %get-tuple-element.48), channel_id=1, source_target_pairs={{0,14},{1,15},{2,12},{3,13},{4,10},{5,11},{6,8},{7,9},{8,6},{9,7},... | collective-permute-start | bytes 196616 | tf_op jit(solution)/shard_map/ppermute | solution.py:386
  105.1 1.5 collective-permute-done.17.refs_4_
  106.5 4.2 %collective-permute-done.18.refs_5_ = bf16[256,128]{1,0:T(8,128)(2,1)S(1)} collective-permute-done((bf16[256,128]{1,0:T(8,128)(2,1)S(1)}, bf16[256,128]{1,0:T(8,128)(2,1)S(1)}, u32[]{:S(2)}, u32[]{:S(2)}) %collective-permute-start.18) | collective-permute-done | bytes 65568 | tf_op jit(solution)/shard_map/ppermute | solution.py:386
  110.8 1.6 %copy-done.1 = bf16[1024,1024]{1,0:T(8,128)(2,1)S(1)} copy-done((bf16[1024,1024]{1,0:T(8,128)(2,1)S(1)}, bf16[1024,1024]{1,0:T(8,128)(2,1)}, u32[]{:S(2)}) %copy-start.1) | copy-done | bytes 2097176
  112.4 4.8 %tail.1 = (bf16[256,1024]{1,0:T(8,128)(2,1)}, bf16[128,1152]{1,0:T(8,128)(2,1)S(1)}, bf16[128,1152]{1,0:T(8,128)(2,1)S(1)}) custom-call(s32[11]{0:T(128)S(1)} %pad_add_fusion.place_ref, bf16[256,128]{1,0:T(8,128)(2,1)S(1)} %get-tuple-element.41.refs_0_, bf16[256,128]{1,0:T(8,128)(2,1)S(1)} %collective-permute-done.14.refs_1_, ...), custom_call_target="tpu_custom_call" | custom-call | tf_op jit(solution)/shard_map/tail/pallas_call | solution.py:225
  117.2 0.1 collective-permute-start.21
  117.3 1.5 %collective-permute-done.21.got_ref = bf16[128,1152]{1,0:T(8,128)(2,1)S(1)} collective-permute-done((bf16[128,1152]{1,0:T(8,128)(2,1)S(1)}, bf16[128,1152]{1,0:T(8,128)(2,1)S(1)}, u32[]{:S(2)}, u32[]{:S(2)}) %collective-permute-start.21) | collective-permute-done | bytes 294944 | tf_op jit(solution)/shard_map/ppermute | solution.py:404
  118.7 1.7 %pair_up.1 = (bf16[16,1152]{1,0:T(8,128)(2,1)S(1)}, bf16[16,1152]{1,0:T(8,128)(2,1)S(1)}, bf16[16,1152]{1,0:T(8,128)(2,1)S(1)}, bf16[16,1152]{1,0:T(8,128)(2,1)S...) custom-call(s32[11]{0:T(128)S(1)} %pad_add_fusion.place_ref, ...), custom_call_target="tpu_custom_call" | custom-call | tf_op jit(solution)/shard_map/pair_up/pallas_call | solution.py:282
  120.5 0.8 collective-permute-start.22
  121.3 3.1 %collective-permute-start.23 = (bf16[16,1152]{1,0:T(8,128)(2,1)S(1)}, bf16[16,1152]{1,0:T(8,128)(2,1)S(1)}, u32[]{:S(2)}, u32[]{:S(2)}) collective-permute-start(bf16[16,1152]{1,0:T(8,128)(2,1)S(1)} %get-tuple-element.54), channel_id=1, source_target_pairs={{0,4},{1,5},{2,6},{3,7},{4,0},{5,1},{6,2},{7,3},{8,12},{9,13},{10,... | collective-permute-start | bytes 110600 | tf_op jit(solution)/shard_map/ppermute | solution.py:406
  124.4 0.9 collective-permute-start.24
  125.3 2.0 %collective-permute-start.25 = (bf16[16,1152]{1,0:T(8,128)(2,1)S(1)}, bf16[16,1152]{1,0:T(8,128)(2,1)S(1)}, u32[]{:S(2)}, u32[]{:S(2)}) collective-permute-start(bf16[16,1152]{1,0:T(8,128)(2,1)S(1)} %get-tuple-element.56), channel_id=1, source_target_pairs={{0,8},{1,9},{2,10},{3,11},{4,12},{5,13},{6,14},{7,15},{8,0},{9,1},... | collective-permute-start | bytes 110600 | tf_op jit(solution)/shard_map/ppermute | solution.py:406
  127.3 1.1 collective-permute-start.26
  128.4 2.4 %collective-permute-start.27 = (bf16[16,1152]{1,0:T(8,128)(2,1)S(1)}, bf16[16,1152]{1,0:T(8,128)(2,1)S(1)}, u32[]{:S(2)}, u32[]{:S(2)}) collective-permute-start(bf16[16,1152]{1,0:T(8,128)(2,1)S(1)} %get-tuple-element.58), channel_id=1, source_target_pairs={{0,12},{1,13},{2,14},{3,15},{4,8},{5,9},{6,10},{7,11},{8,4},{9,5},... | collective-permute-start | bytes 110600 | tf_op jit(solution)/shard_map/ppermute | solution.py:406
  130.8 2.2 %collective-permute-start.28 = (bf16[16,1152]{1,0:T(8,128)(2,1)S(1)}, bf16[16,1152]{1,0:T(8,128)(2,1)S(1)}, u32[]{:S(2)}, u32[]{:S(2)}) collective-permute-start(bf16[16,1152]{1,0:T(8,128)(2,1)S(1)} %get-tuple-element.59), channel_id=1, source_target_pairs={{0,14},{1,15},{2,12},{3,13},{4,10},{5,11},{6,8},{7,9},{8,6},{9,7},... | collective-permute-start | bytes 110600 | tf_op jit(solution)/shard_map/ppermute | solution.py:406
  133.0 0.7 collective-permute-done.26.refs_5_
  133.7 0.8 collective-permute-done.27.refs_6_
  134.5 2.9 %collective-permute-done.28.refs_7_ = bf16[16,1152]{1,0:T(8,128)(2,1)S(1)} collective-permute-done((bf16[16,1152]{1,0:T(8,128)(2,1)S(1)}, bf16[16,1152]{1,0:T(8,128)(2,1)S(1)}, u32[]{:S(2)}, u32[]{:S(2)}) %collective-permute-start.28) | collective-permute-done | bytes 36896 | tf_op jit(solution)/shard_map/ppermute | solution.py:406
  137.4 1.4 join.1
  (59 shorter events, 0.6 us)
Async XLA Ops:
  7.2 103.6 %all-gather.2.cloned.1.call-start = ((), (), s32[]{:S(2)}) async-start(), calls=%async_computation.1 | async-start | bytes 2228224 | tf_op jit(solution)/shard_map/all_gather | solution.py:354
  7.9 16.8 %collective-permute-start.1 = (bf16[256,1024]{1,0:T(8,128)(2,1)}, bf16[256,1024]{1,0:T(8,128)(2,1)S(1)}, u32[]{:S(2)}, u32[]{:S(2)}) collective-permute-start(bf16[256,1024]{1,0:T(8,128)(2,1)} %refs_9_.1), channel_id=1, source_target_pairs={{0,4},{1,5},{4,8},{5,9},{8,12},{9,13},{12,14},{13,15},{14,10},{15,... | collective-permute-start | bytes 1572872 | tf_op jit(solution)/shard_map/ppermute | solution.py:360
  11.0 16.5 %collective-permute-start.2 = (bf16[256,1024]{1,0:T(8,128)(2,1)}, bf16[256,1024]{1,0:T(8,128)(2,1)S(1)}, u32[]{:S(2)}, u32[]{:S(2)}) collective-permute-start(bf16[256,1024]{1,0:T(8,128)(2,1)} %refs_9_.1), channel_id=1, source_target_pairs={{0,2},{1,3},{4,0},{5,1},{8,4},{9,5},{12,8},{13,9},{14,12},{15,13},... | collective-permute-start | bytes 1572872 | tf_op jit(solution)/shard_map/ppermute | solution.py:361
  13.1 43.2 %copy-start.15 = (s32[8]{0:T(128)S(1)}, s32[8]{0:T(128)}, u32[]{:S(2)}) copy-start(s32[8]{0:T(128)} %constant.62.clone) | copy-start | bytes 100
  16.4 22.7 %all-to-all-start = ((bf16[8,64,384]{2,1,0:T(8,128)(2,1)}), bf16[8,64,384]{2,1,0:T(8,128)(2,1)S(1)}, u32[]{:S(2)}, u32[]{:S(2)}) async-start(bf16[8,64,384]{2,1,0:T(8,128)(2,1)} %reshape.24), calls=%async_computation | async-start | bytes 786432 | tf_op jit(solution)/shard_map/all_to_all | solution.py:347
  24.7 23.5 %collective-permute-start.3 = (bf16[256,1024]{1,0:T(8,128)(2,1)S(1)}, bf16[256,1024]{1,0:T(8,128)(2,1)S(1)}, u32[]{:S(2)}, u32[]{:S(2)}) collective-permute-start(bf16[256,1024]{1,0:T(8,128)(2,1)S(1)} %collective-permute-done.1.refs_0_), channel_id=1, source_target_pairs={{0,4},{1,5},{4,8},{5,9},{8,12},{9,13},{12,14},{13,15},{14,10},{15,... | collective-permute-start | bytes 1572872 | tf_op jit(solution)/shard_map/ppermute | solution.py:360
  27.5 28.8 %collective-permute-start.4 = (bf16[256,1024]{1,0:T(8,128)(2,1)S(1)}, bf16[256,1024]{1,0:T(8,128)(2,1)S(1)}, u32[]{:S(2)}, u32[]{:S(2)}) collective-permute-start(bf16[256,1024]{1,0:T(8,128)(2,1)S(1)} %collective-permute-done.2.refs_1_), channel_id=1, source_target_pairs={{0,2},{1,3},{4,0},{5,1},{8,4},{9,5},{12,8},{13,9},{14,12},{15,13},... | collective-permute-start | bytes 1572872 | tf_op jit(solution)/shard_map/ppermute | solution.py:361
  39.1 17.7 %collective-permute-start = (bf16[8,64,384]{2,1,0:T(8,128)(2,1)S(1)}, bf16[8,64,384]{2,1,0:T(8,128)(2,1)}, u32[]{:S(2)}, u32[]{:S(2)}) collective-permute-start(bf16[8,64,384]{2,1,0:T(8,128)(2,1)S(1)} %all-to-all-done), channel_id=1, source_target_pairs={{0,1},{1,0},{2,3},{3,2},{4,5},{5,4},{6,7},{7,6},{8,9},{9,8},{10,11... | collective-permute-start | bytes 1179656 | tf_op jit(solution)/shard_map/ppermute | solution.py:350
  48.2 17.3 %collective-permute-start.5 = (bf16[256,1024]{1,0:T(8,128)(2,1)S(1)}, bf16[256,1024]{1,0:T(8,128)(2,1)S(1)}, u32[]{:S(2)}, u32[]{:S(2)}) collective-permute-start(bf16[256,1024]{1,0:T(8,128)(2,1)S(1)} %collective-permute-done.3.refs_0_), channel_id=1, source_target_pairs={{0,4},{1,5},{4,8},{5,9},{8,12},{9,13},{12,14},{13,15},{14,10},{15,... | collective-permute-start | bytes 1572872 | tf_op jit(solution)/shard_map/ppermute | solution.py:360
  56.3 12.4 %collective-permute-start.6 = (bf16[256,1024]{1,0:T(8,128)(2,1)S(1)}, bf16[256,1024]{1,0:T(8,128)(2,1)S(1)}, u32[]{:S(2)}, u32[]{:S(2)}) collective-permute-start(bf16[256,1024]{1,0:T(8,128)(2,1)S(1)} %collective-permute-done.4.refs_1_), channel_id=1, source_target_pairs={{0,2},{1,3},{4,0},{5,1},{8,4},{9,5},{12,8},{13,9},{14,12},{15,13},... | collective-permute-start | bytes 1572872 | tf_op jit(solution)/shard_map/ppermute | solution.py:361
  58.0 11.6 %copy-start.5 = (f32[1024]{0:T(1024)S(1)}, f32[1024]{0:T(1024)}, u32[]{:S(2)}) copy-start(f32[1024]{0:T(1024)} %param.14) | copy-start | bytes 12292
  65.5 10.3 %collective-permute-start.7 = (bf16[128,1024]{1,0:T(8,128)(2,1)S(1)}, bf16[128,1024]{1,0:T(8,128)(2,1)S(1)}, u32[]{:S(2)}, u32[]{:S(2)}) collective-permute-start(bf16[128,1024]{1,0:T(8,128)(2,1)S(1)} %slice.10), channel_id=1, source_target_pairs={{0,4},{1,5},{4,8},{5,9},{8,12},{9,13},{12,14},{13,15},{14,10},{15,... | collective-permute-start | bytes 786440 | tf_op jit(solution)/shard_map/ppermute | solution.py:366
  68.7 7.5 %collective-permute-start.8 = (bf16[128,1024]{1,0:T(8,128)(2,1)S(1)}, bf16[128,1024]{1,0:T(8,128)(2,1)S(1)}, u32[]{:S(2)}, u32[]{:S(2)}) collective-permute-start(bf16[128,1024]{1,0:T(8,128)(2,1)S(1)} %slice.11), channel_id=1, source_target_pairs={{0,2},{1,3},{4,0},{5,1},{8,4},{9,5},{12,8},{13,9},{14,12},{15,13},... | collective-permute-start | bytes 786440 | tf_op jit(solution)/shard_map/ppermute | solution.py:367
  70.7 3.1 %copy-start.14 = (s32[8]{0:T(128)S(1)}, s32[8]{0:T(128)}, u32[]{:S(2)}) copy-start(s32[8]{0:T(128)} %constant.64.clone) | copy-start | bytes 100
  70.7 3.7 %copy-start = (bf16[256,1024]{1,0:T(8,128)(2,1)S(1)}, bf16[256,1024]{1,0:T(8,128)(2,1)}, u32[]{:S(2)}) copy-start(bf16[256,1024]{1,0:T(8,128)(2,1)} %refs_9_.1) | copy-start | bytes 1572868
  70.7 7.8 %collective-permute-start.10 = (bf16[512,256]{1,0:T(8,128)(2,1)S(1)}, bf16[512,256]{1,0:T(8,128)(2,1)S(1)}, u32[]{:S(2)}, u32[]{:S(2)}) collective-permute-start(bf16[512,256]{1,0:T(8,128)(2,1)S(1)} %get-tuple-element.37.refs_6_), channel_id=1, source_target_pairs={{0,1},{1,0},{2,3},{3,2},{4,5},{5,4},{6,7},{7,6},{8,9},{9,8},{10,11... | collective-permute-start | bytes 786440 | tf_op jit(solution)/shard_map/ppermute | solution.py:375
  71.9 5.1 %copy-start.3 = (bf16[512,128]{1,0:T(8,128)(2,1)}, bf16[512,128]{1,0:T(8,128)(2,1)S(1)}, u32[]{:S(2)}) copy-start(bf16[512,128]{1,0:T(8,128)(2,1)S(1)} %get-tuple-element.33.refs_2_) | copy-start | bytes 393220
  71.9 5.8 %copy-start.13 = (s32[32,8]{0,1:T(8,128)S(1)}, s32[32,8]{0,1:T(8,128)}, u32[]{:S(2)}) copy-start(s32[32,8]{0,1:T(8,128)} %param.21) | copy-start | bytes 3076
  72.0 5.8 %copy-start.12 = (s32[8]{0:T(128)S(1)}, s32[8]{0:T(128)}, u32[]{:S(2)}) copy-start(s32[8]{0:T(128)} %constant.63.clone) | copy-start | bytes 100
  72.0 7.0 %copy-start.11 = (s32[32]{0:T(128)S(1)}, s32[32]{0:T(128)}, u32[]{:S(2)}) copy-start(s32[32]{0:T(128)} %counts_ref.1) | copy-start | bytes 388
  72.0 6.5 %collective-permute-start.11 = (bf16[512,256]{1,0:T(8,128)(2,1)S(1)}, bf16[512,256]{1,0:T(8,128)(2,1)S(1)}, u32[]{:S(2)}, u32[]{:S(2)}) collective-permute-start(bf16[512,256]{1,0:T(8,128)(2,1)S(1)} %get-tuple-element.38.refs_7_), channel_id=1, source_target_pairs={{0,1},{1,0},{2,3},{3,2},{4,5},{5,4},{6,7},{7,6},{8,9},{9,8},{10,11... | collective-permute-start | bytes 786440 | tf_op jit(solution)/shard_map/ppermute | solution.py:375
  73.7 4.8 %collective-permute-start.12 = (bf16[512,256]{1,0:T(8,128)(2,1)S(1)}, bf16[512,256]{1,0:T(8,128)(2,1)S(1)}, u32[]{:S(2)}, u32[]{:S(2)}) collective-permute-start(bf16[512,256]{1,0:T(8,128)(2,1)S(1)} %get-tuple-element.39.refs_8_), channel_id=1, source_target_pairs={{0,1},{1,0},{2,3},{3,2},{4,5},{5,4},{6,7},{7,6},{8,9},{9,8},{10,11... | collective-permute-start | bytes 786440 | tf_op jit(solution)/shard_map/ppermute | solution.py:375
  75.2 0.6 copy-start.6
  75.8 35.0 %copy-start.2 = (bf16[256,1024]{1,0:T(8,128)(2,1)S(1)}, bf16[256,1024]{1,0:T(8,128)(2,1)}, u32[]{:S(2)}) copy-start(bf16[256,1024]{1,0:T(8,128)(2,1)} %refs_11_.1) | copy-start | bytes 1572868
  75.8 35.0 %copy-start.10 = (f32[1024]{0:T(1024)S(1)}, f32[1024]{0:T(1024)}, u32[]{:S(2)}) copy-start(f32[1024]{0:T(1024)} %param.19) | copy-start | bytes 12292
  75.8 2.7 %collective-permute-start.9 = (bf16[256,256]{1,0:T(8,128)(2,1)S(1)}, bf16[256,256]{1,0:T(8,128)(2,1)S(1)}, u32[]{:S(2)}, u32[]{:S(2)}) collective-permute-start(bf16[256,256]{1,0:T(8,128)(2,1)S(1)} %get-tuple-element.36.refs_5_), channel_id=1, source_target_pairs={{0,1},{1,0},{2,3},{3,2},{4,5},{5,4},{6,7},{7,6},{8,9},{9,8},{10,11... | collective-permute-start | bytes 393224 | tf_op jit(solution)/shard_map/ppermute | solution.py:375
  77.0 0.6 copy-start.8
  77.7 1.3 collective-permute-start.13
  79.0 0.9 copy-start.4
  79.9 0.8 copy-start.7
  80.8 0.8 copy-start.9
  93.5 7.9 %collective-permute-start.14 = (bf16[256,128]{1,0:T(8,128)(2,1)S(1)}, bf16[256,128]{1,0:T(8,128)(2,1)S(1)}, u32[]{:S(2)}, u32[]{:S(2)}) collective-permute-start(bf16[256,128]{1,0:T(8,128)(2,1)S(1)} %get-tuple-element.42), channel_id=1, source_target_pairs={{0,2},{1,3},{2,0},{3,1},{4,6},{5,7},{6,4},{7,5},{8,10},{9,11},{10,... | collective-permute-start | bytes 196616 | tf_op jit(solution)/shard_map/ppermute | solution.py:386
  95.6 7.2 %collective-permute-start.15 = (bf16[256,128]{1,0:T(8,128)(2,1)S(1)}, bf16[256,128]{1,0:T(8,128)(2,1)S(1)}, u32[]{:S(2)}, u32[]{:S(2)}) collective-permute-start(bf16[256,128]{1,0:T(8,128)(2,1)S(1)} %get-tuple-element.43), channel_id=1, source_target_pairs={{0,4},{1,5},{2,6},{3,7},{4,0},{5,1},{6,2},{7,3},{8,12},{9,13},{10,... | collective-permute-start | bytes 196616 | tf_op jit(solution)/shard_map/ppermute | solution.py:386
  97.4 7.7 %collective-permute-start.16 = (bf16[256,128]{1,0:T(8,128)(2,1)S(1)}, bf16[256,128]{1,0:T(8,128)(2,1)S(1)}, u32[]{:S(2)}, u32[]{:S(2)}) collective-permute-start(bf16[256,128]{1,0:T(8,128)(2,1)S(1)} %get-tuple-element.44), channel_id=1, source_target_pairs={{0,6},{1,7},{2,4},{3,5},{4,2},{5,3},{6,0},{7,1},{8,14},{9,15},{10,... | collective-permute-start | bytes 196616 | tf_op jit(solution)/shard_map/ppermute | solution.py:386
  97.4 9.1 %collective-permute-start.17 = (bf16[256,128]{1,0:T(8,128)(2,1)S(1)}, bf16[256,128]{1,0:T(8,128)(2,1)S(1)}, u32[]{:S(2)}, u32[]{:S(2)}) collective-permute-start(bf16[256,128]{1,0:T(8,128)(2,1)S(1)} %get-tuple-element.45), channel_id=1, source_target_pairs={{0,8},{1,9},{2,10},{3,11},{4,12},{5,13},{6,14},{7,15},{8,0},{9,1},... | collective-permute-start | bytes 196616 | tf_op jit(solution)/shard_map/ppermute | solution.py:386
  100.1 10.7 %collective-permute-start.18 = (bf16[256,128]{1,0:T(8,128)(2,1)S(1)}, bf16[256,128]{1,0:T(8,128)(2,1)S(1)}, u32[]{:S(2)}, u32[]{:S(2)}) collective-permute-start(bf16[256,128]{1,0:T(8,128)(2,1)S(1)} %get-tuple-element.46), channel_id=1, source_target_pairs={{0,10},{1,11},{2,8},{3,9},{4,14},{5,15},{6,12},{7,13},{8,2},{9,3},... | collective-permute-start | bytes 196616 | tf_op jit(solution)/shard_map/ppermute | solution.py:386
  101.4 9.3 %collective-permute-start.19 = (bf16[256,128]{1,0:T(8,128)(2,1)S(1)}, bf16[256,128]{1,0:T(8,128)(2,1)S(1)}, u32[]{:S(2)}, u32[]{:S(2)}) collective-permute-start(bf16[256,128]{1,0:T(8,128)(2,1)S(1)} %get-tuple-element.47), channel_id=1, source_target_pairs={{0,12},{1,13},{2,14},{3,15},{4,8},{5,9},{6,10},{7,11},{8,4},{9,5},... | collective-permute-start | bytes 196616 | tf_op jit(solution)/shard_map/ppermute | solution.py:386
  102.7 8.0 %collective-permute-start.20 = (bf16[256,128]{1,0:T(8,128)(2,1)S(1)}, bf16[256,128]{1,0:T(8,128)(2,1)S(1)}, u32[]{:S(2)}, u32[]{:S(2)}) collective-permute-start(bf16[256,128]{1,0:T(8,128)(2,1)S(1)} %get-tuple-element.48), channel_id=1, source_target_pairs={{0,14},{1,15},{2,12},{3,13},{4,10},{5,11},{6,8},{7,9},{8,6},{9,7},... | collective-permute-start | bytes 196616 | tf_op jit(solution)/shard_map/ppermute | solution.py:386
  110.8 1.6 %copy-start.1 = (bf16[1024,1024]{1,0:T(8,128)(2,1)S(1)}, bf16[1024,1024]{1,0:T(8,128)(2,1)}, u32[]{:S(2)}) copy-start(bf16[1024,1024]{1,0:T(8,128)(2,1)} %all-gather.2.cloned.1.call-done.refs_8_) | copy-start | bytes 6291460
  117.2 1.6 %collective-permute-start.21 = (bf16[128,1152]{1,0:T(8,128)(2,1)S(1)}, bf16[128,1152]{1,0:T(8,128)(2,1)S(1)}, u32[]{:S(2)}, u32[]{:S(2)}) collective-permute-start(bf16[128,1152]{1,0:T(8,128)(2,1)S(1)} %get-tuple-element.51), channel_id=1, source_target_pairs={{0,1},{1,0},{2,3},{3,2},{4,5},{5,4},{6,7},{7,6},{8,9},{9,8},{10,11... | collective-permute-start | bytes 884744 | tf_op jit(solution)/shard_map/ppermute | solution.py:404
  120.5 8.0 %collective-permute-start.22 = (bf16[16,1152]{1,0:T(8,128)(2,1)S(1)}, bf16[16,1152]{1,0:T(8,128)(2,1)S(1)}, u32[]{:S(2)}, u32[]{:S(2)}) collective-permute-start(bf16[16,1152]{1,0:T(8,128)(2,1)S(1)} %get-tuple-element.53), channel_id=1, source_target_pairs={{0,2},{1,3},{2,0},{3,1},{4,6},{5,7},{6,4},{7,5},{8,10},{9,11},{10,... | collective-permute-start | bytes 110600 | tf_op jit(solution)/shard_map/ppermute | solution.py:406
  121.3 9.5 %collective-permute-start.23 = (bf16[16,1152]{1,0:T(8,128)(2,1)S(1)}, bf16[16,1152]{1,0:T(8,128)(2,1)S(1)}, u32[]{:S(2)}, u32[]{:S(2)}) collective-permute-start(bf16[16,1152]{1,0:T(8,128)(2,1)S(1)} %get-tuple-element.54), channel_id=1, source_target_pairs={{0,4},{1,5},{2,6},{3,7},{4,0},{5,1},{6,2},{7,3},{8,12},{9,13},{10,... | collective-permute-start | bytes 110600 | tf_op jit(solution)/shard_map/ppermute | solution.py:406
  124.4 8.6 %collective-permute-start.24 = (bf16[16,1152]{1,0:T(8,128)(2,1)S(1)}, bf16[16,1152]{1,0:T(8,128)(2,1)S(1)}, u32[]{:S(2)}, u32[]{:S(2)}) collective-permute-start(bf16[16,1152]{1,0:T(8,128)(2,1)S(1)} %get-tuple-element.55), channel_id=1, source_target_pairs={{0,6},{1,7},{2,4},{3,5},{4,2},{5,3},{6,0},{7,1},{8,14},{9,15},{10,... | collective-permute-start | bytes 110600 | tf_op jit(solution)/shard_map/ppermute | solution.py:406
  125.3 7.7 %collective-permute-start.25 = (bf16[16,1152]{1,0:T(8,128)(2,1)S(1)}, bf16[16,1152]{1,0:T(8,128)(2,1)S(1)}, u32[]{:S(2)}, u32[]{:S(2)}) collective-permute-start(bf16[16,1152]{1,0:T(8,128)(2,1)S(1)} %get-tuple-element.56), channel_id=1, source_target_pairs={{0,8},{1,9},{2,10},{3,11},{4,12},{5,13},{6,14},{7,15},{8,0},{9,1},... | collective-permute-start | bytes 110600 | tf_op jit(solution)/shard_map/ppermute | solution.py:406
  127.3 6.4 %collective-permute-start.26 = (bf16[16,1152]{1,0:T(8,128)(2,1)S(1)}, bf16[16,1152]{1,0:T(8,128)(2,1)S(1)}, u32[]{:S(2)}, u32[]{:S(2)}) collective-permute-start(bf16[16,1152]{1,0:T(8,128)(2,1)S(1)} %get-tuple-element.57), channel_id=1, source_target_pairs={{0,10},{1,11},{2,8},{3,9},{4,14},{5,15},{6,12},{7,13},{8,2},{9,3},... | collective-permute-start | bytes 110600 | tf_op jit(solution)/shard_map/ppermute | solution.py:406
  128.4 6.1 %collective-permute-start.27 = (bf16[16,1152]{1,0:T(8,128)(2,1)S(1)}, bf16[16,1152]{1,0:T(8,128)(2,1)S(1)}, u32[]{:S(2)}, u32[]{:S(2)}) collective-permute-start(bf16[16,1152]{1,0:T(8,128)(2,1)S(1)} %get-tuple-element.58), channel_id=1, source_target_pairs={{0,12},{1,13},{2,14},{3,15},{4,8},{5,9},{6,10},{7,11},{8,4},{9,5},... | collective-permute-start | bytes 110600 | tf_op jit(solution)/shard_map/ppermute | solution.py:406
  130.8 6.7 %collective-permute-start.28 = (bf16[16,1152]{1,0:T(8,128)(2,1)S(1)}, bf16[16,1152]{1,0:T(8,128)(2,1)S(1)}, u32[]{:S(2)}, u32[]{:S(2)}) collective-permute-start(bf16[16,1152]{1,0:T(8,128)(2,1)S(1)} %get-tuple-element.59), channel_id=1, source_target_pairs={{0,14},{1,15},{2,12},{3,13},{4,10},{5,11},{6,8},{7,9},{8,6},{9,7},... | collective-permute-start | bytes 110600 | tf_op jit(solution)/shard_map/ppermute | solution.py:406
Sparse Core Ops, SparseCore 0:
  10.2 48.9 all-gather.1

commit v2 on v1

v2 whole, which is shorter than its diff:
```python
import functools
import math

import jax
import jax.numpy as jnp
from jax import lax
from jax.experimental import pallas as pl
from jax.experimental.pallas import tpu as pltpu
from jax.sharding import PartitionSpec as P

D = 1024
HEADS = 16
HEAD_DIM = 64
PROBES = 256
BLOCK = 128
MAXK = 8
TOK_DEV = 256
STATS = 128
CHUNK = 4
EPS = 1e-05
SCALE = 1.0 / math.sqrt(HEAD_DIM)
EXP2_SCALE = SCALE / math.log(2.0)
BF16 = jnp.bfloat16
F32 = jnp.float32
NT = (((1,), (1,)), ((), ()))
VMEM_BYTES = 28 * 1024 * 1024


def whole():
    return pl.BlockSpec(memory_space=pltpu.VMEM)


def scalars():
    return pl.BlockSpec(memory_space=pltpu.SMEM)


def params():
    return pltpu.CompilerParams(vmem_limit_bytes=VMEM_BYTES)


def layer_norm(values, gain):
    wide = values.astype(F32)
    center = wide - jnp.mean(wide, axis=-1, keepdims=True)
    spread = jnp.mean(center * center, axis=-1, keepdims=True)
    return (center * lax.rsqrt(spread + EPS) * gain).astype(BF16)


def head_masked(block, heads):
    if heads == 1:
        return block
    lanes = lax.broadcasted_iota(jnp.int32, block.shape, 1) // HEAD_DIM
    zero = jnp.zeros_like(block)
    return jnp.concatenate([jnp.where(lanes == h, block, zero) for h in range(heads)], axis=0)


def chip_and_core():
    rank = lax.axis_index("seq")
    return lax.shift_right_logical(rank, 1), lax.bitwise_and(rank, 1)


def twin():
    return lax.bitwise_and(lax.axis_index("scan"), 1)


def ring_owners(chip, chips):
    half = lax.shift_right_logical(chip, 1)
    position = jnp.where(lax.bitwise_and(chip, 1) == 1, chips - 1 - half, half)
    offsets = [0]
    for s in range(1, chips // 2):
        offsets += [-s, s]
    offsets.append(chips // 2)
    owners = []
    for offset in offsets:
        spot = lax.rem(position + (offset + chips), chips)
        owners.append(jnp.where(spot < chips // 2, 2 * spot, 2 * (chips - 1 - spot) + 1))
    return owners


def prepare_kernel(
    chips, width, tokens_ref, query_ref, key_ref, value_ref, out_ref, load_ref, cut_ref, rows_ref, sems
):
    chip, _ = chip_and_core()
    mine = twin()
    rows = out_ref.shape[0] // 4
    half = TOK_DEV // 2
    step = half + rows
    copies = []
    for i, ref in enumerate((query_ref, key_ref, value_ref)):
        start = pl.multiple_of(mine * (2 * rows), 2 * rows)
        copies.append((ref.at[pl.ds(start, 2 * rows), :], rows_ref.at[i]))
    for part in range(2):
        start = pl.multiple_of(mine * (2 * rows) + part * rows, rows)
        to = load_ref.at[part * step : part * step + half, :]
        copies.append((tokens_ref.at[part * half : (part + 1) * half, :], to))
        to = load_ref.at[part * step + half : (part + 1) * step, :]
        copies.append((out_ref.at[pl.ds(start, rows), :], to))
    copies = [pltpu.make_async_copy(a, b, sems.at[i]) for i, (a, b) in enumerate(copies)]
    for copy in copies:
        copy.start()
    for copy in copies[:3]:
        copy.wait()
    for k in range(chips):
        lanes = pl.ds(pl.multiple_of(lax.bitwise_xor(chip, k) * width, width), width)
        for i in range(3):
            cut_ref[k, :, i * width : (i + 1) * width] = rows_ref[i, :, lanes]
    for copy in copies[3:]:
        copy.wait()


def prepare(tokens, weights, out_weight, chips, width):
    rows = out_weight.shape[0] // 2
    return pl.pallas_call(
        functools.partial(prepare_kernel, chips, width),
        out_shape=(
            jax.ShapeDtypeStruct((TOK_DEV + rows, D), BF16),
            jax.ShapeDtypeStruct((chips, rows, 3 * width), BF16),
        ),
        in_specs=[pl.BlockSpec(memory_space=pltpu.HBM)] * 5,
        out_specs=(whole(), whole()),
        scratch_shapes=[pltpu.VMEM((3, rows, D), BF16), pltpu.SemaphoreType.DMA((7,))],
        compiler_params=params(),
        name="prepare",
    )(*(pltpu.with_memory_space_constraint(x, pltpu.HBM) for x in (tokens, *weights, out_weight)))


def gather_blocks_kernel(picks, ordered, *refs):
    chip, _ = chip_and_core()
    for at, (i, j) in enumerate(picks):
        refs[-1][lax.bitwise_xor(chip, at) if ordered else at] = refs[i][j]


def gather_blocks(blocks, ordered):
    arrays, picks = [], []
    for array, j in blocks:
        if not any(array is one for one in arrays):
            arrays.append(array)
        picks.append(([array is one for one in arrays].index(True), j))
    return pl.pallas_call(
        functools.partial(gather_blocks_kernel, tuple(picks), ordered),
        out_shape=jax.ShapeDtypeStruct((len(blocks),) + arrays[0].shape[1:], BF16),
        in_specs=[whole()] * len(arrays),
        out_specs=whole(),
        compiler_params=params(),
        name="gather_blocks",
    )(*arrays)


def collect_kernel(places, *refs):
    out_ref = refs[-1]
    rows = out_ref.shape[1] // 2
    for i, at in enumerate(places):
        part = i % 2
        out_ref[i // 2, part * rows : (part + 1) * rows, :] = refs[i][at : at + rows, :]


def collect(pieces, rows):
    places = tuple(at + TOK_DEV // 2 for _, at in pieces)
    return pl.pallas_call(
        functools.partial(collect_kernel, places),
        out_shape=jax.ShapeDtypeStruct((len(pieces) // 2, rows, D), BF16),
        in_specs=[whole()] * len(pieces),
        out_specs=whole(),
        compiler_params=params(),
        name="collect",
    )(*(array for array, _ in pieces))


def pair_rows_kernel(chips, ringed, *refs):
    out_ref = refs[-1]
    mine = twin()
    chip, _ = chip_and_core()
    owners = ring_owners(chip, chips) if ringed else range(chips)
    at = 0
    for own_ref, twin_ref in zip(refs[0:-1:2], refs[1:-1:2]):
        for i in range(own_ref.shape[0]):
            out_ref[owners[at], mine] = own_ref[i]
            out_ref[owners[at], 1 - mine] = twin_ref[i]
            at += 1


def pair_rows(pairs, chips, ringed):
    rows, columns = pairs[0][0].shape[1:]
    flat = [p for pair in pairs for p in pair]
    return pl.pallas_call(
        functools.partial(pair_rows_kernel, chips, ringed),
        out_shape=jax.ShapeDtypeStruct((chips, 2, rows, columns), BF16),
        in_specs=[whole()] * len(flat),
        out_specs=whole(),
        compiler_params=params(),
        name="pair_rows",
    )(*flat)


def weave_kernel(own_ref, other_ref, out_ref):
    _, core = chip_and_core()
    chips, rows, columns = own_ref.shape
    for c in range(chips):
        own, other = own_ref[c], other_ref[c]
        out_ref[2 * c * rows : (2 * c + 1) * rows, :] = jnp.where(core == 0, own, other)
        out_ref[(2 * c + 1) * rows : (2 * c + 2) * rows, :] = jnp.where(core == 0, other, own)


def weave(own, other):
    chips, two, rows, columns = own.shape
    own, other = (x.reshape(chips, two * rows, columns) for x in (own, other))
    return pl.pallas_call(
        weave_kernel,
        out_shape=jax.ShapeDtypeStruct((4 * chips * rows, columns), BF16),
        in_specs=[whole()] * 2,
        out_specs=whole(),
        compiler_params=params(),
        name="weave",
    )(own, other)


def shard_blocks(owner, core):
    first = (owner * 2 + core) * (TOK_DEV // BLOCK)
    return [first + u for u in range(TOK_DEV // BLOCK)]


def absorb(pair_ref, kv_all, owners, core):
    blocks = TOK_DEV // BLOCK
    for t, owner in enumerate(owners):
        for u, block in enumerate(shard_blocks(owner, core)):
            kv_all[block] = pair_ref[t * blocks + u]


def project_kernel(chips, starts, width, shards, before, *refs):
    n = len(starts)
    inputs, (gain_ref, weight_ref), (q_all, kv_all, pair_ref) = refs[:n], refs[n : n + 2], refs[-3:]
    chip, core = chip_and_core()
    owners = ring_owners(chip, chips)
    places = [(ref, at) for ref, spots in zip(inputs, starts) for at in spots]
    for begin in range(0, len(places), CHUNK):
        segments = [ref[at : at + BLOCK, :] for ref, at in places[begin : begin + CHUNK]]
        normed = layer_norm(jnp.concatenate(segments, axis=0), gain_ref[...])
        result = jnp.dot(normed, weight_ref[...], preferred_element_type=F32)
        for j in range(len(segments)):
            i = begin + j
            rows = result[j * BLOCK : (j + 1) * BLOCK]
            t, u = divmod(i, TOK_DEV // BLOCK)
            q_all[owners[shards[t]] * (TOK_DEV // BLOCK) + u] = rows[:, :width].astype(BF16)
            pair_ref[i, 0, :, :width] = rows[:, width : 2 * width].astype(BF16)
            pair_ref[i, 1, :width, :] = jnp.transpose(rows[:, 2 * width :]).astype(BF16)
            if width < BLOCK:
                pair_ref[i, 0, :, width:] = jnp.zeros((BLOCK, BLOCK - width), BF16)
                pair_ref[i, 1, width:, :] = jnp.zeros((BLOCK - width, BLOCK), BF16)
    absorb(pair_ref, kv_all, [owners[s] for s in shards], core)
    for i, held in enumerate(before):
        absorb(refs[n + 4 + i], kv_all, [owners[s] for s in held], 1 - core)


def project(pieces, starts, gain, weight, width, chips, shards, before, state):
    blocks = sum(len(s) for s in starts)
    n = len(pieces)
    total = chips * (TOK_DEV // BLOCK)
    return pl.pallas_call(
        functools.partial(project_kernel, chips, starts, width, shards, before),
        out_shape=(
            jax.ShapeDtypeStruct((total, BLOCK, width), BF16),
            jax.ShapeDtypeStruct((2 * total, 2, BLOCK, BLOCK), BF16),
            jax.ShapeDtypeStruct((blocks, 2, BLOCK, BLOCK), BF16),
        ),
        in_specs=[whole()] * (n + 2 + len(state)),
        out_specs=(whole(),) * 3,
        input_output_aliases={n + 2: 0, n + 3: 1} if state else {},
        compiler_params=params(),
        name="project",
    )(*pieces, gain, weight, *state)


def attend_kernel(chips, group, heads, steps, last, lists_ref, counts_ref, q_all, *refs):
    width = heads * HEAD_DIM
    outs, mixed = refs[-1 - len(steps) : -1], refs[-1]
    chip, core = chip_and_core()
    kv_all = refs[0]
    if last:
        kv_all = refs[1 + len(last)]
        owners = ring_owners(chip, chips)
        for i, held in enumerate(last):
            absorb(refs[1 + i], kv_all, [owners[s] for s in held], 1 - core)
    member = lax.rem(chip, group)
    blocks = TOK_DEV // BLOCK
    per_piece = blocks // group

    def place_of(index):
        target = lax.bitwise_xor(chip, steps[0] + lax.div(index, per_piece))
        within = member * per_piece + lax.rem(index, per_piece)
        return target * blocks + within, (target * 2 + core) * blocks + within

    def attend_block(index, used):
        row, block = place_of(index)
        count = counts_ref[block]
        picked = [lists_ref[block, s] for s in range(used)]
        stacked = head_masked(q_all[row], heads)
        scores = []
        for s, p in enumerate(picked):
            one = lax.dot_general(
                kv_all[p, 0][:, :width], stacked, NT, preferred_element_type=F32
            )
            if s:
                one = one + jnp.where(s < count, 0.0, -jnp.inf).astype(F32)
            scores.append(one)
        scores = jnp.concatenate(scores, axis=0)
        top = jnp.max(scores, axis=0, keepdims=True)
        weights = jnp.exp2((scores - top) * EXP2_SCALE)
        total = jnp.sum(weights, axis=0, keepdims=True)
        values = jnp.concatenate([kv_all[p, 1] for p in picked], axis=1)[:width]
        full = jnp.dot(values, weights.astype(BF16), preferred_element_type=F32)
        full = full * (1.0 / total)
        result = jnp.concatenate(
            [
                full[h * HEAD_DIM : (h + 1) * HEAD_DIM, h * BLOCK : (h + 1) * BLOCK]
                for h in range(heads)
            ],
            axis=0,
        )
        return jnp.transpose(result).astype(BF16)

    def one_pair(pair, carry):
        first, second = 2 * pair, 2 * pair + 1
        most = jnp.maximum(counts_ref[place_of(first)[1]], counts_ref[place_of(second)[1]])
        for used in range(1, MAXK + 1):

            @pl.when(most == used)
            def _(used=used):
                one, two = attend_block(first, used), attend_block(second, used)
                mixed[first] = one
                mixed[second] = two

        return carry

    lax.fori_loop(0, len(steps) * per_piece // 2, one_pair, 0)
    for k in range(len(steps)):
        for part in range(per_piece):
            outs[k][part * BLOCK : (part + 1) * BLOCK, :] = mixed[k * per_piece + part]


def attend(lists, counts, q_all, kv_all, extra, chips, group, heads, steps, last):
    width = heads * HEAD_DIM
    piece = TOK_DEV // group
    kv_shape = [jax.ShapeDtypeStruct(kv_all.shape, BF16)] if last else []
    return pl.pallas_call(
        functools.partial(attend_kernel, chips, group, heads, steps, last),
        out_shape=kv_shape + [jax.ShapeDtypeStruct((piece, width), BF16)] * len(steps),
        in_specs=[scalars()] * 2 + [whole()] * (2 + len(extra)),
        out_specs=[whole()] * (len(kv_shape) + len(steps)),
        input_output_aliases={3: 0} if last else {},
        scratch_shapes=[pltpu.VMEM((len(steps) * (piece // BLOCK), BLOCK, width), BF16)],
        compiler_params=params(),
        name="attend",
    )(lists, counts, q_all, kv_all, *extra)


def tail_kernel(chips, group, heads, split, *refs):
    width = heads * HEAD_DIM
    sets = HEADS // heads
    piece = TOK_DEV // group
    got = refs[:chips]
    weight_ref, tokens_ref, gain_ref, probe_ref, layer_ref = refs[chips : chips + 5]
    part_refs, (stage,) = refs[chips + 5 : -1], refs[-1:]
    chip, core = chip_and_core()
    for k in range(chips):
        source = lax.bitwise_xor(chip, k)
        if group == 1:
            stage[source] = got[k][...]
        else:
            stage[source // group, pl.ds(pl.multiple_of(source % group * piece, piece), piece), :] = got[k][...]
    attended = jnp.concatenate([stage[s] for s in range(sets)], axis=1)
    projected = jnp.dot(attended, weight_ref[...], preferred_element_type=F32)
    layer = (tokens_ref[...].astype(F32) + projected).astype(BF16)
    layer_ref[...] = layer
    pooled = layer_norm(layer, gain_ref[...])
    rows = []

    def emit(lo, value):
        hi = lo + value.shape[1]
        if not split:
            part_refs[0][:, lo:hi] = value.astype(BF16)
            return
        share = PROBES // (2 * chips)
        shaped = value.reshape(chips, 2, share, value.shape[1])
        first, second = shaped[:, 0], shaped[:, 1]
        mine = jnp.where(core == 0, first, second)
        theirs = jnp.where(core == 0, second, first)
        part_refs[0][:, lo:hi] = mine.reshape(chips * share, -1).astype(BF16)
        part_refs[1][:, lo:hi] = theirs.reshape(chips * share, -1).astype(BF16)

    for pair in range(HEADS // 2):
        lo = pair * 2 * HEAD_DIM
        own = pooled[:, lo : lo + 2 * HEAD_DIM]
        stacked = head_masked(probe_ref[:, lo : lo + 2 * HEAD_DIM], 2)
        scores = lax.dot_general(own, stacked, NT, preferred_element_type=F32)
        top = jnp.max(scores, axis=0, keepdims=True)
        weights = jnp.exp2((scores - top) * EXP2_SCALE)
        total = jnp.sum(weights, axis=0, keepdims=True)
        flipped = jnp.transpose(own.astype(F32)).astype(BF16)
        full = jnp.dot(flipped, weights.astype(BF16), preferred_element_type=F32) / total
        result = jnp.concatenate([full[:HEAD_DIM, :PROBES], full[HEAD_DIM:, PROBES:]], axis=0)
        emit(lo, jnp.transpose(result))
        logs = top * SCALE + jnp.log(total)
        rows += [logs[:, :PROBES], logs[:, PROBES:]]
    logs = jnp.concatenate(rows, axis=0)
    high = logs.astype(BF16).astype(F32)
    middle = (logs - high).astype(BF16).astype(F32)
    low = logs - high - middle
    rest = jnp.zeros((STATS - 3 * HEADS, PROBES), F32)
    emit(D, jnp.transpose(jnp.concatenate([high, middle, low, rest], axis=0)))


def tail(got, weight, tokens, gain, probes, chips, group, heads, split):
    width = heads * HEAD_DIM
    rows = PROBES // 2 if split else PROBES
    return pl.pallas_call(
        functools.partial(tail_kernel, chips, group, heads, split),
        out_shape=[jax.ShapeDtypeStruct((TOK_DEV, D), BF16)]
        + [jax.ShapeDtypeStruct((rows, D + STATS), BF16)] * (2 if split else 1),
        in_specs=[whole()] * (chips + 4),
        out_specs=[whole()] * (3 if split else 2),
        scratch_shapes=[pltpu.VMEM((HEADS // heads, TOK_DEV, width), BF16)],
        compiler_params=params(),
        name="tail",
    )(*got, weight, tokens, gain, probes)


def read_logs(block):
    pick = lax.broadcasted_iota(jnp.int32, (STATS, STATS), 0)
    head = lax.broadcasted_iota(jnp.int32, (STATS, STATS), 1)
    gather = ((pick < 3 * HEADS) & (pick % HEADS == head)).astype(BF16)
    return jnp.dot(block, gather, preferred_element_type=F32)


def spread_heads(factors):
    row = lax.broadcasted_iota(jnp.int32, (STATS, D), 0)
    lane = lax.broadcasted_iota(jnp.int32, (STATS, D), 1)
    widen = (lane // HEAD_DIM == row).astype(F32)
    return jnp.dot(factors, widen, preferred_element_type=F32, precision=lax.Precision.HIGHEST)


def blend(blocks):
    logs = [read_logs(b[:, D:]) for b in blocks]
    top = functools.reduce(jnp.maximum, logs)
    shares = [jnp.exp(one - top) for one in logs]
    total = functools.reduce(jnp.add, shares)
    rows = blocks[0].shape[0]
    wide = spread_heads(jnp.concatenate([s / total for s in shares], axis=0))
    value = 0.0
    for i, b in enumerate(blocks):
        value = value + wide[i * rows : (i + 1) * rows] * b[:, :D].astype(F32)
    return value, top + jnp.log(total)


def repack(value, logs):
    high = logs.astype(BF16).astype(F32)
    middle = (logs - high).astype(BF16).astype(F32)
    low = logs - high - middle
    rest = jnp.zeros((value.shape[0], STATS - 3 * HEADS), F32)
    return jnp.concatenate(
        [value, high[:, :HEADS], middle[:, :HEADS], low[:, :HEADS], rest], axis=1
    ).astype(BF16)


def deal_kernel(mine_ref, got_ref, *outs_and_stage):
    outs, stage = outs_and_stage[:-1], outs_and_stage[-1]
    chip, _ = chip_and_core()
    packed = repack(*blend([mine_ref[...], got_ref[...]]))
    stage[...] = packed.reshape(stage.shape)
    for k in range(len(outs)):
        outs[k][...] = stage[lax.bitwise_xor(chip, k)]


def deal(mine, got, parts):
    share = mine.shape[0] // parts
    return pl.pallas_call(
        deal_kernel,
        out_shape=[jax.ShapeDtypeStruct((share, D + STATS), BF16)] * parts,
        in_specs=[whole(), whole()],
        out_specs=[whole()] * parts,
        scratch_shapes=[pltpu.VMEM((parts, share, D + STATS), BF16)],
        compiler_params=params(),
        name="deal",
    )(mine, got)


def last_kernel(*refs):
    refs[-1][...] = blend([r[...] for r in refs[:-1]])[0]


def join(parts):
    return pl.pallas_call(
        last_kernel,
        out_shape=jax.ShapeDtypeStruct((parts[0].shape[0], D), F32),
        in_specs=[whole()] * len(parts),
        out_specs=whole(),
        compiler_params=params(),
        name="join",
    )(*parts)


def per_device(
    tokens,
    ln_gain,
    w_query,
    w_key,
    w_value,
    w_out,
    probe_gain,
    probe_queries,
    key_blocks,
    key_counts,
):
    ranks = lax.axis_size("seq")
    chips = ranks // 2
    heads = max(1, HEADS // chips)
    group = max(1, chips // HEADS)
    sets = HEADS // heads
    width = heads * HEAD_DIM
    myself = lax.axis_index("seq")
    core = myself % 2
    order = list(range(0, chips, 2)) + list(range(chips - 1, 0, -2))
    swap = [(i, i ^ 1) for i in range(ranks)]
    same_core = [[2 * c + k for c in range(chips)] for k in range(2)]

    def around(shift):
        return [
            (order[i] * 2 + k, order[(i + shift) % chips] * 2 + k)
            for i in range(chips)
            for k in range(2)
        ]

    def across(k):
        return [(2 * c + q, 2 * (c ^ k) + q) for c in range(chips) for q in range(2)]

    twins = [(i, i ^ 1) for i in range(lax.axis_size("scan"))]
    barrier = lax.optimization_barrier
    depth = w_query.shape[0]
    gain = ln_gain.reshape(1, D)
    half = TOK_DEV // 2
    packed = depth % 64 == 0

    if packed:
        load, parted = prepare(tokens, (w_query, w_key, w_value), w_out, chips, width)
        line = range(chips // 2)
        away = lax.ppermute(
            gather_blocks([(parted, k) for k in range(1, chips, 2)], False), "seq", across(1)
        )
        moved = [
            lax.ppermute(
                gather_blocks([(parted, 2 * k), (away, k)], False), "seq", across(2 * k)
            )
            for k in line[1:]
        ]
    else:
        columns = jnp.stack([w_query, w_key, w_value]).reshape(3, depth, sets, width)
        columns = jnp.transpose(columns, (2, 1, 0, 3)).reshape(sets, depth, 3 * width)
        columns = jnp.repeat(columns, group, axis=0)
        here = lax.all_to_all(
            columns, "seq", split_axis=0, concat_axis=0, tiled=True, axis_index_groups=same_core
        )
        there = lax.ppermute(here, "seq", swap)
        even = jnp.where(core == 0, here, there)
        odd = jnp.where(core == 0, there, here)
        weight = jnp.stack([even, odd], axis=1).reshape(D, 3 * width)
        out_weight = lax.all_gather(w_out, "seq", axis=0, tiled=True)

    load = load if packed else tokens
    length = load.shape[0] // 2
    if packed:
        load, away = barrier((load, away))
    forward = backward = load

    def spread(*shards):
        return [(shard, at) for shard in shards for at in (0, length)]

    state, others = (), []

    def advance(pieces, shards):
        nonlocal state, others
        q_all, kv_all, pair = project(
            [array for array, _ in pieces],
            tuple((at,) for _, at in pieces),
            gain,
            weight,
            width,
            chips,
            shards,
            tuple(held for _, held in others),
            state + tuple(other for other, _ in others),
        )
        state, others = (q_all, kv_all), []
        return pair

    def send(pair, shards):
        others.append((lax.ppermute(pair, "seq", swap), shards))

    arrived, shards = spread(load), (0,)
    for s in range(1, chips // 2 - 1):
        forward = lax.ppermute(forward, "seq", around(1))
        backward = lax.ppermute(backward, "seq", around(-1))
        if packed and s == 1:
            forward, backward, moved[0] = barrier((forward, backward, moved[0]))
        if packed and s == 2:
            sources = [(parted, 0), (away, 0)] + [(m, j) for m in moved for j in range(2)]
            quarter = gather_blocks(sources, True)
            own_half = pair_rows([(quarter, lax.ppermute(quarter, "scan", twins))], chips, False)
            weight = weave(own_half, lax.ppermute(own_half, "seq", swap))
            forward, backward, weight = barrier((forward, backward, weight))
        arrived += spread(forward, backward)
        shards += (2 * s - 1, 2 * s)
    if packed:
        early = collect(arrived, depth // 2)
        early_twin = lax.ppermute(early, "scan", twins)
        weight, early_twin = barrier((weight, early_twin))
    pair = advance(arrived, shards)
    forward = lax.ppermute(forward, "seq", around(1))
    backward = lax.ppermute(backward, "seq", around(-1))
    forward, backward, pair, *state = barrier((forward, backward, pair, *state))
    state = tuple(state)
    final = (
        lax.ppermute(forward[:length], "seq", around(1)),
        lax.ppermute(backward[length:], "seq", around(-1)),
    )
    pair, *final = barrier((pair, *final))
    send(pair, shards)
    held, others = others, []
    last = spread(forward, backward) + [(array, 0) for array in final]
    last_shards = (chips - 3, chips - 2, chips - 1)
    send(advance(last, last_shards), last_shards)
    others = held + others
    if packed:
        middle = collect(spread(forward, backward), depth // 2)
        middle_twin = lax.ppermute(middle, "scan", twins)
        late = collect(last[-2:], depth // 2)
        late_twin = lax.ppermute(late, "scan", twins)
    q_all, kv_all = state
    far = tuple(range(chips // 2, chips))
    near = tuple(range(chips // 2))
    kv_all, *first = attend(
        key_blocks,
        key_counts,
        q_all,
        kv_all,
        [other for other, _ in others],
        chips,
        group,
        heads,
        far,
        tuple(held for _, held in others),
    )
    if packed:
        kv_all, middle_twin, late_twin = barrier((kv_all, middle_twin, late_twin))
        own_half = pair_rows(
            [(early, early_twin), (middle, middle_twin), (late, late_twin)], chips, True
        )
        other_half = lax.ppermute(own_half, "seq", swap)
    sent = [lax.ppermute(first[i], "seq", across(k)) for i, k in enumerate(far)]
    second = attend(key_blocks, key_counts, q_all, kv_all, (), chips, group, heads, near, ())
    got = [second[0]] + [lax.ppermute(second[k], "seq", across(k)) for k in near[1:]] + sent
    if packed:
        out_weight = weave(own_half, other_half)

    share = PROBES // ranks
    split = share % 16 == 0
    layer_out, *parts = tail(
        got,
        out_weight,
        tokens,
        probe_gain.reshape(1, D),
        probe_queries,
        chips,
        group,
        heads,
        split,
    )
    if split:
        mine, theirs = parts
        blocks = deal(mine, lax.ppermute(theirs, "seq", swap), chips)
        joined = [blocks[0]] + [
            lax.ppermute(blocks[k], "seq", across(k)) for k in range(1, chips)
        ]
        return layer_out, join(joined)
    rows = lax.all_to_all(
        parts[0].reshape(ranks, share, D + STATS), "seq", split_axis=0, concat_axis=0, tiled=True
    ).astype(F32)
    logs = rows[:, :, D : D + 3 * HEADS].reshape(ranks, share, 3, HEADS).sum(axis=2)
    factors = jnp.exp(logs - jnp.max(logs, axis=0, keepdims=True))
    factors = factors / jnp.sum(factors, axis=0, keepdims=True)
    probe_out = jnp.sum(jnp.repeat(factors, HEAD_DIM, axis=2) * rows[:, :, :D], axis=0)
    return layer_out, probe_out


def solution(mesh):
    return jax.shard_map(
        per_device,
        mesh=mesh,
        in_specs=(
            P(("scan", "seq"), None),
            P(),
            P("seq", None),
            P("seq", None),
            P("seq", None),
            P("seq", None),
            P(),
            P(),
            P("scan", None),
            P("scan"),
        ),
        out_specs=(P(("scan", "seq"), None), P(("scan", "seq"), None)),
        check_vma=False,
    )
```

time: 147 us -> 125 us (0.85)
  between operations: 14.3 us -> 0.88 us
  local copies, waits for them, and re-layouts: 11.4 us -> 2.27 us
  waiting for transfers between devices: 43.2 us -> 51.2 us
  starting transfers between devices: 49.3 us -> 44 us
  other arithmetic: 2.81 us -> 0 us
  Pallas kernels: 24.6 us -> 26.7 us
    ppermute x23 -> x29, waiting for transfers between devices: 12.1 us -> 43.8 us  [the longest x3 14.2 us: per_device(): lax.ppermute(gather_blocks([(parted, 2 * k), (away, k)], False), 'seq', a...]
    ppermute x3, starting transfers between devices: 14 us -> 1.89 us  [per_device(): forward = lax.ppermute(forward, 'seq', around(1))]
    all_to_all x1 -> x0, waiting for transfers between devices: 11.4 us -> none  [per_device(): lax.all_to_all(cut, 'seq', split_axis=0, concat_axis=0, tiled=True, axis_...]
    ppermute x3, waiting for transfers between devices: 18.6 us -> 7.42 us  [per_device(): forward = lax.ppermute(forward, 'seq', around(1))]
    ppermute x23 -> x29, starting transfers between devices: 28.8 us -> 37.9 us  [the longest x7 11.8 us: per_device(): lax.ppermute(blocks[k], 'seq', across(k))]
    all_to_all x1 -> x0, starting transfers between devices: 6.27 us -> none  [per_device(): lax.all_to_all(cut, 'seq', split_axis=0, concat_axis=0, tiled=True, axis_...]
    unnamed x36 -> x17, local copies, waits for them, and re-layouts: 8.32 us -> 2.23 us
    ppermute x3, starting transfers between devices: 0.25 us -> 4.19 us  [per_device(): backward = lax.ppermute(backward, 'seq', around(-1))]
  transfers between devices with their start and end apart: 31 -> 35, of which waited for: 12 -> 16; matrix products, arithmetic and copies ran while one was open for 6% -> 1% of each run, Pallas kernels for 12% -> 14%
where the time goes in v2:
time: 125 us
  waiting for transfers between devices  51.2 us (41%)
  starting transfers between devices  44 us (35%)
  Pallas kernels  26.7 us (21%)
  local copies, waits for them, and re-layouts  2.27 us (2%)
    ppermute x3, waiting for transfers between devices, per_device(): lax.ppermute(gather_blocks([(parted, 2 * k), (away, k)], False), 'seq', a...  14.2 us
    ppermute x7, starting transfers between devices, per_device(): lax.ppermute(blocks[k], 'seq', across(k))  11.8 us
    pallas_call x2, Pallas kernels, attend(): pl.pallas_call(functools.partial(attend_kernel, chips, group, heads, step...  11.7 us
    ppermute x4, starting transfers between devices, per_device(): sent = [lax.ppermute(first[i], 'seq', across(k)) for i, k in enumerate(far)]  7.65 us
    ppermute x3, waiting for transfers between devices, per_device(): forward = lax.ppermute(forward, 'seq', around(1))  7.42 us
    ppermute x1, waiting for transfers between devices, per_device(): early_twin = lax.ppermute(early, 'scan', twins)  6.58 us
    ppermute x4, waiting for transfers between devices, per_device(): sent = [lax.ppermute(first[i], 'seq', across(k)) for i, k in enumerate(far)]  6.04 us
    pallas_call x2, Pallas kernels, project(): pl.pallas_call(functools.partial(project_kernel, chips, starts, width, sh...  5.86 us
  transfers between devices with their start and end apart: 35, of which 16 were waited for; matrix products, arithmetic and copies ran while one was open for 1% of the time, Pallas kernels for 14%

profile of v2, /device:TPU:0, one launch (start us, length us, event | category | flops | bytes accessed | tf_op | source)
XLA Modules:
  0.0 125.0 jit_solution(3604644573039006581)
XLA Ops:
  0.6 1.2 prepare.1
  1.9 3.0 %collective-permute-start = (bf16[4,32,384]{2,1,0:T(8,128)(2,1)S(1)}, bf16[4,32,384]{2,1,0:T(8,128)(2,1)S(1)}, u32[]{:S(2)}, u32[]{:S(2)}) collective-permute-start(bf16[4,32,384]{2,1,0:T(8,128)(2,1)S(1)} %gather_blocks.5), channel_id=1, source_target_pairs={{0,2},{1,3},{2,0},{3,1},{4,6},{5,7},{6,4},{7,5},{8,10},{9,11},{10,... | collective-permute-start | bytes 294920 | tf_op jit(solution)/shard_map/ppermute | solution.py:544
  4.9 2.8 %collective-permute-done.refs_1_ = bf16[4,32,384]{2,1,0:T(8,128)(2,1)S(1)} collective-permute-done((bf16[4,32,384]{2,1,0:T(8,128)(2,1)S(1)}, bf16[4,32,384]{2,1,0:T(8,128)(2,1)S(1)}, u32[]{:S(2)}, u32[]{:S(2)}) %collective-permute-start) | collective-permute-done | bytes 98336 | tf_op jit(solution)/shard_map/ppermute | solution.py:544
  7.7 1.9 %collective-permute-start.1 = (bf16[288,1024]{1,0:T(8,128)(2,1)S(1)}, bf16[288,1024]{1,0:T(8,128)(2,1)S(1)}, u32[]{:S(2)}, u32[]{:S(2)}) collective-permute-start(bf16[288,1024]{1,0:T(8,128)(2,1)S(1)} %get-tuple-element.53.refs_0_.refs_1_), channel_id=1, source_target_pairs={{0,4},{1,5},{4,8},{5,9},{8,12},{9,13},{12,14},{13,15},{14,10},{15,... | collective-permute-start | bytes 1769480 | tf_op jit(solution)/shard_map/ppermute | solution.py:598
  9.6 0.1 collective-permute-start.2
  9.7 1.9 %collective-permute-start.3 = (bf16[2,32,384]{2,1,0:T(8,128)(2,1)S(1)}, bf16[2,32,384]{2,1,0:T(8,128)(2,1)S(1)}, u32[]{:S(2)}, u32[]{:S(2)}) collective-permute-start(bf16[2,32,384]{2,1,0:T(8,128)(2,1)S(1)} %gather_blocks.6), channel_id=1, source_target_pairs={{0,4},{1,5},{2,6},{3,7},{4,0},{5,1},{6,2},{7,3},{8,12},{9,13},{10,... | collective-permute-start | bytes 147464 | tf_op jit(solution)/shard_map/ppermute | solution.py:548
  11.6 2.6 %collective-permute-start.6 = (bf16[2,32,384]{2,1,0:T(8,128)(2,1)S(1)}, bf16[2,32,384]{2,1,0:T(8,128)(2,1)S(1)}, u32[]{:S(2)}, u32[]{:S(2)}) collective-permute-start(bf16[2,32,384]{2,1,0:T(8,128)(2,1)S(1)} %gather_blocks.7), channel_id=1, source_target_pairs={{0,8},{1,9},{2,10},{3,11},{4,12},{5,13},{6,14},{7,15},{8,0},{9,1},... | collective-permute-start | bytes 147464 | tf_op jit(solution)/shard_map/ppermute | solution.py:548
  14.2 10.7 %collective-permute-done.3.refs_2_ = bf16[2,32,384]{2,1,0:T(8,128)(2,1)S(1)} collective-permute-done((bf16[2,32,384]{2,1,0:T(8,128)(2,1)S(1)}, bf16[2,32,384]{2,1,0:T(8,128)(2,1)S(1)}, u32[]{:S(2)}, u32[]{:S(2)}) %collective-permute-start.3) | collective-permute-done | bytes 49184 | tf_op jit(solution)/shard_map/ppermute | solution.py:548
  24.9 2.0 %collective-permute-done.6.refs_3_ = bf16[2,32,384]{2,1,0:T(8,128)(2,1)S(1)} collective-permute-done((bf16[2,32,384]{2,1,0:T(8,128)(2,1)S(1)}, bf16[2,32,384]{2,1,0:T(8,128)(2,1)S(1)}, u32[]{:S(2)}, u32[]{:S(2)}) %collective-permute-start.6) | collective-permute-done | bytes 49184 | tf_op jit(solution)/shard_map/ppermute | solution.py:548
  26.9 1.6 %collective-permute-done.7.refs_4_ = bf16[2,32,384]{2,1,0:T(8,128)(2,1)S(1)} collective-permute-done((bf16[2,32,384]{2,1,0:T(8,128)(2,1)S(1)}, bf16[2,32,384]{2,1,0:T(8,128)(2,1)S(1)}, u32[]{:S(2)}, u32[]{:S(2)}) %collective-permute-start.7) | collective-permute-done | bytes 49184 | tf_op jit(solution)/shard_map/ppermute | solution.py:548
  28.5 1.6 %collective-permute-start.8 = (bf16[8,32,384]{2,1,0:T(8,128)(2,1)S(1)}, bf16[8,32,384]{2,1,0:T(8,128)(2,1)S(1)}, u32[]{:S(2)}, u32[]{:S(2)}) collective-permute-start(bf16[8,32,384]{2,1,0:T(8,128)(2,1)S(1)} %gather_blocks.9.refs_0_), channel_id=1, source_target_pairs={{0,16},{16,0},{1,17},{17,1},{2,18},{18,2},{3,19},{19,3},{4,20},{20... | collective-permute-start | bytes 589832 | tf_op jit(solution)/shard_map/ppermute | solution.py:605
  30.1 0.0 collective-permute-start.4
  30.1 2.0 %collective-permute-start.5 = (bf16[288,1024]{1,0:T(8,128)(2,1)S(1)}, bf16[288,1024]{1,0:T(8,128)(2,1)S(1)}, u32[]{:S(2)}, u32[]{:S(2)}) collective-permute-start(bf16[288,1024]{1,0:T(8,128)(2,1)S(1)} %collective-permute-done.2.refs_4_.refs_5_), channel_id=1, source_target_pairs={{0,2},{1,3},{4,0},{5,1},{8,4},{9,5},{12,8},{13,9},{14,12},{15,13},... | collective-permute-start | bytes 1769480 | tf_op jit(solution)/shard_map/ppermute | solution.py:599
  32.1 2.1 %collective-permute-done.8.refs_1_ = bf16[8,32,384]{2,1,0:T(8,128)(2,1)S(1)} collective-permute-done((bf16[8,32,384]{2,1,0:T(8,128)(2,1)S(1)}, bf16[8,32,384]{2,1,0:T(8,128)(2,1)S(1)}, u32[]{:S(2)}, u32[]{:S(2)}) %collective-permute-start.8) | collective-permute-done | bytes 196640 | tf_op jit(solution)/shard_map/ppermute | solution.py:605
  34.3 0.1 collective-permute-start.9
  34.4 1.7 %collective-permute-done.9 = bf16[8,2,32,384]{3,2,1,0:T(8,128)(2,1)S(1)} collective-permute-done((bf16[8,2,32,384]{3,2,1,0:T(8,128)(2,1)S(1)}, bf16[8,2,32,384]{3,2,1,0:T(8,128)(2,1)S(1)}, u32[]{:S(2)}, u32[]{:S(2)}) %collective-permute-start.9) | collective-permute-done | bytes 393248 | tf_op jit(solution)/shard_map/ppermute | solution.py:606
  36.1 0.1 weave.2.refs_11_.refs_7_
  36.1 0.0 copy-start.4
  36.2 7.4 %collective-permute-done.4.refs_6_.refs_7_ = bf16[288,1024]{1,0:T(8,128)(2,1)S(1)} collective-permute-done((bf16[288,1024]{1,0:T(8,128)(2,1)S(1)}, bf16[288,1024]{1,0:T(8,128)(2,1)S(1)}, u32[]{:S(2)}, u32[]{:S(2)}) %collective-permute-start.4) | collective-permute-done | bytes 589856 | tf_op jit(solution)/shard_map/ppermute | solution.py:598
  43.6 0.0 collective-permute-start.10
  43.6 2.0 %collective-permute-start.11 = (bf16[288,1024]{1,0:T(8,128)(2,1)S(1)}, bf16[288,1024]{1,0:T(8,128)(2,1)S(1)}, u32[]{:S(2)}, u32[]{:S(2)}) collective-permute-start(bf16[288,1024]{1,0:T(8,128)(2,1)S(1)} %collective-permute-done.5.refs_8_.refs_9_), channel_id=1, source_target_pairs={{0,2},{1,3},{4,0},{5,1},{8,4},{9,5},{12,8},{13,9},{14,12},{15,13},... | collective-permute-start | bytes 1769480 | tf_op jit(solution)/shard_map/ppermute | solution.py:616
  45.6 0.6 collective-permute-start.12
  46.2 6.6 %collective-permute-done.12.refs_1_ = bf16[5,32,1024]{2,1,0:T(8,128)(2,1)S(1)} collective-permute-done((bf16[5,32,1024]{2,1,0:T(8,128)(2,1)S(1)}, bf16[5,32,1024]{2,1,0:T(8,128)(2,1)S(1)}, u32[]{:S(2)}, u32[]{:S(2)}) %collective-permute-start.12) | collective-permute-done | bytes 327712 | tf_op jit(solution)/shard_map/ppermute | solution.py:612
  52.8 0.8 copy-done.2
  53.5 3.5 %project.2 = (bf16[16,128,128]{2,1,0:T(8,128)(2,1)S(1)}, bf16[32,2,128,128]{3,2,1,0:T(8,128)(2,1)S(1)}, bf16[10,2,128,128]{3,2,1,0:T(8,128)(2,1)}) custom-call(bf16[288,1024]{1,0:T(8,128)(2,1)S(1)} %get-tuple-element.53.refs_0_.refs_1_, bf16[288,1024]{1,0:T(8,128)(2,1)S(1)} %get-tuple-element.53.refs_0_.refs_1_, ...), custom_call_target="tpu_custom_call" | custom-call | tf_op jit(solution)/shard_map/project/pallas_call | solution.py:257
  57.0 0.1 collective-permute-start.13
  57.1 2.1 %collective-permute-start.14 = (bf16[144,1024]{1,0:T(8,128)(2,1)S(1)}, bf16[144,1024]{1,0:T(8,128)(2,1)S(1)}, u32[]{:S(2)}, u32[]{:S(2)}) collective-permute-start(bf16[144,1024]{1,0:T(8,128)(2,1)S(1)} %slice.7), channel_id=1, source_target_pairs={{0,2},{1,3},{4,0},{5,1},{8,4},{9,5},{12,8},{13,9},{14,12},{15,13},... | collective-permute-start | bytes 884744 | tf_op jit(solution)/shard_map/ppermute | solution.py:621
  59.2 4.6 %collective-permute-done.13.refs_4_.refs_0_ = bf16[144,1024]{1,0:T(8,128)(2,1)S(1)} collective-permute-done((bf16[144,1024]{1,0:T(8,128)(2,1)S(1)}, bf16[144,1024]{1,0:T(8,128)(2,1)S(1)}, u32[]{:S(2)}, u32[]{:S(2)}) %collective-permute-start.13) | collective-permute-done | bytes 294944 | tf_op jit(solution)/shard_map/ppermute | solution.py:620
  63.8 0.1 collective-permute-done.14.refs_5_.refs_1_
  63.9 2.4 %project.3 = (bf16[16,128,128]{2,1,0:T(8,128)(2,1)S(1)}, bf16[32,2,128,128]{3,2,1,0:T(8,128)(2,1)S(1)}, bf16[6,2,128,128]{3,2,1,0:T(8,128)(2,1)}) custom-call(bf16[288,1024]{1,0:T(8,128)(2,1)S(1)} %collective-permute-done.10.refs_0_.refs_1_, ...), custom_call_target="tpu_custom_call", output_to_operand_aliasing={{0}: (8, {}), {1}: (9, {})} | custom-call | tf_op jit(solution)/shard_map/project/pallas_call | solution.py:257
  66.3 0.5 collective-permute-start.16
  66.8 0.9 collective-permute-start.17
  67.8 1.1 collective-permute-start.18
  68.9 0.8 copy.16.lists_ref
  69.7 0.0 copy-start.6
  69.7 0.7 copy-done.6
  70.4 5.9 %attend.2 = (bf16[32,2,128,128]{3,2,1,0:T(8,128)(2,1)S(1)}, bf16[256,128]{1,0:T(8,128)(2,1)S(1)}, bf16[256,128]{1,0:T(8,128)(2,1)S(1)}, bf16[256,128]{1,0:T(8,128)(2,1)S(1)}, bf16[256,128]{1,0:T(8,128)(2,1)S(1)}) custom-call(s32[32,8]{1,0:T(8,128)S(1)} %copy.16.lists_ref, s32[32]{0:T(128)S(1)} %copy-done.6, ...), custom_call_target="tpu_custom_call", output_to_operand_aliasing={{0}: (3, {})} | custom-call | tf_op jit(solution)/shard_map/attend/pallas_call | solution.py:343
  76.4 1.0 pair_rows.3
  77.4 0.1 collective-permute-start.26
  77.5 5.8 %attend.3 = (bf16[256,128]{1,0:T(8,128)(2,1)S(1)}, bf16[256,128]{1,0:T(8,128)(2,1)S(1)}, bf16[256,128]{1,0:T(8,128)(2,1)S(1)}, bf16[256,128]{1,0:T(8,128)(2,1)S(1)}) custom-call(s32[32,8]{1,0:T(8,128)S(1)} %copy.16.lists_ref, s32[32]{0:T(128)S(1)} %copy-done.7, bf16[16,128,128]{2,1,0:T(8,128)(2,1)S(1)} %get-tuple-element.72.q_all, ...), custom_call_target="tpu_custom_call" | custom-call | tf_op jit(solution)/shard_map/attend/pallas_call | solution.py:343
  83.3 2.1 %collective-permute-start.19 = (bf16[256,128]{1,0:T(8,128)(2,1)S(1)}, bf16[256,128]{1,0:T(8,128)(2,1)S(1)}, u32[]{:S(2)}, u32[]{:S(2)}) collective-permute-start(bf16[256,128]{1,0:T(8,128)(2,1)S(1)} %get-tuple-element.79), channel_id=1, source_target_pairs={{0,2},{1,3},{2,0},{3,1},{4,6},{5,7},{6,4},{7,5},{8,10},{9,11},{10,... | collective-permute-start | bytes 196616 | tf_op jit(solution)/shard_map/ppermute | solution.py:658
  85.3 1.8 %collective-permute-start.20 = (bf16[256,128]{1,0:T(8,128)(2,1)S(1)}, bf16[256,128]{1,0:T(8,128)(2,1)S(1)}, u32[]{:S(2)}, u32[]{:S(2)}) collective-permute-start(bf16[256,128]{1,0:T(8,128)(2,1)S(1)} %get-tuple-element.80), channel_id=1, source_target_pairs={{0,4},{1,5},{2,6},{3,7},{4,0},{5,1},{6,2},{7,3},{8,12},{9,13},{10,... | collective-permute-start | bytes 196616 | tf_op jit(solution)/shard_map/ppermute | solution.py:658
  87.1 1.8 %collective-permute-start.22 = (bf16[256,128]{1,0:T(8,128)(2,1)S(1)}, bf16[256,128]{1,0:T(8,128)(2,1)S(1)}, u32[]{:S(2)}, u32[]{:S(2)}) collective-permute-start(bf16[256,128]{1,0:T(8,128)(2,1)S(1)} %get-tuple-element.82), channel_id=1, source_target_pairs={{0,8},{1,9},{2,10},{3,11},{4,12},{5,13},{6,14},{7,15},{8,0},{9,1},... | collective-permute-start | bytes 196616 | tf_op jit(solution)/shard_map/ppermute | solution.py:656
  88.9 2.3 %collective-permute-start.23 = (bf16[256,128]{1,0:T(8,128)(2,1)S(1)}, bf16[256,128]{1,0:T(8,128)(2,1)S(1)}, u32[]{:S(2)}, u32[]{:S(2)}) collective-permute-start(bf16[256,128]{1,0:T(8,128)(2,1)S(1)} %get-tuple-element.83), channel_id=1, source_target_pairs={{0,10},{1,11},{2,8},{3,9},{4,14},{5,15},{6,12},{7,13},{8,2},{9,3},... | collective-permute-start | bytes 196616 | tf_op jit(solution)/shard_map/ppermute | solution.py:656
  91.2 2.1 %collective-permute-start.24 = (bf16[256,128]{1,0:T(8,128)(2,1)S(1)}, bf16[256,128]{1,0:T(8,128)(2,1)S(1)}, u32[]{:S(2)}, u32[]{:S(2)}) collective-permute-start(bf16[256,128]{1,0:T(8,128)(2,1)S(1)} %get-tuple-element.84), channel_id=1, source_target_pairs={{0,12},{1,13},{2,14},{3,15},{4,8},{5,9},{6,10},{7,11},{8,4},{9,5},... | collective-permute-start | bytes 196616 | tf_op jit(solution)/shard_map/ppermute | solution.py:656
  93.3 1.4 %collective-permute-start.25 = (bf16[256,128]{1,0:T(8,128)(2,1)S(1)}, bf16[256,128]{1,0:T(8,128)(2,1)S(1)}, u32[]{:S(2)}, u32[]{:S(2)}) collective-permute-start(bf16[256,128]{1,0:T(8,128)(2,1)S(1)} %get-tuple-element.85), channel_id=1, source_target_pairs={{0,14},{1,15},{2,12},{3,13},{4,10},{5,11},{6,8},{7,9},{8,6},{9,7},... | collective-permute-start | bytes 196616 | tf_op jit(solution)/shard_map/ppermute | solution.py:656
  94.8 0.1 weave.3.refs_8_
  94.9 1.3 %collective-permute-done.22.refs_4_ = bf16[256,128]{1,0:T(8,128)(2,1)S(1)} collective-permute-done((bf16[256,128]{1,0:T(8,128)(2,1)S(1)}, bf16[256,128]{1,0:T(8,128)(2,1)S(1)}, u32[]{:S(2)}, u32[]{:S(2)}) %collective-permute-start.22) | collective-permute-done | bytes 65568 | tf_op jit(solution)/shard_map/ppermute | solution.py:656
  96.3 4.7 %collective-permute-done.23.refs_5_ = bf16[256,128]{1,0:T(8,128)(2,1)S(1)} collective-permute-done((bf16[256,128]{1,0:T(8,128)(2,1)S(1)}, bf16[256,128]{1,0:T(8,128)(2,1)S(1)}, u32[]{:S(2)}, u32[]{:S(2)}) %collective-permute-start.23) | collective-permute-done | bytes 65568 | tf_op jit(solution)/shard_map/ppermute | solution.py:656
  101.0 4.0 %tail.1 = (bf16[256,1024]{1,0:T(8,128)(2,1)}, bf16[128,1152]{1,0:T(8,128)(2,1)S(1)}, bf16[128,1152]{1,0:T(8,128)(2,1)S(1)}) custom-call(bf16[256,128]{1,0:T(8,128)(2,1)S(1)} %get-tuple-element.78.refs_0_, bf16[256,128]{1,0:T(8,128)(2,1)S(1)} %collective-permute-done.19.refs_1_, bf16[256,128]{1,0:T(8,128)(2,1)S(1)} %collective-permute-done.20.refs_2_, ...), custom_call_target="tpu_custom_call" | custom-call | tf_op jit(solution)/shard_map/tail/pallas_call | solution.py:414
  105.0 0.1 collective-permute-start.27
  105.1 1.6 %collective-permute-done.27.got_ref = bf16[128,1152]{1,0:T(8,128)(2,1)S(1)} collective-permute-done((bf16[128,1152]{1,0:T(8,128)(2,1)S(1)}, bf16[128,1152]{1,0:T(8,128)(2,1)S(1)}, u32[]{:S(2)}, u32[]{:S(2)}) %collective-permute-start.27) | collective-permute-done | bytes 294944 | tf_op jit(solution)/shard_map/ppermute | solution.py:677
  106.6 1.2 deal.1
  107.8 0.3 collective-permute-start.28
  108.1 2.8 %collective-permute-start.29 = (bf16[16,1152]{1,0:T(8,128)(2,1)S(1)}, bf16[16,1152]{1,0:T(8,128)(2,1)S(1)}, u32[]{:S(2)}, u32[]{:S(2)}) collective-permute-start(bf16[16,1152]{1,0:T(8,128)(2,1)S(1)} %get-tuple-element.94), channel_id=1, source_target_pairs={{0,4},{1,5},{2,6},{3,7},{4,0},{5,1},{6,2},{7,3},{8,12},{9,13},{10,... | collective-permute-start | bytes 110600 | tf_op jit(solution)/shard_map/ppermute | solution.py:679
  111.0 1.0 collective-permute-start.30
  112.0 1.7 %collective-permute-start.31 = (bf16[16,1152]{1,0:T(8,128)(2,1)S(1)}, bf16[16,1152]{1,0:T(8,128)(2,1)S(1)}, u32[]{:S(2)}, u32[]{:S(2)}) collective-permute-start(bf16[16,1152]{1,0:T(8,128)(2,1)S(1)} %get-tuple-element.96), channel_id=1, source_target_pairs={{0,8},{1,9},{2,10},{3,11},{4,12},{5,13},{6,14},{7,15},{8,0},{9,1},... | collective-permute-start | bytes 110600 | tf_op jit(solution)/shard_map/ppermute | solution.py:679
  113.7 1.2 collective-permute-start.32
  114.9 2.1 %collective-permute-start.33 = (bf16[16,1152]{1,0:T(8,128)(2,1)S(1)}, bf16[16,1152]{1,0:T(8,128)(2,1)S(1)}, u32[]{:S(2)}, u32[]{:S(2)}) collective-permute-start(bf16[16,1152]{1,0:T(8,128)(2,1)S(1)} %get-tuple-element.98), channel_id=1, source_target_pairs={{0,12},{1,13},{2,14},{3,15},{4,8},{5,9},{6,10},{7,11},{8,4},{9,5},... | collective-permute-start | bytes 110600 | tf_op jit(solution)/shard_map/ppermute | solution.py:679
  117.0 2.7 %collective-permute-start.34 = (bf16[16,1152]{1,0:T(8,128)(2,1)S(1)}, bf16[16,1152]{1,0:T(8,128)(2,1)S(1)}, u32[]{:S(2)}, u32[]{:S(2)}) collective-permute-start(bf16[16,1152]{1,0:T(8,128)(2,1)S(1)} %get-tuple-element.99), channel_id=1, source_target_pairs={{0,14},{1,15},{2,12},{3,13},{4,10},{5,11},{6,8},{7,9},{8,6},{9,7},... | collective-permute-start | bytes 110600 | tf_op jit(solution)/shard_map/ppermute | solution.py:679
  119.7 0.8 collective-permute-done.32.refs_5_
  120.5 0.5 collective-permute-done.33.refs_6_
  121.0 2.6 %collective-permute-done.34.refs_7_ = bf16[16,1152]{1,0:T(8,128)(2,1)S(1)} collective-permute-done((bf16[16,1152]{1,0:T(8,128)(2,1)S(1)}, bf16[16,1152]{1,0:T(8,128)(2,1)S(1)}, u32[]{:S(2)}, u32[]{:S(2)}) %collective-permute-start.34) | collective-permute-done | bytes 36896 | tf_op jit(solution)/shard_map/ppermute | solution.py:679
  123.7 1.4 %join.1 = f32[16,1024]{1,0:T(8,128)} custom-call(bf16[16,1152]{1,0:T(8,128)(2,1)S(1)} %get-tuple-element.92.refs_0_, bf16[16,1152]{1,0:T(8,128)(2,1)S(1)} %collective-permute-done.28.refs_1_, bf16[16,1152]{1,0:T(8,128)(2,1)S(1)} %collective-permute-done.29.refs_2_, bf16[16,1152]{1,0:T(8,128)(2,1)S(1)} %collective-permute-done.30.refs_3_, ...), custom_call_target="tpu_custom_call" | custom-call | tf_op jit(solution)/shard_map/join/pallas_call | solution.py:490
  (45 shorter events, 0.3 us)
Async XLA Ops:
  1.9 5.8 %collective-permute-start = (bf16[4,32,384]{2,1,0:T(8,128)(2,1)S(1)}, bf16[4,32,384]{2,1,0:T(8,128)(2,1)S(1)}, u32[]{:S(2)}, u32[]{:S(2)}) collective-permute-start(bf16[4,32,384]{2,1,0:T(8,128)(2,1)S(1)} %gather_blocks.5), channel_id=1, source_target_pairs={{0,2},{1,3},{2,0},{3,1},{4,6},{5,7},{6,4},{7,5},{8,10},{9,11},{10,... | collective-permute-start | bytes 294920 | tf_op jit(solution)/shard_map/ppermute | solution.py:544
  7.7 17.2 %collective-permute-start.1 = (bf16[288,1024]{1,0:T(8,128)(2,1)S(1)}, bf16[288,1024]{1,0:T(8,128)(2,1)S(1)}, u32[]{:S(2)}, u32[]{:S(2)}) collective-permute-start(bf16[288,1024]{1,0:T(8,128)(2,1)S(1)} %get-tuple-element.53.refs_0_.refs_1_), channel_id=1, source_target_pairs={{0,4},{1,5},{4,8},{5,9},{8,12},{9,13},{12,14},{13,15},{14,10},{15,... | collective-permute-start | bytes 1769480 | tf_op jit(solution)/shard_map/ppermute | solution.py:598
  9.6 15.3 %collective-permute-start.2 = (bf16[288,1024]{1,0:T(8,128)(2,1)S(1)}, bf16[288,1024]{1,0:T(8,128)(2,1)S(1)}, u32[]{:S(2)}, u32[]{:S(2)}) collective-permute-start(bf16[288,1024]{1,0:T(8,128)(2,1)S(1)} %get-tuple-element.53.refs_0_.refs_1_), channel_id=1, source_target_pairs={{0,2},{1,3},{4,0},{5,1},{8,4},{9,5},{12,8},{13,9},{14,12},{15,13},... | collective-permute-start | bytes 1769480 | tf_op jit(solution)/shard_map/ppermute | solution.py:599
  9.7 15.1 %collective-permute-start.3 = (bf16[2,32,384]{2,1,0:T(8,128)(2,1)S(1)}, bf16[2,32,384]{2,1,0:T(8,128)(2,1)S(1)}, u32[]{:S(2)}, u32[]{:S(2)}) collective-permute-start(bf16[2,32,384]{2,1,0:T(8,128)(2,1)S(1)} %gather_blocks.6), channel_id=1, source_target_pairs={{0,4},{1,5},{2,6},{3,7},{4,0},{5,1},{6,2},{7,3},{8,12},{9,13},{10,... | collective-permute-start | bytes 147464 | tf_op jit(solution)/shard_map/ppermute | solution.py:548
  11.6 15.2 %collective-permute-start.6 = (bf16[2,32,384]{2,1,0:T(8,128)(2,1)S(1)}, bf16[2,32,384]{2,1,0:T(8,128)(2,1)S(1)}, u32[]{:S(2)}, u32[]{:S(2)}) collective-permute-start(bf16[2,32,384]{2,1,0:T(8,128)(2,1)S(1)} %gather_blocks.7), channel_id=1, source_target_pairs={{0,8},{1,9},{2,10},{3,11},{4,12},{5,13},{6,14},{7,15},{8,0},{9,1},... | collective-permute-start | bytes 147464 | tf_op jit(solution)/shard_map/ppermute | solution.py:548
  14.2 14.2 %collective-permute-start.7 = (bf16[2,32,384]{2,1,0:T(8,128)(2,1)S(1)}, bf16[2,32,384]{2,1,0:T(8,128)(2,1)S(1)}, u32[]{:S(2)}, u32[]{:S(2)}) collective-permute-start(bf16[2,32,384]{2,1,0:T(8,128)(2,1)S(1)} %gather_blocks.8), channel_id=1, source_target_pairs={{0,12},{1,13},{2,14},{3,15},{4,8},{5,9},{6,10},{7,11},{8,4},{9,5},... | collective-permute-start | bytes 147464 | tf_op jit(solution)/shard_map/ppermute | solution.py:548
  28.5 5.7 %collective-permute-start.8 = (bf16[8,32,384]{2,1,0:T(8,128)(2,1)S(1)}, bf16[8,32,384]{2,1,0:T(8,128)(2,1)S(1)}, u32[]{:S(2)}, u32[]{:S(2)}) collective-permute-start(bf16[8,32,384]{2,1,0:T(8,128)(2,1)S(1)} %gather_blocks.9.refs_0_), channel_id=1, source_target_pairs={{0,16},{16,0},{1,17},{17,1},{2,18},{18,2},{3,19},{19,3},{4,20},{20... | collective-permute-start | bytes 589832 | tf_op jit(solution)/shard_map/ppermute | solution.py:605
  30.1 13.5 %collective-permute-start.4 = (bf16[288,1024]{1,0:T(8,128)(2,1)S(1)}, bf16[288,1024]{1,0:T(8,128)(2,1)S(1)}, u32[]{:S(2)}, u32[]{:S(2)}) collective-permute-start(bf16[288,1024]{1,0:T(8,128)(2,1)S(1)} %collective-permute-done.1.refs_2_.refs_3_), channel_id=1, source_target_pairs={{0,4},{1,5},{4,8},{5,9},{8,12},{9,13},{12,14},{13,15},{14,10},{15,... | collective-permute-start | bytes 1769480 | tf_op jit(solution)/shard_map/ppermute | solution.py:598
  30.1 13.5 %collective-permute-start.5 = (bf16[288,1024]{1,0:T(8,128)(2,1)S(1)}, bf16[288,1024]{1,0:T(8,128)(2,1)S(1)}, u32[]{:S(2)}, u32[]{:S(2)}) collective-permute-start(bf16[288,1024]{1,0:T(8,128)(2,1)S(1)} %collective-permute-done.2.refs_4_.refs_5_), channel_id=1, source_target_pairs={{0,2},{1,3},{4,0},{5,1},{8,4},{9,5},{12,8},{13,9},{14,12},{15,13},... | collective-permute-start | bytes 1769480 | tf_op jit(solution)/shard_map/ppermute | solution.py:599
  34.3 1.8 %collective-permute-start.9 = (bf16[8,2,32,384]{3,2,1,0:T(8,128)(2,1)S(1)}, bf16[8,2,32,384]{3,2,1,0:T(8,128)(2,1)S(1)}, u32[]{:S(2)}, u32[]{:S(2)}) collective-permute-start(bf16[8,2,32,384]{3,2,1,0:T(8,128)(2,1)S(1)} %pair_rows.2), channel_id=1, source_target_pairs={{0,1},{1,0},{2,3},{3,2},{4,5},{5,4},{6,7},{7,6},{8,9},{9,8},{10,11... | collective-permute-start | bytes 1179656 | tf_op jit(solution)/shard_map/ppermute | solution.py:606
  36.1 17.4 %copy-start.4 = (f32[1024]{0:T(1024)S(1)}, f32[1024]{0:T(1024)}, u32[]{:S(2)}) copy-start(f32[1024]{0:T(1024)} %param.11) | copy-start | bytes 12292
  43.6 13.4 %collective-permute-start.10 = (bf16[288,1024]{1,0:T(8,128)(2,1)S(1)}, bf16[288,1024]{1,0:T(8,128)(2,1)S(1)}, u32[]{:S(2)}, u32[]{:S(2)}) collective-permute-start(bf16[288,1024]{1,0:T(8,128)(2,1)S(1)} %collective-permute-done.4.refs_6_.refs_7_), channel_id=1, source_target_pairs={{0,4},{1,5},{4,8},{5,9},{8,12},{9,13},{12,14},{13,15},{14,10},{15,... | collective-permute-start | bytes 1769480 | tf_op jit(solution)/shard_map/ppermute | solution.py:615
  43.6 13.4 %collective-permute-start.11 = (bf16[288,1024]{1,0:T(8,128)(2,1)S(1)}, bf16[288,1024]{1,0:T(8,128)(2,1)S(1)}, u32[]{:S(2)}, u32[]{:S(2)}) collective-permute-start(bf16[288,1024]{1,0:T(8,128)(2,1)S(1)} %collective-permute-done.5.refs_8_.refs_9_), channel_id=1, source_target_pairs={{0,2},{1,3},{4,0},{5,1},{8,4},{9,5},{12,8},{13,9},{14,12},{15,13},... | collective-permute-start | bytes 1769480 | tf_op jit(solution)/shard_map/ppermute | solution.py:616
  45.6 7.1 %collective-permute-start.12 = (bf16[5,32,1024]{2,1,0:T(8,128)(2,1)S(1)}, bf16[5,32,1024]{2,1,0:T(8,128)(2,1)S(1)}, u32[]{:S(2)}, u32[]{:S(2)}) collective-permute-start(bf16[5,32,1024]{2,1,0:T(8,128)(2,1)S(1)} %collect.3.refs_0_), channel_id=1, source_target_pairs={{0,16},{16,0},{1,17},{17,1},{2,18},{18,2},{3,19},{19,3},{4,20},{20... | collective-permute-start | bytes 983048 | tf_op jit(solution)/shard_map/ppermute | solution.py:612
  52.8 0.8 copy-start.2
  57.0 6.8 %collective-permute-start.13 = (bf16[144,1024]{1,0:T(8,128)(2,1)S(1)}, bf16[144,1024]{1,0:T(8,128)(2,1)S(1)}, u32[]{:S(2)}, u32[]{:S(2)}) collective-permute-start(bf16[144,1024]{1,0:T(8,128)(2,1)S(1)} %slice.6), channel_id=1, source_target_pairs={{0,4},{1,5},{4,8},{5,9},{8,12},{9,13},{12,14},{13,15},{14,10},{15,... | collective-permute-start | bytes 884744 | tf_op jit(solution)/shard_map/ppermute | solution.py:620
  57.1 6.8 %collective-permute-start.14 = (bf16[144,1024]{1,0:T(8,128)(2,1)S(1)}, bf16[144,1024]{1,0:T(8,128)(2,1)S(1)}, u32[]{:S(2)}, u32[]{:S(2)}) collective-permute-start(bf16[144,1024]{1,0:T(8,128)(2,1)S(1)} %slice.7), channel_id=1, source_target_pairs={{0,2},{1,3},{4,0},{5,1},{8,4},{9,5},{12,8},{13,9},{14,12},{15,13},... | collective-permute-start | bytes 884744 | tf_op jit(solution)/shard_map/ppermute | solution.py:621
  63.9 5.8 %collective-permute-start.15 = (bf16[10,2,128,128]{3,2,1,0:T(8,128)(2,1)}, bf16[10,2,128,128]{3,2,1,0:T(8,128)(2,1)}, u32[]{:S(2)}, u32[]{:S(2)}) collective-permute-start(bf16[10,2,128,128]{3,2,1,0:T(8,128)(2,1)} %get-tuple-element.74), channel_id=1, source_target_pairs={{0,1},{1,0},{2,3},{3,2},{4,5},{5,4},{6,7},{7,6},{8,9},{9,8},{10,11... | collective-permute-start | bytes 1966088 | tf_op jit(solution)/shard_map/ppermute | solution.py:594
  66.3 3.4 %collective-permute-start.16 = (bf16[6,2,128,128]{3,2,1,0:T(8,128)(2,1)}, bf16[6,2,128,128]{3,2,1,0:T(8,128)(2,1)S(1)}, u32[]{:S(2)}, u32[]{:S(2)}) collective-permute-start(bf16[6,2,128,128]{3,2,1,0:T(8,128)(2,1)} %get-tuple-element.75), channel_id=1, source_target_pairs={{0,1},{1,0},{2,3},{3,2},{4,5},{5,4},{6,7},{7,6},{8,9},{9,8},{10,11... | collective-permute-start | bytes 1179656 | tf_op jit(solution)/shard_map/ppermute | solution.py:594
  66.8 9.5 %collective-permute-start.17 = (bf16[2,32,1024]{2,1,0:T(8,128)(2,1)S(1)}, bf16[2,32,1024]{2,1,0:T(8,128)(2,1)}, u32[]{:S(2)}, u32[]{:S(2)}) collective-permute-start(bf16[2,32,1024]{2,1,0:T(8,128)(2,1)S(1)} %collect.4.refs_2_), channel_id=1, source_target_pairs={{0,16},{16,0},{1,17},{17,1},{2,18},{18,2},{3,19},{19,3},{4,20},{20... | collective-permute-start | bytes 393224 | tf_op jit(solution)/shard_map/ppermute | solution.py:632
  67.8 8.6 %collective-permute-start.18 = (bf16[1,32,1024]{2,1,0:T(8,128)(2,1)S(1)}, bf16[1,32,1024]{2,1,0:T(8,128)(2,1)}, u32[]{:S(2)}, u32[]{:S(2)}) collective-permute-start(bf16[1,32,1024]{2,1,0:T(8,128)(2,1)S(1)} %collect.5.refs_4_), channel_id=1, source_target_pairs={{0,16},{16,0},{1,17},{17,1},{2,18},{18,2},{3,19},{19,3},{4,20},{20... | collective-permute-start | bytes 196616 | tf_op jit(solution)/shard_map/ppermute | solution.py:634
  69.7 6.7 %copy-start.3 = (bf16[5,32,1024]{2,1,0:T(8,128)(2,1)S(1)}, bf16[5,32,1024]{2,1,0:T(8,128)(2,1)}, u32[]{:S(2)}) copy-start(bf16[5,32,1024]{2,1,0:T(8,128)(2,1)} %copy-done.2) | copy-start | bytes 983044
  69.7 0.7 copy-start.6
  70.4 7.1 %copy-start.7 = (s32[32]{0:T(128)S(1)}, s32[32]{0:T(128)}, u32[]{:S(2)}) copy-start(s32[32]{0:T(128)} %counts_ref.3) | copy-start | bytes 388
  77.4 16.0 %collective-permute-start.26 = (bf16[8,2,32,1024]{3,2,1,0:T(8,128)(2,1)S(1)}, bf16[8,2,32,1024]{3,2,1,0:T(8,128)(2,1)S(1)}, u32[]{:S(2)}, u32[]{:S(2)}) collective-permute-start(bf16[8,2,32,1024]{3,2,1,0:T(8,128)(2,1)S(1)} %pair_rows.3), channel_id=1, source_target_pairs={{0,1},{1,0},{2,3},{3,2},{4,5},{5,4},{6,7},{7,6},{8,9},{9,8},{10,11... | collective-permute-start | bytes 3145736 | tf_op jit(solution)/shard_map/ppermute | solution.py:655
  83.3 5.6 %collective-permute-start.19 = (bf16[256,128]{1,0:T(8,128)(2,1)S(1)}, bf16[256,128]{1,0:T(8,128)(2,1)S(1)}, u32[]{:S(2)}, u32[]{:S(2)}) collective-permute-start(bf16[256,128]{1,0:T(8,128)(2,1)S(1)} %get-tuple-element.79), channel_id=1, source_target_pairs={{0,2},{1,3},{2,0},{3,1},{4,6},{5,7},{6,4},{7,5},{8,10},{9,11},{10,... | collective-permute-start | bytes 196616 | tf_op jit(solution)/shard_map/ppermute | solution.py:658
  85.3 5.9 %collective-permute-start.20 = (bf16[256,128]{1,0:T(8,128)(2,1)S(1)}, bf16[256,128]{1,0:T(8,128)(2,1)S(1)}, u32[]{:S(2)}, u32[]{:S(2)}) collective-permute-start(bf16[256,128]{1,0:T(8,128)(2,1)S(1)} %get-tuple-element.80), channel_id=1, source_target_pairs={{0,4},{1,5},{2,6},{3,7},{4,0},{5,1},{6,2},{7,3},{8,12},{9,13},{10,... | collective-permute-start | bytes 196616 | tf_op jit(solution)/shard_map/ppermute | solution.py:658
  87.1 7.8 %collective-permute-start.21 = (bf16[256,128]{1,0:T(8,128)(2,1)S(1)}, bf16[256,128]{1,0:T(8,128)(2,1)S(1)}, u32[]{:S(2)}, u32[]{:S(2)}) collective-permute-start(bf16[256,128]{1,0:T(8,128)(2,1)S(1)} %get-tuple-element.81), channel_id=1, source_target_pairs={{0,6},{1,7},{2,4},{3,5},{4,2},{5,3},{6,0},{7,1},{8,14},{9,15},{10,... | collective-permute-start | bytes 196616 | tf_op jit(solution)/shard_map/ppermute | solution.py:658
  87.1 9.2 %collective-permute-start.22 = (bf16[256,128]{1,0:T(8,128)(2,1)S(1)}, bf16[256,128]{1,0:T(8,128)(2,1)S(1)}, u32[]{:S(2)}, u32[]{:S(2)}) collective-permute-start(bf16[256,128]{1,0:T(8,128)(2,1)S(1)} %get-tuple-element.82), channel_id=1, source_target_pairs={{0,8},{1,9},{2,10},{3,11},{4,12},{5,13},{6,14},{7,15},{8,0},{9,1},... | collective-permute-start | bytes 196616 | tf_op jit(solution)/shard_map/ppermute | solution.py:656
  88.9 12.1 %collective-permute-start.23 = (bf16[256,128]{1,0:T(8,128)(2,1)S(1)}, bf16[256,128]{1,0:T(8,128)(2,1)S(1)}, u32[]{:S(2)}, u32[]{:S(2)}) collective-permute-start(bf16[256,128]{1,0:T(8,128)(2,1)S(1)} %get-tuple-element.83), channel_id=1, source_target_pairs={{0,10},{1,11},{2,8},{3,9},{4,14},{5,15},{6,12},{7,13},{8,2},{9,3},... | collective-permute-start | bytes 196616 | tf_op jit(solution)/shard_map/ppermute | solution.py:656
  91.2 9.8 %collective-permute-start.24 = (bf16[256,128]{1,0:T(8,128)(2,1)S(1)}, bf16[256,128]{1,0:T(8,128)(2,1)S(1)}, u32[]{:S(2)}, u32[]{:S(2)}) collective-permute-start(bf16[256,128]{1,0:T(8,128)(2,1)S(1)} %get-tuple-element.84), channel_id=1, source_target_pairs={{0,12},{1,13},{2,14},{3,15},{4,8},{5,9},{6,10},{7,11},{8,4},{9,5},... | collective-permute-start | bytes 196616 | tf_op jit(solution)/shard_map/ppermute | solution.py:656
  93.3 7.6 %collective-permute-start.25 = (bf16[256,128]{1,0:T(8,128)(2,1)S(1)}, bf16[256,128]{1,0:T(8,128)(2,1)S(1)}, u32[]{:S(2)}, u32[]{:S(2)}) collective-permute-start(bf16[256,128]{1,0:T(8,128)(2,1)S(1)} %get-tuple-element.85), channel_id=1, source_target_pairs={{0,14},{1,15},{2,12},{3,13},{4,10},{5,11},{6,8},{7,9},{8,6},{9,7},... | collective-permute-start | bytes 196616 | tf_op jit(solution)/shard_map/ppermute | solution.py:656
  94.8 6.2 %copy-start = (bf16[256,1024]{1,0:T(8,128)(2,1)S(1)}, bf16[256,1024]{1,0:T(8,128)(2,1)}, u32[]{:S(2)}) copy-start(bf16[256,1024]{1,0:T(8,128)(2,1)} %refs_9_.1) | copy-start | bytes 1572868
  94.8 6.2 %copy-start.1 = (bf16[256,1024]{1,0:T(8,128)(2,1)S(1)}, bf16[256,1024]{1,0:T(8,128)(2,1)}, u32[]{:S(2)}) copy-start(bf16[256,1024]{1,0:T(8,128)(2,1)} %refs_11_.1) | copy-start | bytes 1572868
  94.8 6.2 %copy-start.5 = (f32[1024]{0:T(1024)S(1)}, f32[1024]{0:T(1024)}, u32[]{:S(2)}) copy-start(f32[1024]{0:T(1024)} %param.16) | copy-start | bytes 12292
  105.0 1.6 %collective-permute-start.27 = (bf16[128,1152]{1,0:T(8,128)(2,1)S(1)}, bf16[128,1152]{1,0:T(8,128)(2,1)S(1)}, u32[]{:S(2)}, u32[]{:S(2)}) collective-permute-start(bf16[128,1152]{1,0:T(8,128)(2,1)S(1)} %get-tuple-element.91), channel_id=1, source_target_pairs={{0,1},{1,0},{2,3},{3,2},{4,5},{5,4},{6,7},{7,6},{8,9},{9,8},{10,11... | collective-permute-start | bytes 884744 | tf_op jit(solution)/shard_map/ppermute | solution.py:677
  107.8 7.1 %collective-permute-start.28 = (bf16[16,1152]{1,0:T(8,128)(2,1)S(1)}, bf16[16,1152]{1,0:T(8,128)(2,1)S(1)}, u32[]{:S(2)}, u32[]{:S(2)}) collective-permute-start(bf16[16,1152]{1,0:T(8,128)(2,1)S(1)} %get-tuple-element.93), channel_id=1, source_target_pairs={{0,2},{1,3},{2,0},{3,1},{4,6},{5,7},{6,4},{7,5},{8,10},{9,11},{10,... | collective-permute-start | bytes 110600 | tf_op jit(solution)/shard_map/ppermute | solution.py:679
  108.1 8.9 %collective-permute-start.29 = (bf16[16,1152]{1,0:T(8,128)(2,1)S(1)}, bf16[16,1152]{1,0:T(8,128)(2,1)S(1)}, u32[]{:S(2)}, u32[]{:S(2)}) collective-permute-start(bf16[16,1152]{1,0:T(8,128)(2,1)S(1)} %get-tuple-element.94), channel_id=1, source_target_pairs={{0,4},{1,5},{2,6},{3,7},{4,0},{5,1},{6,2},{7,3},{8,12},{9,13},{10,... | collective-permute-start | bytes 110600 | tf_op jit(solution)/shard_map/ppermute | solution.py:679
  111.0 8.7 %collective-permute-start.30 = (bf16[16,1152]{1,0:T(8,128)(2,1)S(1)}, bf16[16,1152]{1,0:T(8,128)(2,1)S(1)}, u32[]{:S(2)}, u32[]{:S(2)}) collective-permute-start(bf16[16,1152]{1,0:T(8,128)(2,1)S(1)} %get-tuple-element.95), channel_id=1, source_target_pairs={{0,6},{1,7},{2,4},{3,5},{4,2},{5,3},{6,0},{7,1},{8,14},{9,15},{10,... | collective-permute-start | bytes 110600 | tf_op jit(solution)/shard_map/ppermute | solution.py:679
  112.0 7.7 %collective-permute-start.31 = (bf16[16,1152]{1,0:T(8,128)(2,1)S(1)}, bf16[16,1152]{1,0:T(8,128)(2,1)S(1)}, u32[]{:S(2)}, u32[]{:S(2)}) collective-permute-start(bf16[16,1152]{1,0:T(8,128)(2,1)S(1)} %get-tuple-element.96), channel_id=1, source_target_pairs={{0,8},{1,9},{2,10},{3,11},{4,12},{5,13},{6,14},{7,15},{8,0},{9,1},... | collective-permute-start | bytes 110600 | tf_op jit(solution)/shard_map/ppermute | solution.py:679
  113.7 6.8 %collective-permute-start.32 = (bf16[16,1152]{1,0:T(8,128)(2,1)S(1)}, bf16[16,1152]{1,0:T(8,128)(2,1)S(1)}, u32[]{:S(2)}, u32[]{:S(2)}) collective-permute-start(bf16[16,1152]{1,0:T(8,128)(2,1)S(1)} %get-tuple-element.97), channel_id=1, source_target_pairs={{0,10},{1,11},{2,8},{3,9},{4,14},{5,15},{6,12},{7,13},{8,2},{9,3},... | collective-permute-start | bytes 110600 | tf_op jit(solution)/shard_map/ppermute | solution.py:679
  114.9 6.1 %collective-permute-start.33 = (bf16[16,1152]{1,0:T(8,128)(2,1)S(1)}, bf16[16,1152]{1,0:T(8,128)(2,1)S(1)}, u32[]{:S(2)}, u32[]{:S(2)}) collective-permute-start(bf16[16,1152]{1,0:T(8,128)(2,1)S(1)} %get-tuple-element.98), channel_id=1, source_target_pairs={{0,12},{1,13},{2,14},{3,15},{4,8},{5,9},{6,10},{7,11},{8,4},{9,5},... | collective-permute-start | bytes 110600 | tf_op jit(solution)/shard_map/ppermute | solution.py:679
  117.0 6.7 %collective-permute-start.34 = (bf16[16,1152]{1,0:T(8,128)(2,1)S(1)}, bf16[16,1152]{1,0:T(8,128)(2,1)S(1)}, u32[]{:S(2)}, u32[]{:S(2)}) collective-permute-start(bf16[16,1152]{1,0:T(8,128)(2,1)S(1)} %get-tuple-element.99), channel_id=1, source_target_pairs={{0,14},{1,15},{2,12},{3,13},{4,10},{5,11},{6,8},{7,9},{8,6},{9,7},... | collective-permute-start | bytes 110600 | tf_op jit(solution)/shard_map/ppermute | solution.py:679

commit v3 on v2

--- a/solution.py
+++ b/solution.py
@@ -352,13 +352,13 @@
     )(lists, counts, q_all, kv_all, *extra)
 
 
-def tail_kernel(chips, group, heads, split, *refs):
+def tail_kernel(chips, group, heads, split, parts, *refs):
     width = heads * HEAD_DIM
     sets = HEADS // heads
     piece = TOK_DEV // group
     got = refs[:chips]
-    weight_ref, tokens_ref, gain_ref, probe_ref, layer_ref = refs[chips : chips + 5]
-    part_refs, (stage,) = refs[chips + 5 : -1], refs[-1:]
+    tokens_ref, gain_ref, probe_ref, *weight_refs = refs[chips : chips + 3 + parts]
+    layer_ref, *part_refs, stage = refs[chips + 3 + parts :]
     chip, core = chip_and_core()
     for k in range(chips):
         source = lax.bitwise_xor(chip, k)
@@ -366,8 +366,24 @@
             stage[source] = got[k][...]
         else:
             stage[source // group, pl.ds(pl.multiple_of(source % group * piece, piece), piece), :] = got[k][...]
-    attended = jnp.concatenate([stage[s] for s in range(sets)], axis=1)
-    projected = jnp.dot(attended, weight_ref[...], preferred_element_type=F32)
+    if parts == 1:
+        attended = jnp.concatenate([stage[s] for s in range(sets)], axis=1)
+        projected = jnp.dot(attended, weight_refs[0][...], preferred_element_type=F32)
+    else:
+        left = lax.broadcasted_iota(jnp.int32, (TOK_DEV, width), 1) < HEAD_DIM
+        ours, theirs = [], []
+        for s in range(0, sets, 2):
+            one, two = stage[s], stage[s + 1]
+            first = jnp.where(left, one, pltpu.roll(two, HEAD_DIM, axis=1))
+            second = jnp.where(left, pltpu.roll(one, HEAD_DIM, axis=1), two)
+            ours.append(jnp.where(core == 0, first, second))
+            theirs.append(jnp.where(core == 0, second, first))
+        projected = jnp.dot(
+            jnp.concatenate(ours, axis=1), weight_refs[0][...], preferred_element_type=F32
+        )
+        projected += jnp.dot(
+            jnp.concatenate(theirs, axis=1), weight_refs[1][...], preferred_element_type=F32
+        )
     layer = (tokens_ref[...].astype(F32) + projected).astype(BF16)
     layer_ref[...] = layer
     pooled = layer_norm(layer, gain_ref[...])
@@ -408,19 +424,19 @@
     emit(D, jnp.transpose(jnp.concatenate([high, middle, low, rest], axis=0)))
 
 
-def tail(got, weight, tokens, gain, probes, chips, group, heads, split):
+def tail(got, weights, tokens, gain, probes, chips, group, heads, split):
     width = heads * HEAD_DIM
     rows = PROBES // 2 if split else PROBES
     return pl.pallas_call(
-        functools.partial(tail_kernel, chips, group, heads, split),
+        functools.partial(tail_kernel, chips, group, heads, split, len(weights)),
         out_shape=[jax.ShapeDtypeStruct((TOK_DEV, D), BF16)]
         + [jax.ShapeDtypeStruct((rows, D + STATS), BF16)] * (2 if split else 1),
-        in_specs=[whole()] * (chips + 4),
+        in_specs=[whole()] * (chips + 3 + len(weights)),
         out_specs=[whole()] * (3 if split else 2),
         scratch_shapes=[pltpu.VMEM((HEADS // heads, TOK_DEV, width), BF16)],
         compiler_params=params(),
         name="tail",
-    )(*got, weight, tokens, gain, probes)
+    )(*got, tokens, gain, probes, *weights)
 
 
 def read_logs(block):
@@ -561,7 +577,7 @@
         even = jnp.where(core == 0, here, there)
         odd = jnp.where(core == 0, there, here)
         weight = jnp.stack([even, odd], axis=1).reshape(D, 3 * width)
-        out_weight = lax.all_gather(w_out, "seq", axis=0, tiled=True)
+        out_weights = [lax.all_gather(w_out, "seq", axis=0, tiled=True)]
 
     load = load if packed else tokens
     length = load.shape[0] // 2
@@ -620,22 +636,25 @@
         lax.ppermute(forward[:length], "seq", around(1)),
         lax.ppermute(backward[length:], "seq", around(-1)),
     )
-    pair, *final = barrier((pair, *final))
-    send(pair, shards)
-    held, others = others, []
-    last = spread(forward, backward) + [(array, 0) for array in final]
-    last_shards = (chips - 3, chips - 2, chips - 1)
-    send(advance(last, last_shards), last_shards)
-    others = held + others
     if packed:
         middle = collect(spread(forward, backward), depth // 2)
         middle_twin = lax.ppermute(middle, "scan", twins)
-        late = collect(last[-2:], depth // 2)
+        q_all, kv_all, middle_twin = barrier((*state, middle_twin))
+        state = (q_all, kv_all)
+    near_shards = (chips - 3, chips - 2)
+    near = advance(spread(forward, backward), near_shards)
+    pair, near, *final = barrier((pair, near, *final))
+    send(pair, shards)
+    send(near, near_shards)
+    held, others = others, []
+    last = [(array, 0) for array in final]
+    send(advance(last, (chips - 1,)), (chips - 1,))
+    others = held + others
+    if packed:
+        late = collect(last, depth // 2)
         late_twin = lax.ppermute(late, "scan", twins)
     q_all, kv_all = state
-    far = tuple(range(chips // 2, chips))
-    near = tuple(range(chips // 2))
-    kv_all, *first = attend(
+    attended = attend(
         key_blocks,
         key_counts,
         q_all,
@@ -644,26 +663,24 @@
         chips,
         group,
         heads,
-        far,
+        tuple(range(chips)),
         tuple(held for _, held in others),
-    )
+    )[1:]
     if packed:
-        kv_all, middle_twin, late_twin = barrier((kv_all, middle_twin, late_twin))
+        first, middle_twin, late_twin = barrier((attended[0], middle_twin, late_twin))
+        attended = [first, *attended[1:]]
         own_half = pair_rows(
             [(early, early_twin), (middle, middle_twin), (late, late_twin)], chips, True
         )
         other_half = lax.ppermute(own_half, "seq", swap)
-    sent = [lax.ppermute(first[i], "seq", across(k)) for i, k in enumerate(far)]
-    second = attend(key_blocks, key_counts, q_all, kv_all, (), chips, group, heads, near, ())
-    got = [second[0]] + [lax.ppermute(second[k], "seq", across(k)) for k in near[1:]] + sent
-    if packed:
-        out_weight = weave(own_half, other_half)
+        out_weights = [half.reshape(D // 2, D) for half in (own_half, other_half)]
+    got = [attended[0]] + [lax.ppermute(attended[k], "seq", across(k)) for k in range(1, chips)]
 
     share = PROBES // ranks
     split = share % 16 == 0
     layer_out, *parts = tail(
         got,
-        out_weight,
+        out_weights,
         tokens,
         probe_gain.reshape(1, D),
         probe_queries,

time: 125 us -> 122 us (0.976)
  starting transfers between devices: 44 us -> 42.6 us
    ppermute x1, waiting for transfers between devices: 4.62 us -> 0.01 us  [per_device(): lax.ppermute(forward[:length], 'seq', around(1))]
    ppermute x1, waiting for transfers between devices: 0.01 us -> 4.47 us  [per_device(): middle_twin = lax.ppermute(middle, 'scan', twins)]
    pallas_call x2 -> x1, Pallas kernels: 11.7 us -> 10.4 us  [attend(): pl.pallas_call(functools.partial(attend_kernel, chips, group, heads, step...]
    pallas_call x2 -> x3, Pallas kernels: 5.86 us -> 6.91 us  [project(): pl.pallas_call(functools.partial(project_kernel, chips, starts, width, sh...]
  transfers between devices with their start and end apart: 35 -> 36, of which waited for: 16 -> 18; matrix products, arithmetic and copies ran while one was open for 1% -> 1% of each run, Pallas kernels for 14% -> 14%
where the time goes in v3:
time: 122 us; the launch traced here: 121 us
  waiting for transfers between devices  51 us (42%)
  starting transfers between devices  42.6 us (35%)
  Pallas kernels  25.5 us (21%)
  local copies, waits for them, and re-layouts  1.48 us (1%)
    ppermute x3, waiting for transfers between devices, per_device(): lax.ppermute(gather_blocks([(parted, 2 * k), (away, k)], False), 'seq', a...  14.2 us
    ppermute x7, starting transfers between devices, per_device(): lax.ppermute(blocks[k], 'seq', across(k))  12.4 us
    ppermute x7, starting transfers between devices, per_device(): lax.ppermute(attended[k], 'seq', across(k))  10.4 us
    pallas_call x1, Pallas kernels, attend(): pl.pallas_call(functools.partial(attend_kernel, chips, group, heads, step...  10.4 us
    ppermute x3, waiting for transfers between devices, per_device(): forward = lax.ppermute(forward, 'seq', around(1))  8.17 us
    pallas_call x3, Pallas kernels, project(): pl.pallas_call(functools.partial(project_kernel, chips, starts, width, sh...  6.91 us
    ppermute x1, waiting for transfers between devices, per_device(): early_twin = lax.ppermute(early, 'scan', twins)  6.58 us
    ppermute x7, waiting for transfers between devices, per_device(): lax.ppermute(attended[k], 'seq', across(k))  5.57 us
  transfers between devices with their start and end apart: 36, of which 18 were waited for; matrix products, arithmetic and copies ran while one was open for 1% of the time, Pallas kernels for 14%

profile of v3, /device:TPU:0, one launch (start us, length us, event | category | flops | bytes accessed | tf_op | source)
XLA Modules:
  0.0 121.4 jit_solution(16389216631009991314)
XLA Ops:
  0.6 1.2 %prepare.1 = (bf16[288,1024]{1,0:T(8,128)(2,1)S(1)}, bf16[8,32,384]{2,1,0:T(8,128)(2,1)S(1)}) custom-call(bf16[256,1024]{1,0:T(8,128)(2,1)} %refs_8_.1, bf16[64,1024]{1,0:T(8,128)(2,1)} %query_ref.1, bf16[64,1024]{1,0:T(8,128)(2,1)} %key_ref.1, bf16[64,1024]{1,0:T(8,128)(2,1)} %value_ref.1, bf16[64,1024]{1,0:T(8,128)(2,1)} %out_ref.1), custom_call_target="tpu_custom_call" | custom-call | tf_op jit(solution)/shard_map/prepare/pallas_call | solution.py:112
  1.9 3.0 %collective-permute-start = (bf16[4,32,384]{2,1,0:T(8,128)(2,1)S(1)}, bf16[4,32,384]{2,1,0:T(8,128)(2,1)S(1)}, u32[]{:S(2)}, u32[]{:S(2)}) collective-permute-start(bf16[4,32,384]{2,1,0:T(8,128)(2,1)S(1)} %gather_blocks.5), channel_id=1, source_target_pairs={{0,2},{1,3},{2,0},{3,1},{4,6},{5,7},{6,4},{7,5},{8,10},{9,11},{10,... | collective-permute-start | bytes 294920 | tf_op jit(solution)/shard_map/ppermute | solution.py:560
  4.9 2.8 %collective-permute-done.refs_1_ = bf16[4,32,384]{2,1,0:T(8,128)(2,1)S(1)} collective-permute-done((bf16[4,32,384]{2,1,0:T(8,128)(2,1)S(1)}, bf16[4,32,384]{2,1,0:T(8,128)(2,1)S(1)}, u32[]{:S(2)}, u32[]{:S(2)}) %collective-permute-start) | collective-permute-done | bytes 98336 | tf_op jit(solution)/shard_map/ppermute | solution.py:560
  7.7 1.9 %collective-permute-start.1 = (bf16[288,1024]{1,0:T(8,128)(2,1)S(1)}, bf16[288,1024]{1,0:T(8,128)(2,1)S(1)}, u32[]{:S(2)}, u32[]{:S(2)}) collective-permute-start(bf16[288,1024]{1,0:T(8,128)(2,1)S(1)} %get-tuple-element.59.refs_0_.refs_1_), channel_id=1, source_target_pairs={{0,4},{1,5},{4,8},{5,9},{8,12},{9,13},{12,14},{13,15},{14,10},{15,... | collective-permute-start | bytes 1769480 | tf_op jit(solution)/shard_map/ppermute | solution.py:614
  9.6 0.1 collective-permute-start.2
  9.7 1.9 %collective-permute-start.3 = (bf16[2,32,384]{2,1,0:T(8,128)(2,1)S(1)}, bf16[2,32,384]{2,1,0:T(8,128)(2,1)S(1)}, u32[]{:S(2)}, u32[]{:S(2)}) collective-permute-start(bf16[2,32,384]{2,1,0:T(8,128)(2,1)S(1)} %gather_blocks.6), channel_id=1, source_target_pairs={{0,4},{1,5},{2,6},{3,7},{4,0},{5,1},{6,2},{7,3},{8,12},{9,13},{10,... | collective-permute-start | bytes 147464 | tf_op jit(solution)/shard_map/ppermute | solution.py:564
  11.6 2.6 %collective-permute-start.6 = (bf16[2,32,384]{2,1,0:T(8,128)(2,1)S(1)}, bf16[2,32,384]{2,1,0:T(8,128)(2,1)S(1)}, u32[]{:S(2)}, u32[]{:S(2)}) collective-permute-start(bf16[2,32,384]{2,1,0:T(8,128)(2,1)S(1)} %gather_blocks.7), channel_id=1, source_target_pairs={{0,8},{1,9},{2,10},{3,11},{4,12},{5,13},{6,14},{7,15},{8,0},{9,1},... | collective-permute-start | bytes 147464 | tf_op jit(solution)/shard_map/ppermute | solution.py:564
  14.2 10.7 %collective-permute-done.3.refs_2_ = bf16[2,32,384]{2,1,0:T(8,128)(2,1)S(1)} collective-permute-done((bf16[2,32,384]{2,1,0:T(8,128)(2,1)S(1)}, bf16[2,32,384]{2,1,0:T(8,128)(2,1)S(1)}, u32[]{:S(2)}, u32[]{:S(2)}) %collective-permute-start.3) | collective-permute-done | bytes 49184 | tf_op jit(solution)/shard_map/ppermute | solution.py:564
  24.9 2.0 %collective-permute-done.6.refs_3_ = bf16[2,32,384]{2,1,0:T(8,128)(2,1)S(1)} collective-permute-done((bf16[2,32,384]{2,1,0:T(8,128)(2,1)S(1)}, bf16[2,32,384]{2,1,0:T(8,128)(2,1)S(1)}, u32[]{:S(2)}, u32[]{:S(2)}) %collective-permute-start.6) | collective-permute-done | bytes 49184 | tf_op jit(solution)/shard_map/ppermute | solution.py:564
  26.9 1.6 %collective-permute-done.7.refs_4_ = bf16[2,32,384]{2,1,0:T(8,128)(2,1)S(1)} collective-permute-done((bf16[2,32,384]{2,1,0:T(8,128)(2,1)S(1)}, bf16[2,32,384]{2,1,0:T(8,128)(2,1)S(1)}, u32[]{:S(2)}, u32[]{:S(2)}) %collective-permute-start.7) | collective-permute-done | bytes 49184 | tf_op jit(solution)/shard_map/ppermute | solution.py:564
  28.5 1.6 %collective-permute-start.8 = (bf16[8,32,384]{2,1,0:T(8,128)(2,1)S(1)}, bf16[8,32,384]{2,1,0:T(8,128)(2,1)S(1)}, u32[]{:S(2)}, u32[]{:S(2)}) collective-permute-start(bf16[8,32,384]{2,1,0:T(8,128)(2,1)S(1)} %gather_blocks.9.refs_0_), channel_id=1, source_target_pairs={{0,16},{16,0},{1,17},{17,1},{2,18},{18,2},{3,19},{19,3},{4,20},{20... | collective-permute-start | bytes 589832 | tf_op jit(solution)/shard_map/ppermute | solution.py:621
  30.1 2.0 %collective-permute-start.5 = (bf16[288,1024]{1,0:T(8,128)(2,1)S(1)}, bf16[288,1024]{1,0:T(8,128)(2,1)S(1)}, u32[]{:S(2)}, u32[]{:S(2)}) collective-permute-start(bf16[288,1024]{1,0:T(8,128)(2,1)S(1)} %collective-permute-done.2.refs_4_.refs_5_), channel_id=1, source_target_pairs={{0,2},{1,3},{4,0},{5,1},{8,4},{9,5},{12,8},{13,9},{14,12},{15,13},... | collective-permute-start | bytes 1769480 | tf_op jit(solution)/shard_map/ppermute | solution.py:615
  32.1 2.1 %collective-permute-done.8.refs_1_ = bf16[8,32,384]{2,1,0:T(8,128)(2,1)S(1)} collective-permute-done((bf16[8,32,384]{2,1,0:T(8,128)(2,1)S(1)}, bf16[8,32,384]{2,1,0:T(8,128)(2,1)S(1)}, u32[]{:S(2)}, u32[]{:S(2)}) %collective-permute-start.8) | collective-permute-done | bytes 196640 | tf_op jit(solution)/shard_map/ppermute | solution.py:621
  34.3 0.1 collective-permute-start.9
  34.4 1.7 %collective-permute-done.9 = bf16[8,2,32,384]{3,2,1,0:T(8,128)(2,1)S(1)} collective-permute-done((bf16[8,2,32,384]{3,2,1,0:T(8,128)(2,1)S(1)}, bf16[8,2,32,384]{3,2,1,0:T(8,128)(2,1)S(1)}, u32[]{:S(2)}, u32[]{:S(2)}) %collective-permute-start.9) | collective-permute-done | bytes 393248 | tf_op jit(solution)/shard_map/ppermute | solution.py:622
  36.1 0.1 weave.1.refs_11_.refs_5_.refs_3_
  36.1 0.0 copy-start.4
  36.2 7.4 %collective-permute-done.4.refs_6_.refs_7_ = bf16[288,1024]{1,0:T(8,128)(2,1)S(1)} collective-permute-done((bf16[288,1024]{1,0:T(8,128)(2,1)S(1)}, bf16[288,1024]{1,0:T(8,128)(2,1)S(1)}, u32[]{:S(2)}, u32[]{:S(2)}) %collective-permute-start.4) | collective-permute-done | bytes 589856 | tf_op jit(solution)/shard_map/ppermute | solution.py:614
  43.6 2.0 %collective-permute-start.11 = (bf16[288,1024]{1,0:T(8,128)(2,1)S(1)}, bf16[288,1024]{1,0:T(8,128)(2,1)S(1)}, u32[]{:S(2)}, u32[]{:S(2)}) collective-permute-start(bf16[288,1024]{1,0:T(8,128)(2,1)S(1)} %collective-permute-done.5.refs_8_.refs_9_), channel_id=1, source_target_pairs={{0,2},{1,3},{4,0},{5,1},{8,4},{9,5},{12,8},{13,9},{14,12},{15,13},... | collective-permute-start | bytes 1769480 | tf_op jit(solution)/shard_map/ppermute | solution.py:632
  45.6 0.6 collective-permute-start.12
  46.2 6.6 %collective-permute-done.12.refs_1_ = bf16[5,32,1024]{2,1,0:T(8,128)(2,1)S(1)} collective-permute-done((bf16[5,32,1024]{2,1,0:T(8,128)(2,1)S(1)}, bf16[5,32,1024]{2,1,0:T(8,128)(2,1)S(1)}, u32[]{:S(2)}, u32[]{:S(2)}) %collective-permute-start.12) | collective-permute-done | bytes 327712 | tf_op jit(solution)/shard_map/ppermute | solution.py:628
  52.8 3.5 %project.3 = (bf16[16,128,128]{2,1,0:T(8,128)(2,1)S(1)}, bf16[32,2,128,128]{3,2,1,0:T(8,128)(2,1)S(1)}, bf16[10,2,128,128]{3,2,1,0:T(8,128)(2,1)}) custom-call(bf16[288,1024]{1,0:T(8,128)(2,1)S(1)} %get-tuple-element.59.refs_0_.refs_1_, bf16[288,1024]{1,0:T(8,128)(2,1)S(1)} %get-tuple-element.59.refs_0_.refs_1_, ...), custom_call_target="tpu_custom_call" | custom-call | tf_op jit(solution)/shard_map/project/pallas_call | solution.py:257
  56.2 0.8 collective-permute-done.10.refs_0_.refs_1_
  57.0 0.1 collective-permute-start.14
  57.1 2.1 %collective-permute-start.15 = (bf16[144,1024]{1,0:T(8,128)(2,1)S(1)}, bf16[144,1024]{1,0:T(8,128)(2,1)S(1)}, u32[]{:S(2)}, u32[]{:S(2)}) collective-permute-start(bf16[144,1024]{1,0:T(8,128)(2,1)S(1)} %slice.7), channel_id=1, source_target_pairs={{0,2},{1,3},{4,0},{5,1},{8,4},{9,5},{12,8},{13,9},{14,12},{15,13},... | collective-permute-start | bytes 884744 | tf_op jit(solution)/shard_map/ppermute | solution.py:637
  59.2 0.6 collective-permute-start.13
  59.8 4.5 %collective-permute-done.13.refs_3_ = bf16[2,32,1024]{2,1,0:T(8,128)(2,1)S(1)} collective-permute-done((bf16[2,32,1024]{2,1,0:T(8,128)(2,1)S(1)}, bf16[2,32,1024]{2,1,0:T(8,128)(2,1)S(1)}, u32[]{:S(2)}, u32[]{:S(2)}) %collective-permute-start.13) | collective-permute-done | bytes 131104 | tf_op jit(solution)/shard_map/ppermute | solution.py:641
  64.2 2.0 %project.4 = (bf16[16,128,128]{2,1,0:T(8,128)(2,1)S(1)}, bf16[32,2,128,128]{3,2,1,0:T(8,128)(2,1)S(1)}, bf16[4,2,128,128]{3,2,1,0:T(8,128)(2,1)}) custom-call(bf16[288,1024]{1,0:T(8,128)(2,1)S(1)} %collective-permute-done.10.refs_0_.refs_1_, ...), custom_call_target="tpu_custom_call", output_to_operand_aliasing={{0}: (6, {}), {1}: (7, {})} | custom-call | tf_op jit(solution)/shard_map/project/pallas_call | solution.py:257
  66.2 0.1 collective-permute-start.16
  66.3 0.5 collective-permute-start.17
  66.8 1.5 %project.5 = (bf16[16,128,128]{2,1,0:T(8,128)(2,1)S(1)}, bf16[32,2,128,128]{3,2,1,0:T(8,128)(2,1)S(1)}, bf16[2,2,128,128]{3,2,1,0:T(8,128)(2,1)}) custom-call(bf16[144,1024]{1,0:T(8,128)(2,1)S(1)} %collective-permute-done.14.refs_0_, bf16[144,1024]{1,0:T(8,128)(2,1)S(1)} %collective-permute-done.15.refs_1_, ...), custom_call_target="tpu_custom_call", output_to_operand_aliasing={{0}: (4, {}), {1}: (5, {})} | custom-call | tf_op jit(solution)/shard_map/project/pallas_call | solution.py:257
  68.3 0.1 collective-permute-start.18
  68.3 0.5 collective-permute-start.19
  68.8 0.8 copy.17.lists_ref
  69.6 0.3 collective-permute-done.18.refs_3_
  70.0 0.7 copy-done.6
  70.6 10.4 %attend.1 = (bf16[32,2,128,128]{3,2,1,0:T(8,128)(2,1)S(1)}, bf16[256,128]{1,0:T(8,128)(2,1)S(1)}, bf16[256,128]{1,0:T(8,128)(2,1)S(1)}, bf16[256,128]{1,0:T(8,12...) custom-call(s32[32,8]{1,0:T(8,128)S(1)} %copy.17.lists_ref, ...), custom_call_target="tpu_custom_call", output_to_operand_aliasing={{0}: (3, {})} | custom-call | tf_op jit(solution)/shard_map/attend/pallas_call | solution.py:343
  81.0 0.1 pair_rows.3
  81.1 0.1 collective-permute-start.27
  81.2 1.7 %collective-permute-start.20 = (bf16[256,128]{1,0:T(8,128)(2,1)S(1)}, bf16[256,128]{1,0:T(8,128)(2,1)S(1)}, u32[]{:S(2)}, u32[]{:S(2)}) collective-permute-start(bf16[256,128]{1,0:T(8,128)(2,1)S(1)} %get-tuple-element.91), channel_id=1, source_target_pairs={{0,2},{1,3},{2,0},{3,1},{4,6},{5,7},{6,4},{7,5},{8,10},{9,11},{10,... | collective-permute-start | bytes 196616 | tf_op jit(solution)/shard_map/ppermute | solution.py:677
  82.9 0.0 collective-permute-start.21
  82.9 1.8 %collective-permute-start.22 = (bf16[256,128]{1,0:T(8,128)(2,1)S(1)}, bf16[256,128]{1,0:T(8,128)(2,1)S(1)}, u32[]{:S(2)}, u32[]{:S(2)}) collective-permute-start(bf16[256,128]{1,0:T(8,128)(2,1)S(1)} %get-tuple-element.93), channel_id=1, source_target_pairs={{0,6},{1,7},{2,4},{3,5},{4,2},{5,3},{6,0},{7,1},{8,14},{9,15},{10,... | collective-permute-start | bytes 196616 | tf_op jit(solution)/shard_map/ppermute | solution.py:677
  84.8 0.2 collective-permute-start.23
  84.9 0.8 collective-permute-done.20.refs_1_
  85.7 3.1 %collective-permute-start.24 = (bf16[256,128]{1,0:T(8,128)(2,1)S(1)}, bf16[256,128]{1,0:T(8,128)(2,1)S(1)}, u32[]{:S(2)}, u32[]{:S(2)}) collective-permute-start(bf16[256,128]{1,0:T(8,128)(2,1)S(1)} %get-tuple-element.95), channel_id=1, source_target_pairs={{0,10},{1,11},{2,8},{3,9},{4,14},{5,15},{6,12},{7,13},{8,2},{9,3},... | collective-permute-start | bytes 196616 | tf_op jit(solution)/shard_map/ppermute | solution.py:677
  88.8 0.4 collective-permute-start.25
  89.2 3.2 %collective-permute-start.26 = (bf16[256,128]{1,0:T(8,128)(2,1)S(1)}, bf16[256,128]{1,0:T(8,128)(2,1)S(1)}, u32[]{:S(2)}, u32[]{:S(2)}) collective-permute-start(bf16[256,128]{1,0:T(8,128)(2,1)S(1)} %get-tuple-element.97), channel_id=1, source_target_pairs={{0,14},{1,15},{2,12},{3,13},{4,10},{5,11},{6,8},{7,9},{8,6},{9,7},... | collective-permute-start | bytes 196616 | tf_op jit(solution)/shard_map/ppermute | solution.py:677
  92.4 1.5 %collective-permute-done.23.refs_4_ = bf16[256,128]{1,0:T(8,128)(2,1)S(1)} collective-permute-done((bf16[256,128]{1,0:T(8,128)(2,1)S(1)}, bf16[256,128]{1,0:T(8,128)(2,1)S(1)}, u32[]{:S(2)}, u32[]{:S(2)}) %collective-permute-start.23) | collective-permute-done | bytes 65568 | tf_op jit(solution)/shard_map/ppermute | solution.py:677
  93.9 3.3 %collective-permute-done.24.refs_5_ = bf16[256,128]{1,0:T(8,128)(2,1)S(1)} collective-permute-done((bf16[256,128]{1,0:T(8,128)(2,1)S(1)}, bf16[256,128]{1,0:T(8,128)(2,1)S(1)}, u32[]{:S(2)}, u32[]{:S(2)}) %collective-permute-start.24) | collective-permute-done | bytes 65568 | tf_op jit(solution)/shard_map/ppermute | solution.py:677
  97.2 4.1 %tail.1 = (bf16[256,1024]{1,0:T(8,128)(2,1)}, bf16[128,1152]{1,0:T(8,128)(2,1)S(1)}, bf16[128,1152]{1,0:T(8,128)(2,1)S(1)}) custom-call(bf16[256,128]{1,0:T(8,128)(2,1)S(1)} %get-tuple-element.90.refs_0_, bf16[256,128]{1,0:T(8,128)(2,1)S(1)} %collective-permute-done.20.refs_1_, bf16[256,128]{1,0:T(8,128)(2,1)S(1)} %collective-permute-done.21.refs_2_, ...), custom_call_target="tpu_custom_call" | custom-call | tf_op jit(solution)/shard_map/tail/pallas_call | solution.py:430
  101.3 0.1 collective-permute-start.28
  101.4 1.6 %collective-permute-done.28.got_ref = bf16[128,1152]{1,0:T(8,128)(2,1)S(1)} collective-permute-done((bf16[128,1152]{1,0:T(8,128)(2,1)S(1)}, bf16[128,1152]{1,0:T(8,128)(2,1)S(1)}, u32[]{:S(2)}, u32[]{:S(2)}) %collective-permute-start.28) | collective-permute-done | bytes 294944 | tf_op jit(solution)/shard_map/ppermute | solution.py:694
  103.0 1.2 deal.1
  104.2 1.0 collective-permute-start.29
  105.2 2.8 %collective-permute-start.30 = (bf16[16,1152]{1,0:T(8,128)(2,1)S(1)}, bf16[16,1152]{1,0:T(8,128)(2,1)S(1)}, u32[]{:S(2)}, u32[]{:S(2)}) collective-permute-start(bf16[16,1152]{1,0:T(8,128)(2,1)S(1)} %get-tuple-element.106), channel_id=1, source_target_pairs={{0,4},{1,5},{2,6},{3,7},{4,0},{5,1},{6,2},{7,3},{8,12},{9,13},{10,... | collective-permute-start | bytes 110600 | tf_op jit(solution)/shard_map/ppermute | solution.py:696
  108.0 0.9 collective-permute-start.31
  108.9 1.5 %collective-permute-start.32 = (bf16[16,1152]{1,0:T(8,128)(2,1)S(1)}, bf16[16,1152]{1,0:T(8,128)(2,1)S(1)}, u32[]{:S(2)}, u32[]{:S(2)}) collective-permute-start(bf16[16,1152]{1,0:T(8,128)(2,1)S(1)} %get-tuple-element.108), channel_id=1, source_target_pairs={{0,8},{1,9},{2,10},{3,11},{4,12},{5,13},{6,14},{7,15},{8,0},{9,1},... | collective-permute-start | bytes 110600 | tf_op jit(solution)/shard_map/ppermute | solution.py:696
  110.5 1.4 %collective-permute-start.33 = (bf16[16,1152]{1,0:T(8,128)(2,1)S(1)}, bf16[16,1152]{1,0:T(8,128)(2,1)S(1)}, u32[]{:S(2)}, u32[]{:S(2)}) collective-permute-start(bf16[16,1152]{1,0:T(8,128)(2,1)S(1)} %get-tuple-element.109), channel_id=1, source_target_pairs={{0,10},{1,11},{2,8},{3,9},{4,14},{5,15},{6,12},{7,13},{8,2},{9,3},... | collective-permute-start | bytes 110600 | tf_op jit(solution)/shard_map/ppermute | solution.py:696
  111.9 1.5 %collective-permute-start.34 = (bf16[16,1152]{1,0:T(8,128)(2,1)S(1)}, bf16[16,1152]{1,0:T(8,128)(2,1)S(1)}, u32[]{:S(2)}, u32[]{:S(2)}) collective-permute-start(bf16[16,1152]{1,0:T(8,128)(2,1)S(1)} %get-tuple-element.110), channel_id=1, source_target_pairs={{0,12},{1,13},{2,14},{3,15},{4,8},{5,9},{6,10},{7,11},{8,4},{9,5},... | collective-permute-start | bytes 110600 | tf_op jit(solution)/shard_map/ppermute | solution.py:696
  113.3 3.3 %collective-permute-start.35 = (bf16[16,1152]{1,0:T(8,128)(2,1)S(1)}, bf16[16,1152]{1,0:T(8,128)(2,1)S(1)}, u32[]{:S(2)}, u32[]{:S(2)}) collective-permute-start(bf16[16,1152]{1,0:T(8,128)(2,1)S(1)} %get-tuple-element.111), channel_id=1, source_target_pairs={{0,14},{1,15},{2,12},{3,13},{4,10},{5,11},{6,8},{7,9},{8,6},{9,7},... | collective-permute-start | bytes 110600 | tf_op jit(solution)/shard_map/ppermute | solution.py:696
  116.6 0.8 collective-permute-done.33.refs_5_
  117.4 0.6 collective-permute-done.34.refs_6_
  118.0 2.0 %collective-permute-done.35.refs_7_ = bf16[16,1152]{1,0:T(8,128)(2,1)S(1)} collective-permute-done((bf16[16,1152]{1,0:T(8,128)(2,1)S(1)}, bf16[16,1152]{1,0:T(8,128)(2,1)S(1)}, u32[]{:S(2)}, u32[]{:S(2)}) %collective-permute-start.35) | collective-permute-done | bytes 36896 | tf_op jit(solution)/shard_map/ppermute | solution.py:696
  120.0 1.4 %join.1 = f32[16,1024]{1,0:T(8,128)} custom-call(bf16[16,1152]{1,0:T(8,128)(2,1)S(1)} %get-tuple-element.104.refs_0_, bf16[16,1152]{1,0:T(8,128)(2,1)S(1)} %collective-permute-done.29.refs_1_, bf16[16,1152]{1,0:T(8,128)(2,1)S(1)} %collective-permute-done.30.refs_2_, bf16[16,1152]{1,0:T(8,128)(2,1)S(1)} %collective-permute-done.31.refs_3_, ...), custom_call_target="tpu_custom_call" | custom-call | tf_op jit(solution)/shard_map/join/pallas_call | solution.py:506
  (44 shorter events, 0.3 us)
Async XLA Ops:
  1.9 5.8 %collective-permute-start = (bf16[4,32,384]{2,1,0:T(8,128)(2,1)S(1)}, bf16[4,32,384]{2,1,0:T(8,128)(2,1)S(1)}, u32[]{:S(2)}, u32[]{:S(2)}) collective-permute-start(bf16[4,32,384]{2,1,0:T(8,128)(2,1)S(1)} %gather_blocks.5), channel_id=1, source_target_pairs={{0,2},{1,3},{2,0},{3,1},{4,6},{5,7},{6,4},{7,5},{8,10},{9,11},{10,... | collective-permute-start | bytes 294920 | tf_op jit(solution)/shard_map/ppermute | solution.py:560
  7.7 17.2 %collective-permute-start.1 = (bf16[288,1024]{1,0:T(8,128)(2,1)S(1)}, bf16[288,1024]{1,0:T(8,128)(2,1)S(1)}, u32[]{:S(2)}, u32[]{:S(2)}) collective-permute-start(bf16[288,1024]{1,0:T(8,128)(2,1)S(1)} %get-tuple-element.59.refs_0_.refs_1_), channel_id=1, source_target_pairs={{0,4},{1,5},{4,8},{5,9},{8,12},{9,13},{12,14},{13,15},{14,10},{15,... | collective-permute-start | bytes 1769480 | tf_op jit(solution)/shard_map/ppermute | solution.py:614
  9.6 15.3 %collective-permute-start.2 = (bf16[288,1024]{1,0:T(8,128)(2,1)S(1)}, bf16[288,1024]{1,0:T(8,128)(2,1)S(1)}, u32[]{:S(2)}, u32[]{:S(2)}) collective-permute-start(bf16[288,1024]{1,0:T(8,128)(2,1)S(1)} %get-tuple-element.59.refs_0_.refs_1_), channel_id=1, source_target_pairs={{0,2},{1,3},{4,0},{5,1},{8,4},{9,5},{12,8},{13,9},{14,12},{15,13},... | collective-permute-start | bytes 1769480 | tf_op jit(solution)/shard_map/ppermute | solution.py:615
  9.7 15.1 %collective-permute-start.3 = (bf16[2,32,384]{2,1,0:T(8,128)(2,1)S(1)}, bf16[2,32,384]{2,1,0:T(8,128)(2,1)S(1)}, u32[]{:S(2)}, u32[]{:S(2)}) collective-permute-start(bf16[2,32,384]{2,1,0:T(8,128)(2,1)S(1)} %gather_blocks.6), channel_id=1, source_target_pairs={{0,4},{1,5},{2,6},{3,7},{4,0},{5,1},{6,2},{7,3},{8,12},{9,13},{10,... | collective-permute-start | bytes 147464 | tf_op jit(solution)/shard_map/ppermute | solution.py:564
  11.6 15.2 %collective-permute-start.6 = (bf16[2,32,384]{2,1,0:T(8,128)(2,1)S(1)}, bf16[2,32,384]{2,1,0:T(8,128)(2,1)S(1)}, u32[]{:S(2)}, u32[]{:S(2)}) collective-permute-start(bf16[2,32,384]{2,1,0:T(8,128)(2,1)S(1)} %gather_blocks.7), channel_id=1, source_target_pairs={{0,8},{1,9},{2,10},{3,11},{4,12},{5,13},{6,14},{7,15},{8,0},{9,1},... | collective-permute-start | bytes 147464 | tf_op jit(solution)/shard_map/ppermute | solution.py:564
  14.2 14.2 %collective-permute-start.7 = (bf16[2,32,384]{2,1,0:T(8,128)(2,1)S(1)}, bf16[2,32,384]{2,1,0:T(8,128)(2,1)S(1)}, u32[]{:S(2)}, u32[]{:S(2)}) collective-permute-start(bf16[2,32,384]{2,1,0:T(8,128)(2,1)S(1)} %gather_blocks.8), channel_id=1, source_target_pairs={{0,12},{1,13},{2,14},{3,15},{4,8},{5,9},{6,10},{7,11},{8,4},{9,5},... | collective-permute-start | bytes 147464 | tf_op jit(solution)/shard_map/ppermute | solution.py:564
  28.5 5.7 %collective-permute-start.8 = (bf16[8,32,384]{2,1,0:T(8,128)(2,1)S(1)}, bf16[8,32,384]{2,1,0:T(8,128)(2,1)S(1)}, u32[]{:S(2)}, u32[]{:S(2)}) collective-permute-start(bf16[8,32,384]{2,1,0:T(8,128)(2,1)S(1)} %gather_blocks.9.refs_0_), channel_id=1, source_target_pairs={{0,16},{16,0},{1,17},{17,1},{2,18},{18,2},{3,19},{19,3},{4,20},{20... | collective-permute-start | bytes 589832 | tf_op jit(solution)/shard_map/ppermute | solution.py:621
  30.1 13.5 %collective-permute-start.4 = (bf16[288,1024]{1,0:T(8,128)(2,1)S(1)}, bf16[288,1024]{1,0:T(8,128)(2,1)S(1)}, u32[]{:S(2)}, u32[]{:S(2)}) collective-permute-start(bf16[288,1024]{1,0:T(8,128)(2,1)S(1)} %collective-permute-done.1.refs_2_.refs_3_), channel_id=1, source_target_pairs={{0,4},{1,5},{4,8},{5,9},{8,12},{9,13},{12,14},{13,15},{14,10},{15,... | collective-permute-start | bytes 1769480 | tf_op jit(solution)/shard_map/ppermute | solution.py:614
  30.1 13.5 %collective-permute-start.5 = (bf16[288,1024]{1,0:T(8,128)(2,1)S(1)}, bf16[288,1024]{1,0:T(8,128)(2,1)S(1)}, u32[]{:S(2)}, u32[]{:S(2)}) collective-permute-start(bf16[288,1024]{1,0:T(8,128)(2,1)S(1)} %collective-permute-done.2.refs_4_.refs_5_), channel_id=1, source_target_pairs={{0,2},{1,3},{4,0},{5,1},{8,4},{9,5},{12,8},{13,9},{14,12},{15,13},... | collective-permute-start | bytes 1769480 | tf_op jit(solution)/shard_map/ppermute | solution.py:615
  34.3 1.8 %collective-permute-start.9 = (bf16[8,2,32,384]{3,2,1,0:T(8,128)(2,1)S(1)}, bf16[8,2,32,384]{3,2,1,0:T(8,128)(2,1)S(1)}, u32[]{:S(2)}, u32[]{:S(2)}) collective-permute-start(bf16[8,2,32,384]{3,2,1,0:T(8,128)(2,1)S(1)} %pair_rows.2), channel_id=1, source_target_pairs={{0,1},{1,0},{2,3},{3,2},{4,5},{5,4},{6,7},{7,6},{8,9},{9,8},{10,11... | collective-permute-start | bytes 1179656 | tf_op jit(solution)/shard_map/ppermute | solution.py:622
  36.1 16.6 %copy-start.4 = (f32[1024]{0:T(1024)S(1)}, f32[1024]{0:T(1024)}, u32[]{:S(2)}) copy-start(f32[1024]{0:T(1024)} %param.11) | copy-start | bytes 12292
  43.6 13.4 %collective-permute-start.10 = (bf16[288,1024]{1,0:T(8,128)(2,1)S(1)}, bf16[288,1024]{1,0:T(8,128)(2,1)S(1)}, u32[]{:S(2)}, u32[]{:S(2)}) collective-permute-start(bf16[288,1024]{1,0:T(8,128)(2,1)S(1)} %collective-permute-done.4.refs_6_.refs_7_), channel_id=1, source_target_pairs={{0,4},{1,5},{4,8},{5,9},{8,12},{9,13},{12,14},{13,15},{14,10},{15,... | collective-permute-start | bytes 1769480 | tf_op jit(solution)/shard_map/ppermute | solution.py:631
  43.6 13.4 %collective-permute-start.11 = (bf16[288,1024]{1,0:T(8,128)(2,1)S(1)}, bf16[288,1024]{1,0:T(8,128)(2,1)S(1)}, u32[]{:S(2)}, u32[]{:S(2)}) collective-permute-start(bf16[288,1024]{1,0:T(8,128)(2,1)S(1)} %collective-permute-done.5.refs_8_.refs_9_), channel_id=1, source_target_pairs={{0,2},{1,3},{4,0},{5,1},{8,4},{9,5},{12,8},{13,9},{14,12},{15,13},... | collective-permute-start | bytes 1769480 | tf_op jit(solution)/shard_map/ppermute | solution.py:632
  45.6 7.1 %collective-permute-start.12 = (bf16[5,32,1024]{2,1,0:T(8,128)(2,1)S(1)}, bf16[5,32,1024]{2,1,0:T(8,128)(2,1)S(1)}, u32[]{:S(2)}, u32[]{:S(2)}) collective-permute-start(bf16[5,32,1024]{2,1,0:T(8,128)(2,1)S(1)} %collect.3.refs_0_), channel_id=1, source_target_pairs={{0,16},{16,0},{1,17},{17,1},{2,18},{18,2},{3,19},{19,3},{4,20},{20... | collective-permute-start | bytes 983048 | tf_op jit(solution)/shard_map/ppermute | solution.py:628
  57.0 9.2 %collective-permute-start.14 = (bf16[144,1024]{1,0:T(8,128)(2,1)S(1)}, bf16[144,1024]{1,0:T(8,128)(2,1)S(1)}, u32[]{:S(2)}, u32[]{:S(2)}) collective-permute-start(bf16[144,1024]{1,0:T(8,128)(2,1)S(1)} %slice.6), channel_id=1, source_target_pairs={{0,4},{1,5},{4,8},{5,9},{8,12},{9,13},{12,14},{13,15},{14,10},{15,... | collective-permute-start | bytes 884744 | tf_op jit(solution)/shard_map/ppermute | solution.py:636
  57.1 9.1 %collective-permute-start.15 = (bf16[144,1024]{1,0:T(8,128)(2,1)S(1)}, bf16[144,1024]{1,0:T(8,128)(2,1)S(1)}, u32[]{:S(2)}, u32[]{:S(2)}) collective-permute-start(bf16[144,1024]{1,0:T(8,128)(2,1)S(1)} %slice.7), channel_id=1, source_target_pairs={{0,2},{1,3},{4,0},{5,1},{8,4},{9,5},{12,8},{13,9},{14,12},{15,13},... | collective-permute-start | bytes 884744 | tf_op jit(solution)/shard_map/ppermute | solution.py:637
  59.2 5.0 %collective-permute-start.13 = (bf16[2,32,1024]{2,1,0:T(8,128)(2,1)S(1)}, bf16[2,32,1024]{2,1,0:T(8,128)(2,1)S(1)}, u32[]{:S(2)}, u32[]{:S(2)}) collective-permute-start(bf16[2,32,1024]{2,1,0:T(8,128)(2,1)S(1)} %collect.4.refs_2_), channel_id=1, source_target_pairs={{0,16},{16,0},{1,17},{17,1},{2,18},{18,2},{3,19},{19,3},{4,20},{20... | collective-permute-start | bytes 393224 | tf_op jit(solution)/shard_map/ppermute | solution.py:641
  64.2 2.0 %copy-start.2 = (bf16[2,32,1024]{2,1,0:T(8,128)(2,1)}, bf16[2,32,1024]{2,1,0:T(8,128)(2,1)S(1)}, u32[]{:S(2)}) copy-start(bf16[2,32,1024]{2,1,0:T(8,128)(2,1)S(1)} %collective-permute-done.13.refs_3_) | copy-start | bytes 393220
  66.2 3.7 %collective-permute-start.16 = (bf16[10,2,128,128]{3,2,1,0:T(8,128)(2,1)}, bf16[10,2,128,128]{3,2,1,0:T(8,128)(2,1)}, u32[]{:S(2)}, u32[]{:S(2)}) collective-permute-start(bf16[10,2,128,128]{3,2,1,0:T(8,128)(2,1)} %get-tuple-element.85), channel_id=1, source_target_pairs={{0,1},{1,0},{2,3},{3,2},{4,5},{5,4},{6,7},{7,6},{8,9},{9,8},{10,11... | collective-permute-start | bytes 1966088 | tf_op jit(solution)/shard_map/ppermute | solution.py:610
  66.3 3.7 %collective-permute-start.17 = (bf16[4,2,128,128]{3,2,1,0:T(8,128)(2,1)}, bf16[4,2,128,128]{3,2,1,0:T(8,128)(2,1)}, u32[]{:S(2)}, u32[]{:S(2)}) collective-permute-start(bf16[4,2,128,128]{3,2,1,0:T(8,128)(2,1)} %get-tuple-element.86), channel_id=1, source_target_pairs={{0,1},{1,0},{2,3},{3,2},{4,5},{5,4},{6,7},{7,6},{8,9},{9,8},{10,11... | collective-permute-start | bytes 786440 | tf_op jit(solution)/shard_map/ppermute | solution.py:610
  68.3 1.7 %collective-permute-start.18 = (bf16[2,2,128,128]{3,2,1,0:T(8,128)(2,1)}, bf16[2,2,128,128]{3,2,1,0:T(8,128)(2,1)}, u32[]{:S(2)}, u32[]{:S(2)}) collective-permute-start(bf16[2,2,128,128]{3,2,1,0:T(8,128)(2,1)} %get-tuple-element.87), channel_id=1, source_target_pairs={{0,1},{1,0},{2,3},{3,2},{4,5},{5,4},{6,7},{7,6},{8,9},{9,8},{10,11... | collective-permute-start | bytes 393224 | tf_op jit(solution)/shard_map/ppermute | solution.py:610
  68.3 12.7 %collective-permute-start.19 = (bf16[1,32,1024]{2,1,0:T(8,128)(2,1)S(1)}, bf16[1,32,1024]{2,1,0:T(8,128)(2,1)S(1)}, u32[]{:S(2)}, u32[]{:S(2)}) collective-permute-start(bf16[1,32,1024]{2,1,0:T(8,128)(2,1)S(1)} %collect.5.refs_4_), channel_id=1, source_target_pairs={{0,16},{16,0},{1,17},{17,1},{2,18},{18,2},{3,19},{19,3},{4,20},{20... | collective-permute-start | bytes 196616 | tf_op jit(solution)/shard_map/ppermute | solution.py:655
  69.6 11.4 %copy-start.3 = (bf16[2,32,1024]{2,1,0:T(8,128)(2,1)S(1)}, bf16[2,32,1024]{2,1,0:T(8,128)(2,1)}, u32[]{:S(2)}) copy-start(bf16[2,32,1024]{2,1,0:T(8,128)(2,1)} %copy-done.2) | copy-start | bytes 393220
  70.0 0.7 copy-start.6
  70.6 26.6 %copy-start = (bf16[256,1024]{1,0:T(8,128)(2,1)S(1)}, bf16[256,1024]{1,0:T(8,128)(2,1)}, u32[]{:S(2)}) copy-start(bf16[256,1024]{1,0:T(8,128)(2,1)} %refs_8_.1) | copy-start | bytes 1572868
  70.6 26.6 %copy-start.1 = (bf16[256,1024]{1,0:T(8,128)(2,1)S(1)}, bf16[256,1024]{1,0:T(8,128)(2,1)}, u32[]{:S(2)}) copy-start(bf16[256,1024]{1,0:T(8,128)(2,1)} %refs_10_.1) | copy-start | bytes 1572868
  70.6 26.6 %copy-start.5 = (f32[1024]{0:T(1024)S(1)}, f32[1024]{0:T(1024)}, u32[]{:S(2)}) copy-start(f32[1024]{0:T(1024)} %param.16) | copy-start | bytes 12292
  81.1 16.1 %collective-permute-start.27 = (bf16[8,2,32,1024]{3,2,1,0:T(8,128)(2,1)S(1)}, bf16[8,2,32,1024]{3,2,1,0:T(8,128)(2,1)S(1)}, u32[]{:S(2)}, u32[]{:S(2)}) collective-permute-start(bf16[8,2,32,1024]{3,2,1,0:T(8,128)(2,1)S(1)} %pair_rows.3), channel_id=1, source_target_pairs={{0,1},{1,0},{2,3},{3,2},{4,5},{5,4},{6,7},{7,6},{8,9},{9,8},{10,11... | collective-permute-start | bytes 3145736 | tf_op jit(solution)/shard_map/ppermute | solution.py:675
  81.2 4.5 %collective-permute-start.20 = (bf16[256,128]{1,0:T(8,128)(2,1)S(1)}, bf16[256,128]{1,0:T(8,128)(2,1)S(1)}, u32[]{:S(2)}, u32[]{:S(2)}) collective-permute-start(bf16[256,128]{1,0:T(8,128)(2,1)S(1)} %get-tuple-element.91), channel_id=1, source_target_pairs={{0,2},{1,3},{2,0},{3,1},{4,6},{5,7},{6,4},{7,5},{8,10},{9,11},{10,... | collective-permute-start | bytes 196616 | tf_op jit(solution)/shard_map/ppermute | solution.py:677
  82.9 5.9 %collective-permute-start.21 = (bf16[256,128]{1,0:T(8,128)(2,1)S(1)}, bf16[256,128]{1,0:T(8,128)(2,1)S(1)}, u32[]{:S(2)}, u32[]{:S(2)}) collective-permute-start(bf16[256,128]{1,0:T(8,128)(2,1)S(1)} %get-tuple-element.92), channel_id=1, source_target_pairs={{0,4},{1,5},{2,6},{3,7},{4,0},{5,1},{6,2},{7,3},{8,12},{9,13},{10,... | collective-permute-start | bytes 196616 | tf_op jit(solution)/shard_map/ppermute | solution.py:677
  82.9 6.2 %collective-permute-start.22 = (bf16[256,128]{1,0:T(8,128)(2,1)S(1)}, bf16[256,128]{1,0:T(8,128)(2,1)S(1)}, u32[]{:S(2)}, u32[]{:S(2)}) collective-permute-start(bf16[256,128]{1,0:T(8,128)(2,1)S(1)} %get-tuple-element.93), channel_id=1, source_target_pairs={{0,6},{1,7},{2,4},{3,5},{4,2},{5,3},{6,0},{7,1},{8,14},{9,15},{10,... | collective-permute-start | bytes 196616 | tf_op jit(solution)/shard_map/ppermute | solution.py:677
  84.8 9.1 %collective-permute-start.23 = (bf16[256,128]{1,0:T(8,128)(2,1)S(1)}, bf16[256,128]{1,0:T(8,128)(2,1)S(1)}, u32[]{:S(2)}, u32[]{:S(2)}) collective-permute-start(bf16[256,128]{1,0:T(8,128)(2,1)S(1)} %get-tuple-element.94), channel_id=1, source_target_pairs={{0,8},{1,9},{2,10},{3,11},{4,12},{5,13},{6,14},{7,15},{8,0},{9,1},... | collective-permute-start | bytes 196616 | tf_op jit(solution)/shard_map/ppermute | solution.py:677
  85.7 11.5 %collective-permute-start.24 = (bf16[256,128]{1,0:T(8,128)(2,1)S(1)}, bf16[256,128]{1,0:T(8,128)(2,1)S(1)}, u32[]{:S(2)}, u32[]{:S(2)}) collective-permute-start(bf16[256,128]{1,0:T(8,128)(2,1)S(1)} %get-tuple-element.95), channel_id=1, source_target_pairs={{0,10},{1,11},{2,8},{3,9},{4,14},{5,15},{6,12},{7,13},{8,2},{9,3},... | collective-permute-start | bytes 196616 | tf_op jit(solution)/shard_map/ppermute | solution.py:677
  88.8 8.4 %collective-permute-start.25 = (bf16[256,128]{1,0:T(8,128)(2,1)S(1)}, bf16[256,128]{1,0:T(8,128)(2,1)S(1)}, u32[]{:S(2)}, u32[]{:S(2)}) collective-permute-start(bf16[256,128]{1,0:T(8,128)(2,1)S(1)} %get-tuple-element.96), channel_id=1, source_target_pairs={{0,12},{1,13},{2,14},{3,15},{4,8},{5,9},{6,10},{7,11},{8,4},{9,5},... | collective-permute-start | bytes 196616 | tf_op jit(solution)/shard_map/ppermute | solution.py:677
  89.2 8.0 %collective-permute-start.26 = (bf16[256,128]{1,0:T(8,128)(2,1)S(1)}, bf16[256,128]{1,0:T(8,128)(2,1)S(1)}, u32[]{:S(2)}, u32[]{:S(2)}) collective-permute-start(bf16[256,128]{1,0:T(8,128)(2,1)S(1)} %get-tuple-element.97), channel_id=1, source_target_pairs={{0,14},{1,15},{2,12},{3,13},{4,10},{5,11},{6,8},{7,9},{8,6},{9,7},... | collective-permute-start | bytes 196616 | tf_op jit(solution)/shard_map/ppermute | solution.py:677
  101.3 1.6 %collective-permute-start.28 = (bf16[128,1152]{1,0:T(8,128)(2,1)S(1)}, bf16[128,1152]{1,0:T(8,128)(2,1)S(1)}, u32[]{:S(2)}, u32[]{:S(2)}) collective-permute-start(bf16[128,1152]{1,0:T(8,128)(2,1)S(1)} %get-tuple-element.103), channel_id=1, source_target_pairs={{0,1},{1,0},{2,3},{3,2},{4,5},{5,4},{6,7},{7,6},{8,9},{9,8},{10,11... | collective-permute-start | bytes 884744 | tf_op jit(solution)/shard_map/ppermute | solution.py:694
  104.2 7.7 %collective-permute-start.29 = (bf16[16,1152]{1,0:T(8,128)(2,1)S(1)}, bf16[16,1152]{1,0:T(8,128)(2,1)S(1)}, u32[]{:S(2)}, u32[]{:S(2)}) collective-permute-start(bf16[16,1152]{1,0:T(8,128)(2,1)S(1)} %get-tuple-element.105), channel_id=1, source_target_pairs={{0,2},{1,3},{2,0},{3,1},{4,6},{5,7},{6,4},{7,5},{8,10},{9,11},{10,... | collective-permute-start | bytes 110600 | tf_op jit(solution)/shard_map/ppermute | solution.py:696
  105.2 8.1 %collective-permute-start.30 = (bf16[16,1152]{1,0:T(8,128)(2,1)S(1)}, bf16[16,1152]{1,0:T(8,128)(2,1)S(1)}, u32[]{:S(2)}, u32[]{:S(2)}) collective-permute-start(bf16[16,1152]{1,0:T(8,128)(2,1)S(1)} %get-tuple-element.106), channel_id=1, source_target_pairs={{0,4},{1,5},{2,6},{3,7},{4,0},{5,1},{6,2},{7,3},{8,12},{9,13},{10,... | collective-permute-start | bytes 110600 | tf_op jit(solution)/shard_map/ppermute | solution.py:696
  108.0 8.6 %collective-permute-start.31 = (bf16[16,1152]{1,0:T(8,128)(2,1)S(1)}, bf16[16,1152]{1,0:T(8,128)(2,1)S(1)}, u32[]{:S(2)}, u32[]{:S(2)}) collective-permute-start(bf16[16,1152]{1,0:T(8,128)(2,1)S(1)} %get-tuple-element.107), channel_id=1, source_target_pairs={{0,6},{1,7},{2,4},{3,5},{4,2},{5,3},{6,0},{7,1},{8,14},{9,15},{10,... | collective-permute-start | bytes 110600 | tf_op jit(solution)/shard_map/ppermute | solution.py:696
  108.9 7.7 %collective-permute-start.32 = (bf16[16,1152]{1,0:T(8,128)(2,1)S(1)}, bf16[16,1152]{1,0:T(8,128)(2,1)S(1)}, u32[]{:S(2)}, u32[]{:S(2)}) collective-permute-start(bf16[16,1152]{1,0:T(8,128)(2,1)S(1)} %get-tuple-element.108), channel_id=1, source_target_pairs={{0,8},{1,9},{2,10},{3,11},{4,12},{5,13},{6,14},{7,15},{8,0},{9,1},... | collective-permute-start | bytes 110600 | tf_op jit(solution)/shard_map/ppermute | solution.py:696
  110.5 6.9 %collective-permute-start.33 = (bf16[16,1152]{1,0:T(8,128)(2,1)S(1)}, bf16[16,1152]{1,0:T(8,128)(2,1)S(1)}, u32[]{:S(2)}, u32[]{:S(2)}) collective-permute-start(bf16[16,1152]{1,0:T(8,128)(2,1)S(1)} %get-tuple-element.109), channel_id=1, source_target_pairs={{0,10},{1,11},{2,8},{3,9},{4,14},{5,15},{6,12},{7,13},{8,2},{9,3},... | collective-permute-start | bytes 110600 | tf_op jit(solution)/shard_map/ppermute | solution.py:696
  111.9 6.1 %collective-permute-start.34 = (bf16[16,1152]{1,0:T(8,128)(2,1)S(1)}, bf16[16,1152]{1,0:T(8,128)(2,1)S(1)}, u32[]{:S(2)}, u32[]{:S(2)}) collective-permute-start(bf16[16,1152]{1,0:T(8,128)(2,1)S(1)} %get-tuple-element.110), channel_id=1, source_target_pairs={{0,12},{1,13},{2,14},{3,15},{4,8},{5,9},{6,10},{7,11},{8,4},{9,5},... | collective-permute-start | bytes 110600 | tf_op jit(solution)/shard_map/ppermute | solution.py:696
  113.3 6.7 %collective-permute-start.35 = (bf16[16,1152]{1,0:T(8,128)(2,1)S(1)}, bf16[16,1152]{1,0:T(8,128)(2,1)S(1)}, u32[]{:S(2)}, u32[]{:S(2)}) collective-permute-start(bf16[16,1152]{1,0:T(8,128)(2,1)S(1)} %get-tuple-element.111), channel_id=1, source_target_pairs={{0,14},{1,15},{2,12},{3,13},{4,10},{5,11},{6,8},{7,9},{8,6},{9,7},... | collective-permute-start | bytes 110600 | tf_op jit(solution)/shard_map/ppermute | solution.py:696

commit v4 on v3

--- a/solution.py
+++ b/solution.py
@@ -77,50 +77,112 @@
 
 
 def prepare_kernel(
-    chips, width, tokens_ref, query_ref, key_ref, value_ref, out_ref, load_ref, cut_ref, rows_ref, sems
+    width, tokens_ref, query_ref, key_ref, value_ref, out_ref, load_ref, mine_ref, theirs_ref, rows_ref, sems
 ):
-    chip, _ = chip_and_core()
-    mine = twin()
+    chip, core = chip_and_core()
     rows = out_ref.shape[0] // 4
     half = TOK_DEV // 2
     step = half + rows
     copies = []
-    for i, ref in enumerate((query_ref, key_ref, value_ref)):
-        start = pl.multiple_of(mine * (2 * rows), 2 * rows)
-        copies.append((ref.at[pl.ds(start, 2 * rows), :], rows_ref.at[i]))
     for part in range(2):
-        start = pl.multiple_of(mine * (2 * rows) + part * rows, rows)
+        start = pl.multiple_of(twin() * (2 * rows) + part * rows, rows)
         to = load_ref.at[part * step : part * step + half, :]
         copies.append((tokens_ref.at[part * half : (part + 1) * half, :], to))
         to = load_ref.at[part * step + half : (part + 1) * step, :]
         copies.append((out_ref.at[pl.ds(start, rows), :], to))
+    for i, ref in enumerate((query_ref, key_ref, value_ref)):
+        copies.append((ref, rows_ref.at[i]))
     copies = [pltpu.make_async_copy(a, b, sems.at[i]) for i, (a, b) in enumerate(copies)]
     for copy in copies:
         copy.start()
-    for copy in copies[:3]:
+    for copy in copies:
         copy.wait()
-    for k in range(chips):
-        lanes = pl.ds(pl.multiple_of(lax.bitwise_xor(chip, k) * width, width), width)
-        for i in range(3):
-            cut_ref[k, :, i * width : (i + 1) * width] = rows_ref[i, :, lanes]
-    for copy in copies[3:]:
-        copy.wait()
-
-
-def prepare(tokens, weights, out_weight, chips, width):
+    for ref, side in ((mine_ref, core), (theirs_ref, 1 - core)):
+        for j in range(2):
+            target = lax.bitwise_xor(chip, 2 * twin() + side + 4 * j)
+            lanes = pl.ds(pl.multiple_of(target * width, width), width)
+            for i in range(3):
+                ref[j, :, i * width : (i + 1) * width] = rows_ref[i, :, lanes]
+
+
+def prepare(tokens, weights, out_weight, width):
     rows = out_weight.shape[0] // 2
-    return pl.pallas_call(
-        functools.partial(prepare_kernel, chips, width),
-        out_shape=(
-            jax.ShapeDtypeStruct((TOK_DEV + rows, D), BF16),
-            jax.ShapeDtypeStruct((chips, rows, 3 * width), BF16),
-        ),
+    block = jax.ShapeDtypeStruct((2, 2 * rows, 3 * width), BF16)
+    return pl.pallas_call(
+        functools.partial(prepare_kernel, width),
+        out_shape=(jax.ShapeDtypeStruct((TOK_DEV + rows, D), BF16), block, block),
         in_specs=[pl.BlockSpec(memory_space=pltpu.HBM)] * 5,
-        out_specs=(whole(), whole()),
-        scratch_shapes=[pltpu.VMEM((3, rows, D), BF16), pltpu.SemaphoreType.DMA((7,))],
+        out_specs=(whole(),) * 3,
+        scratch_shapes=[pltpu.VMEM((3, 2 * rows, D), BF16), pltpu.SemaphoreType.DMA((7,))],
         compiler_params=params(),
         name="prepare",
     )(*(pltpu.with_memory_space_constraint(x, pltpu.HBM) for x in (tokens, *weights, out_weight)))
+
+
+def bundle_kernel(mine_ref, got_ref, *outs):
+    _, core = chip_and_core()
+    rows = mine_ref.shape[1]
+    for j, ref in enumerate(outs):
+        mine, got = mine_ref[j], got_ref[j]
+        ref[:rows, :] = jnp.where(core == 0, mine, got)
+        ref[rows:, :] = jnp.where(core == 0, got, mine)
+
+
+def bundle(mine, got):
+    _, rows, columns = mine.shape
+    return pl.pallas_call(
+        bundle_kernel,
+        out_shape=[jax.ShapeDtypeStruct((2 * rows, columns), BF16)] * 2,
+        in_specs=[whole()] * 2,
+        out_specs=[whole()] * 2,
+        compiler_params=params(),
+        name="bundle",
+    )(mine, got)
+
+
+def keep_kernel(own_ref, near_ref, far_ref, out_ref):
+    _, core = chip_and_core()
+    out_ref[0] = jnp.where(2 * twin() + core == 0, own_ref[...], near_ref[...])
+    out_ref[1] = far_ref[...]
+
+
+def keep(own, near, far):
+    return pl.pallas_call(
+        keep_kernel,
+        out_shape=jax.ShapeDtypeStruct((2,) + own.shape, BF16),
+        in_specs=[whole()] * 3,
+        out_specs=whole(),
+        compiler_params=params(),
+        name="keep",
+    )(own, near, far)
+
+
+def assemble_kernel(own_ref, twin_ref, other_ref, out_ref, stage):
+    chip, core = chip_and_core()
+    role = 2 * twin() + core
+    for j in range(2):
+        for flip, block in (
+            (0, own_ref[j]),
+            (2, twin_ref[j]),
+            (1, other_ref[j]),
+            (3, other_ref[2 + j]),
+        ):
+            source = lax.bitwise_xor(chip, lax.bitwise_xor(role, flip) + 4 * j)
+            stage[source] = block
+    out_ref[...] = stage[...].reshape(out_ref.shape)
+
+
+def assemble(own, twin_blocks, other):
+    _, rows, columns = own.shape
+    return pl.pallas_call(
+        assemble_kernel,
+        out_shape=jax.ShapeDtypeStruct((8 * rows, columns), BF16),
+        in_specs=[whole()] * 3,
+        out_specs=whole(),
+        scratch_shapes=[pltpu.VMEM((8, rows, columns), BF16)],
+        compiler_params=params(),
+        name="assemble",
+    )(own, twin_blocks, other)
 
 
 def gather_blocks_kernel(picks, ordered, *refs):
@@ -394,13 +456,16 @@
         if not split:
             part_refs[0][:, lo:hi] = value.astype(BF16)
             return
-        share = PROBES // (2 * chips)
-        shaped = value.reshape(chips, 2, share, value.shape[1])
-        first, second = shaped[:, 0], shaped[:, 1]
-        mine = jnp.where(core == 0, first, second)
-        theirs = jnp.where(core == 0, second, first)
-        part_refs[0][:, lo:hi] = mine.reshape(chips * share, -1).astype(BF16)
-        part_refs[1][:, lo:hi] = theirs.reshape(chips * share, -1).astype(BF16)
+        lines, share = chips // 2, PROBES // (2 * chips)
+        shaped = value.reshape(lines, 2, 2, share, value.shape[1])
+        side = lax.bitwise_and(chip, 1)
+        near = jnp.where(side == 0, shaped[:, 0], shaped[:, 1])
+        far = jnp.where(side == 0, shaped[:, 1], shaped[:, 0])
+        for i, rows_of in enumerate((near, far)):
+            mine = jnp.where(core == 0, rows_of[:, 0], rows_of[:, 1])
+            theirs = jnp.where(core == 0, rows_of[:, 1], rows_of[:, 0])
+            part_refs[2 * i][:, lo:hi] = mine.reshape(lines * share, -1).astype(BF16)
+            part_refs[2 * i + 1][:, lo:hi] = theirs.reshape(lines * share, -1).astype(BF16)
 
     for pair in range(HEADS // 2):
         lo = pair * 2 * HEAD_DIM
@@ -426,13 +491,13 @@
 
 def tail(got, weights, tokens, gain, probes, chips, group, heads, split):
     width = heads * HEAD_DIM
-    rows = PROBES // 2 if split else PROBES
+    rows = PROBES // 4 if split else PROBES
     return pl.pallas_call(
         functools.partial(tail_kernel, chips, group, heads, split, len(weights)),
         out_shape=[jax.ShapeDtypeStruct((TOK_DEV, D), BF16)]
-        + [jax.ShapeDtypeStruct((rows, D + STATS), BF16)] * (2 if split else 1),
+        + [jax.ShapeDtypeStruct((rows, D + STATS), BF16)] * (4 if split else 1),
         in_specs=[whole()] * (chips + 3 + len(weights)),
-        out_specs=[whole()] * (3 if split else 2),
+        out_specs=[whole()] * (5 if split else 2),
         scratch_shapes=[pltpu.VMEM((HEADS // heads, TOK_DEV, width), BF16)],
         compiler_params=params(),
         name="tail",
@@ -476,26 +541,27 @@
     ).astype(BF16)
 
 
-def deal_kernel(mine_ref, got_ref, *outs_and_stage):
-    outs, stage = outs_and_stage[:-1], outs_and_stage[-1]
+def deal_kernel(count, *refs):
+    outs, stage = refs[count:-1], refs[-1]
     chip, _ = chip_and_core()
-    packed = repack(*blend([mine_ref[...], got_ref[...]]))
+    line = lax.shift_right_logical(chip, 1)
+    packed = repack(*blend([ref[...] for ref in refs[:count]]))
     stage[...] = packed.reshape(stage.shape)
     for k in range(len(outs)):
-        outs[k][...] = stage[lax.bitwise_xor(chip, k)]
-
-
-def deal(mine, got, parts):
-    share = mine.shape[0] // parts
-    return pl.pallas_call(
-        deal_kernel,
+        outs[k][...] = stage[lax.bitwise_xor(line, k)]
+
+
+def deal(blocks, parts):
+    share = blocks[0].shape[0] // parts
+    return pl.pallas_call(
+        functools.partial(deal_kernel, len(blocks)),
         out_shape=[jax.ShapeDtypeStruct((share, D + STATS), BF16)] * parts,
-        in_specs=[whole(), whole()],
+        in_specs=[whole()] * len(blocks),
         out_specs=[whole()] * parts,
         scratch_shapes=[pltpu.VMEM((parts, share, D + STATS), BF16)],
         compiler_params=params(),
         name="deal",
-    )(mine, got)
+    )(*blocks)
 
 
 def last_kernel(*refs):
@@ -552,20 +618,22 @@
     depth = w_query.shape[0]
     gain = ln_gain.reshape(1, D)
     half = TOK_DEV // 2
-    packed = depth % 64 == 0
+    packed = depth == 64 and chips == 8
 
     if packed:
-        load, parted = prepare(tokens, (w_query, w_key, w_value), w_out, chips, width)
-        line = range(chips // 2)
-        away = lax.ppermute(
-            gather_blocks([(parted, k) for k in range(1, chips, 2)], False), "seq", across(1)
-        )
-        moved = [
-            lax.ppermute(
-                gather_blocks([(parted, 2 * k), (away, k)], False), "seq", across(2 * k)
-            )
-            for k in line[1:]
-        ]
+        load, mine, theirs = prepare(tokens, (w_query, w_key, w_value), w_out, width)
+        sent = bundle(mine, lax.ppermute(theirs, "seq", swap))
+
+        def serve(offset):
+            pairs = []
+            for x in range(lax.axis_size("scan")):
+                for rank in range(ranks):
+                    flip = 2 * (x & 1) + (rank & 1) + offset
+                    if flip:
+                        pairs.append((x * ranks + rank, x * ranks + (rank ^ (2 * flip))))
+            return pairs
+
+        moved = [lax.ppermute(sent[j], ("scan", "seq"), serve(4 * j)) for j in range(2)]
     else:
         columns = jnp.stack([w_query, w_key, w_value]).reshape(3, depth, sets, width)
         columns = jnp.transpose(columns, (2, 1, 0, 3)).reshape(sets, depth, 3 * width)
@@ -581,8 +649,6 @@
 
     load = load if packed else tokens
     length = load.shape[0] // 2
-    if packed:
-        load, away = barrier((load, away))
     forward = backward = load
 
     def spread(*shards):
@@ -614,12 +680,14 @@
         forward = lax.ppermute(forward, "seq", around(1))
         backward = lax.ppermute(backward, "seq", around(-1))
         if packed and s == 1:
-            forward, backward, moved[0] = barrier((forward, backward, moved[0]))
+            forward, backward, *moved = barrier((forward, backward, *moved))
         if packed and s == 2:
-            sources = [(parted, 0), (away, 0)] + [(m, j) for m in moved for j in range(2)]
-            quarter = gather_blocks(sources, True)
-            own_half = pair_rows([(quarter, lax.ppermute(quarter, "scan", twins))], chips, False)
-            weight = weave(own_half, lax.ppermute(own_half, "seq", swap))
+            blocks = keep(sent[0], *moved)
+            twin_blocks = lax.ppermute(blocks, "scan", twins)
+            joint = gather_blocks(
+                [(blocks, 0), (blocks, 1), (twin_blocks, 0), (twin_blocks, 1)], False
+            )
+            weight = assemble(blocks, twin_blocks, lax.ppermute(joint, "seq", swap))
             forward, backward, weight = barrier((forward, backward, weight))
         arrived += spread(forward, backward)
         shards += (2 * s - 1, 2 * s)
@@ -690,10 +758,16 @@
         split,
     )
     if split:
-        mine, theirs = parts
-        blocks = deal(mine, lax.ppermute(theirs, "seq", swap), chips)
-        joined = [blocks[0]] + [
-            lax.ppermute(blocks[k], "seq", across(k)) for k in range(1, chips)
+        mine, core_part, side_part, both_part = parts
+        blocks = [
+            mine,
+            lax.ppermute(side_part, "seq", across(1)),
+            lax.ppermute(both_part, "seq", [(i, i ^ 3) for i in range(ranks)]),
+            lax.ppermute(core_part, "seq", swap),
+        ]
+        lines = deal(blocks, chips // 2)
+        joined = [lines[0]] + [
+            lax.ppermute(lines[k], "seq", across(2 * k)) for k in range(1, chips // 2)
         ]
         return layer_out, join(joined)
     rows = lax.all_to_all(

time: 122 us -> 120 us (0.984)
  starting transfers between devices: 42.6 us -> 35.3 us
  waiting for transfers between devices: 51 us -> 56.4 us
    ppermute x14 -> x11, starting transfers between devices: 21.7 us -> 14.1 us  [the longest x3 5.46 us: per_device(): lax.ppermute(lines[k], 'seq', across(2 * k))]
    ppermute x14 -> x11, waiting for transfers between devices: 25.8 us -> 28.2 us  [the longest x2 14.9 us: per_device(): lax.ppermute(sent[j], ('scan', 'seq'), serve(4 * j))]
    ppermute x3, waiting for transfers between devices: 8.17 us -> 9.93 us  [per_device(): forward = lax.ppermute(forward, 'seq', around(1))]
    ppermute x3, starting transfers between devices: 1.89 us -> 3.58 us  [per_device(): forward = lax.ppermute(forward, 'seq', around(1))]
    pallas_call x3 -> x5, Pallas kernels: 2.48 us -> 2.66 us  [the longest x1 1.29 us: prepare(): pl.pallas_call(functools.partial(prepare_kernel, width), out_shape=(jax.S...]
  transfers between devices with their start and end apart: 36 -> 33, of which waited for: 18 -> 16; matrix products, arithmetic and copies ran while one was open for 1% -> 1% of each run, Pallas kernels for 14% -> 15%
where the time goes in v4:
time: 120 us
  waiting for transfers between devices  56.4 us (47%)
  starting transfers between devices  35.3 us (29%)
  Pallas kernels  25.8 us (22%)
  local copies, waits for them, and re-layouts  1.48 us (1%)
    ppermute x2, waiting for transfers between devices, per_device(): lax.ppermute(sent[j], ('scan', 'seq'), serve(4 * j))  14.9 us
    pallas_call x1, Pallas kernels, attend(): pl.pallas_call(functools.partial(attend_kernel, chips, group, heads, step...  10.9 us
    ppermute x7, starting transfers between devices, per_device(): lax.ppermute(attended[k], 'seq', across(k))  10.3 us
    ppermute x3, waiting for transfers between devices, per_device(): forward = lax.ppermute(forward, 'seq', around(1))  9.93 us
    pallas_call x3, Pallas kernels, project(): pl.pallas_call(functools.partial(project_kernel, chips, starts, width, sh...  6.9 us
    ppermute x1, waiting for transfers between devices, per_device(): early_twin = lax.ppermute(early, 'scan', twins)  6.88 us
    ppermute x7, waiting for transfers between devices, per_device(): lax.ppermute(attended[k], 'seq', across(k))  6.01 us
    ppermute x3, starting transfers between devices, per_device(): lax.ppermute(lines[k], 'seq', across(2 * k))  5.46 us
  transfers between devices with their start and end apart: 33, of which 16 were waited for; matrix products, arithmetic and copies ran while one was open for 1% of the time, Pallas kernels for 15%

profile of v4, /device:TPU:0, one launch (start us, length us, event | category | flops | bytes accessed | tf_op | source)
XLA Modules:
  0.0 119.9 jit_solution(9664131769511687680)
XLA Ops:
  0.6 1.3 %prepare.1 = (bf16[288,1024]{1,0:T(8,128)(2,1)S(1)}, bf16[2,64,384]{2,1,0:T(8,128)(2,1)S(1)}, bf16[2,64,384]{2,1,0:T(8,128)(2,1)S(1)}) custom-call(bf16[256,1024]{1,0:T(8,128)(2,1)} %refs_8_.1, bf16[64,1024]{1,0:T(8,128)(2,1)} %query_ref.1, bf16[64,1024]{1,0:T(8,128)(2,1)} %key_ref.1, bf16[64,1024]{1,0:T(8,128)(2,1)} %value_ref.1, bf16[64,1024]{1,0:T(8,128)(2,1)} %out_ref.1), custom_call_target="tpu_custom_call" | custom-call | tf_op jit(solution)/shard_map/prepare/pallas_call | solution.py:111
  1.9 3.1 %collective-permute-start = (bf16[288,1024]{1,0:T(8,128)(2,1)S(1)}, bf16[288,1024]{1,0:T(8,128)(2,1)S(1)}, u32[]{:S(2)}, u32[]{:S(2)}) collective-permute-start(bf16[288,1024]{1,0:T(8,128)(2,1)S(1)} %get-tuple-element.57.refs_0_.refs_1_), channel_id=1, source_target_pairs={{0,4},{1,5},{4,8},{5,9},{8,12},{9,13},{12,14},{13,15},{14,10},{15,... | collective-permute-start | bytes 1769480 | tf_op jit(solution)/shard_map/ppermute | solution.py:680
  5.0 0.0 collective-permute-start.1
  5.0 0.0 collective-permute-start.2
  5.0 1.3 %collective-permute-done.2.got_ref = bf16[2,64,384]{2,1,0:T(8,128)(2,1)S(1)} collective-permute-done((bf16[2,64,384]{2,1,0:T(8,128)(2,1)S(1)}, bf16[2,64,384]{2,1,0:T(8,128)(2,1)S(1)}, u32[]{:S(2)}, u32[]{:S(2)}) %collective-permute-start.2) | collective-permute-done | bytes 98336 | tf_op jit(solution)/shard_map/ppermute | solution.py:625
  6.4 0.7 collective-permute-start.3
  7.0 3.1 %collective-permute-start.4 = (bf16[128,384]{1,0:T(8,128)(2,1)S(1)}, bf16[128,384]{1,0:T(8,128)(2,1)S(1)}, u32[]{:S(2)}, u32[]{:S(2)}) collective-permute-start(bf16[128,384]{1,0:T(8,128)(2,1)S(1)} %get-tuple-element.61), channel_id=1, source_target_pairs={{0,8},{1,11},{2,10},{3,9},{4,12},{5,15},{6,14},{7,13},{8,0},{9,3},... | collective-permute-start | bytes 294920 | tf_op jit(solution)/shard_map/ppermute | solution.py:636
  10.1 14.9 %collective-permute-done.4.far_ref = bf16[128,384]{1,0:T(8,128)(2,1)S(1)} collective-permute-done((bf16[128,384]{1,0:T(8,128)(2,1)S(1)}, bf16[128,384]{1,0:T(8,128)(2,1)S(1)}, u32[]{:S(2)}, u32[]{:S(2)}) %collective-permute-start.4) | collective-permute-done | bytes 98336 | tf_op jit(solution)/shard_map/ppermute | solution.py:636
  25.1 2.6 %collective-permute-start.7 = (bf16[2,128,384]{2,1,0:T(8,128)(2,1)S(1)}, bf16[2,128,384]{2,1,0:T(8,128)(2,1)S(1)}, u32[]{:S(2)}, u32[]{:S(2)}) collective-permute-start(bf16[2,128,384]{2,1,0:T(8,128)(2,1)S(1)} %keep.1.refs_0_.own_ref), channel_id=1, source_target_pairs={{0,16},{16,0},{1,17},{17,1},{2,18},{18,2},{3,19},{19,3},{4,20},{20... | collective-permute-start | bytes 589832 | tf_op jit(solution)/shard_map/ppermute | solution.py:686
  27.6 2.0 %collective-permute-start.6 = (bf16[288,1024]{1,0:T(8,128)(2,1)S(1)}, bf16[288,1024]{1,0:T(8,128)(2,1)S(1)}, u32[]{:S(2)}, u32[]{:S(2)}) collective-permute-start(bf16[288,1024]{1,0:T(8,128)(2,1)S(1)} %collective-permute-done.1.refs_4_.refs_5_), channel_id=1, source_target_pairs={{0,2},{1,3},{4,0},{5,1},{8,4},{9,5},{12,8},{13,9},{14,12},{15,13},... | collective-permute-start | bytes 1769480 | tf_op jit(solution)/shard_map/ppermute | solution.py:681
  29.7 1.6 %collective-permute-done.7.refs_1_.twin_ref = bf16[2,128,384]{2,1,0:T(8,128)(2,1)S(1)} collective-permute-done((bf16[2,128,384]{2,1,0:T(8,128)(2,1)S(1)}, bf16[2,128,384]{2,1,0:T(8,128)(2,1)S(1)}, u32[]{:S(2)}, u32[]{:S(2)}) %collective-permute-start.7) | collective-permute-done | bytes 196640 | tf_op jit(solution)/shard_map/ppermute | solution.py:686
  31.3 0.1 collective-permute-start.8
  31.4 1.7 %collective-permute-done.8.other_ref = bf16[4,128,384]{2,1,0:T(8,128)(2,1)S(1)} collective-permute-done((bf16[4,128,384]{2,1,0:T(8,128)(2,1)S(1)}, bf16[4,128,384]{2,1,0:T(8,128)(2,1)S(1)}, u32[]{:S(2)}, u32[]{:S(2)}) %collective-permute-start.8) | collective-permute-done | bytes 393248 | tf_op jit(solution)/shard_map/ppermute | solution.py:690
  33.1 0.2 assemble.1.refs_11_.refs_5_.refs_3_
  33.3 0.0 copy-start.4
  33.3 7.6 %collective-permute-done.5.refs_6_.refs_7_ = bf16[288,1024]{1,0:T(8,128)(2,1)S(1)} collective-permute-done((bf16[288,1024]{1,0:T(8,128)(2,1)S(1)}, bf16[288,1024]{1,0:T(8,128)(2,1)S(1)}, u32[]{:S(2)}, u32[]{:S(2)}) %collective-permute-start.5) | collective-permute-done | bytes 589856 | tf_op jit(solution)/shard_map/ppermute | solution.py:680
  40.9 0.2 collective-permute-done.6.refs_8_.refs_9_
  41.1 1.5 %collective-permute-start.10 = (bf16[288,1024]{1,0:T(8,128)(2,1)S(1)}, bf16[288,1024]{1,0:T(8,128)(2,1)S(1)}, u32[]{:S(2)}, u32[]{:S(2)}) collective-permute-start(bf16[288,1024]{1,0:T(8,128)(2,1)S(1)} %collective-permute-done.6.refs_8_.refs_9_), channel_id=1, source_target_pairs={{0,2},{1,3},{4,0},{5,1},{8,4},{9,5},{12,8},{13,9},{14,12},{15,13},... | collective-permute-start | bytes 1769480 | tf_op jit(solution)/shard_map/ppermute | solution.py:700
  42.7 0.5 collective-permute-start.9
  43.2 0.3 collective-permute-start.11
  43.4 6.9 %collective-permute-done.11.refs_1_ = bf16[5,32,1024]{2,1,0:T(8,128)(2,1)S(1)} collective-permute-done((bf16[5,32,1024]{2,1,0:T(8,128)(2,1)S(1)}, bf16[5,32,1024]{2,1,0:T(8,128)(2,1)S(1)}, u32[]{:S(2)}, u32[]{:S(2)}) %collective-permute-start.11) | collective-permute-done | bytes 327712 | tf_op jit(solution)/shard_map/ppermute | solution.py:696
  50.3 3.5 %project.3 = (bf16[16,128,128]{2,1,0:T(8,128)(2,1)S(1)}, bf16[32,2,128,128]{3,2,1,0:T(8,128)(2,1)S(1)}, bf16[10,2,128,128]{3,2,1,0:T(8,128)(2,1)}) custom-call(bf16[288,1024]{1,0:T(8,128)(2,1)S(1)} %get-tuple-element.57.refs_0_.refs_1_, bf16[288,1024]{1,0:T(8,128)(2,1)S(1)} %get-tuple-element.57.refs_0_.refs_1_, ...), custom_call_target="tpu_custom_call" | custom-call | tf_op jit(solution)/shard_map/project/pallas_call | solution.py:319
  53.8 0.0 collective-permute-done.10.refs_2_.refs_3_
  53.8 2.3 %collective-permute-done.9.refs_0_.refs_1_ = bf16[288,1024]{1,0:T(8,128)(2,1)S(1)} collective-permute-done((bf16[288,1024]{1,0:T(8,128)(2,1)S(1)}, bf16[288,1024]{1,0:T(8,128)(2,1)S(1)}, u32[]{:S(2)}, u32[]{:S(2)}) %collective-permute-start.9) | collective-permute-done | bytes 589856 | tf_op jit(solution)/shard_map/ppermute | solution.py:699
  56.1 0.3 collective-permute-start.13
  56.5 1.8 %collective-permute-start.14 = (bf16[144,1024]{1,0:T(8,128)(2,1)S(1)}, bf16[144,1024]{1,0:T(8,128)(2,1)S(1)}, u32[]{:S(2)}, u32[]{:S(2)}) collective-permute-start(bf16[144,1024]{1,0:T(8,128)(2,1)S(1)} %slice.7), channel_id=1, source_target_pairs={{0,2},{1,3},{4,0},{5,1},{8,4},{9,5},{12,8},{13,9},{14,12},{15,13},... | collective-permute-start | bytes 884744 | tf_op jit(solution)/shard_map/ppermute | solution.py:705
  58.3 0.4 collective-permute-start.12
  58.7 4.6 %collective-permute-done.12.refs_3_ = bf16[2,32,1024]{2,1,0:T(8,128)(2,1)S(1)} collective-permute-done((bf16[2,32,1024]{2,1,0:T(8,128)(2,1)S(1)}, bf16[2,32,1024]{2,1,0:T(8,128)(2,1)S(1)}, u32[]{:S(2)}, u32[]{:S(2)}) %collective-permute-start.12) | collective-permute-done | bytes 131104 | tf_op jit(solution)/shard_map/ppermute | solution.py:709
  63.3 2.0 %project.4 = (bf16[16,128,128]{2,1,0:T(8,128)(2,1)S(1)}, bf16[32,2,128,128]{3,2,1,0:T(8,128)(2,1)S(1)}, bf16[4,2,128,128]{3,2,1,0:T(8,128)(2,1)}) custom-call(bf16[288,1024]{1,0:T(8,128)(2,1)S(1)} %collective-permute-done.9.refs_0_.refs_1_, ...), custom_call_target="tpu_custom_call", output_to_operand_aliasing={{0}: (6, {}), {1}: (7, {})} | custom-call | tf_op jit(solution)/shard_map/project/pallas_call | solution.py:319
  65.3 0.0 collective-permute-done.13.refs_0_
  65.3 0.0 collective-permute-done.14.refs_1_
  65.3 0.1 collective-permute-start.15
  65.4 0.5 collective-permute-start.16
  65.9 1.5 %project.5 = (bf16[16,128,128]{2,1,0:T(8,128)(2,1)S(1)}, bf16[32,2,128,128]{3,2,1,0:T(8,128)(2,1)S(1)}, bf16[2,2,128,128]{3,2,1,0:T(8,128)(2,1)}) custom-call(bf16[144,1024]{1,0:T(8,128)(2,1)S(1)} %collective-permute-done.13.refs_0_, bf16[144,1024]{1,0:T(8,128)(2,1)S(1)} %collective-permute-done.14.refs_1_, ...), custom_call_target="tpu_custom_call", output_to_operand_aliasing={{0}: (4, {}), {1}: (5, {})} | custom-call | tf_op jit(solution)/shard_map/project/pallas_call | solution.py:319
  67.3 0.1 collective-permute-start.17
  67.4 0.3 collective-permute-start.18
  67.8 0.8 copy.17.lists_ref
  68.5 0.5 collective-permute-done.17.refs_3_
  69.0 0.0 collective-permute-done.16.refs_2_
  69.0 0.0 collective-permute-done.15.refs_1_
  69.0 0.7 copy-done.6
  69.7 10.9 %attend.1 = (bf16[32,2,128,128]{3,2,1,0:T(8,128)(2,1)S(1)}, bf16[256,128]{1,0:T(8,128)(2,1)S(1)}, bf16[256,128]{1,0:T(8,128)(2,1)S(1)}, bf16[256,128]{1,0:T(8,12...) custom-call(s32[32,8]{1,0:T(8,128)S(1)} %copy.17.lists_ref, ...), custom_call_target="tpu_custom_call", output_to_operand_aliasing={{0}: (3, {})} | custom-call | tf_op jit(solution)/shard_map/attend/pallas_call | solution.py:405
  80.6 0.1 pair_rows.1
  80.7 0.1 collective-permute-start.26
  80.8 1.6 %collective-permute-start.19 = (bf16[256,128]{1,0:T(8,128)(2,1)S(1)}, bf16[256,128]{1,0:T(8,128)(2,1)S(1)}, u32[]{:S(2)}, u32[]{:S(2)}) collective-permute-start(bf16[256,128]{1,0:T(8,128)(2,1)S(1)} %get-tuple-element.93), channel_id=1, source_target_pairs={{0,2},{1,3},{2,0},{3,1},{4,6},{5,7},{6,4},{7,5},{8,10},{9,11},{10,... | collective-permute-start | bytes 196616 | tf_op jit(solution)/shard_map/ppermute | solution.py:745
  82.4 0.3 collective-permute-start.20
  82.6 1.7 %collective-permute-start.21 = (bf16[256,128]{1,0:T(8,128)(2,1)S(1)}, bf16[256,128]{1,0:T(8,128)(2,1)S(1)}, u32[]{:S(2)}, u32[]{:S(2)}) collective-permute-start(bf16[256,128]{1,0:T(8,128)(2,1)S(1)} %get-tuple-element.95), channel_id=1, source_target_pairs={{0,6},{1,7},{2,4},{3,5},{4,2},{5,3},{6,0},{7,1},{8,14},{9,15},{10,... | collective-permute-start | bytes 196616 | tf_op jit(solution)/shard_map/ppermute | solution.py:745
  84.4 1.0 collective-permute-done.19.refs_1_
  85.3 2.9 %collective-permute-start.23 = (bf16[256,128]{1,0:T(8,128)(2,1)S(1)}, bf16[256,128]{1,0:T(8,128)(2,1)S(1)}, u32[]{:S(2)}, u32[]{:S(2)}) collective-permute-start(bf16[256,128]{1,0:T(8,128)(2,1)S(1)} %get-tuple-element.97), channel_id=1, source_target_pairs={{0,10},{1,11},{2,8},{3,9},{4,14},{5,15},{6,12},{7,13},{8,2},{9,3},... | collective-permute-start | bytes 196616 | tf_op jit(solution)/shard_map/ppermute | solution.py:745
  88.2 0.7 collective-permute-start.24
  88.9 3.1 %collective-permute-start.25 = (bf16[256,128]{1,0:T(8,128)(2,1)S(1)}, bf16[256,128]{1,0:T(8,128)(2,1)S(1)}, u32[]{:S(2)}, u32[]{:S(2)}) collective-permute-start(bf16[256,128]{1,0:T(8,128)(2,1)S(1)} %get-tuple-element.99), channel_id=1, source_target_pairs={{0,14},{1,15},{2,12},{3,13},{4,10},{5,11},{6,8},{7,9},{8,6},{9,7},... | collective-permute-start | bytes 196616 | tf_op jit(solution)/shard_map/ppermute | solution.py:745
  92.0 1.6 %collective-permute-done.22.refs_4_ = bf16[256,128]{1,0:T(8,128)(2,1)S(1)} collective-permute-done((bf16[256,128]{1,0:T(8,128)(2,1)S(1)}, bf16[256,128]{1,0:T(8,128)(2,1)S(1)}, u32[]{:S(2)}, u32[]{:S(2)}) %collective-permute-start.22) | collective-permute-done | bytes 65568 | tf_op jit(solution)/shard_map/ppermute | solution.py:745
  93.6 3.5 %collective-permute-done.23.refs_5_ = bf16[256,128]{1,0:T(8,128)(2,1)S(1)} collective-permute-done((bf16[256,128]{1,0:T(8,128)(2,1)S(1)}, bf16[256,128]{1,0:T(8,128)(2,1)S(1)}, u32[]{:S(2)}, u32[]{:S(2)}) %collective-permute-start.23) | collective-permute-done | bytes 65568 | tf_op jit(solution)/shard_map/ppermute | solution.py:745
  97.1 4.1 %tail.1 = (bf16[256,1024]{1,0:T(8,128)(2,1)}, bf16[64,1152]{1,0:T(8,128)(2,1)S(1)}, bf16[64,1152]{1,0:T(8,128)(2,1)S(1)}, bf16[64,1152]{1,0:T(8,128)(2,1)S(1)}, bf16[64,1152]{1,0:T(8,128)(2,1)S(1)}) custom-call(bf16[256,128]{1,0:T(8,128)(2,1)S(1)} %get-tuple-element.92.refs_0_, bf16[256,128]{1,0:T(8,128)(2,1)S(1)} %collective-permute-done.19.refs_1_, ...), custom_call_target="tpu_custom_call" | custom-call | tf_op jit(solution)/shard_map/tail/pallas_call | solution.py:495
  101.2 0.9 collective-permute-start.27
  102.1 1.4 %collective-permute-start.29 = (bf16[64,1152]{1,0:T(8,128)(2,1)S(1)}, bf16[64,1152]{1,0:T(8,128)(2,1)S(1)}, u32[]{:S(2)}, u32[]{:S(2)}) collective-permute-start(bf16[64,1152]{1,0:T(8,128)(2,1)S(1)} %get-tuple-element.107), channel_id=1, source_target_pairs={{0,1},{1,0},{2,3},{3,2},{4,5},{5,4},{6,7},{7,6},{8,9},{9,8},{10,11... | collective-permute-start | bytes 442376 | tf_op jit(solution)/shard_map/ppermute | solution.py:766
  103.4 4.4 %collective-permute-done.27.refs_1_ = bf16[64,1152]{1,0:T(8,128)(2,1)S(1)} collective-permute-done((bf16[64,1152]{1,0:T(8,128)(2,1)S(1)}, bf16[64,1152]{1,0:T(8,128)(2,1)S(1)}, u32[]{:S(2)}, u32[]{:S(2)}) %collective-permute-start.27) | collective-permute-done | bytes 147488 | tf_op jit(solution)/shard_map/ppermute | solution.py:764
  107.8 0.4 collective-permute-done.28.refs_2_
  108.2 1.2 deal.1
  109.4 3.0 %collective-permute-start.30 = (bf16[16,1152]{1,0:T(8,128)(2,1)S(1)}, bf16[16,1152]{1,0:T(8,128)(2,1)S(1)}, u32[]{:S(2)}, u32[]{:S(2)}) collective-permute-start(bf16[16,1152]{1,0:T(8,128)(2,1)S(1)} %get-tuple-element.109), channel_id=1, source_target_pairs={{0,4},{1,5},{2,6},{3,7},{4,0},{5,1},{6,2},{7,3},{8,12},{9,13},{10,... | collective-permute-start | bytes 110600 | tf_op jit(solution)/shard_map/ppermute | solution.py:770
  112.4 0.1 collective-permute-start.31
  112.4 2.4 %collective-permute-start.32 = (bf16[16,1152]{1,0:T(8,128)(2,1)S(1)}, bf16[16,1152]{1,0:T(8,128)(2,1)S(1)}, u32[]{:S(2)}, u32[]{:S(2)}) collective-permute-start(bf16[16,1152]{1,0:T(8,128)(2,1)S(1)} %get-tuple-element.111), channel_id=1, source_target_pairs={{0,12},{1,13},{2,14},{3,15},{4,8},{5,9},{6,10},{7,11},{8,4},{9,5},... | collective-permute-start | bytes 110600 | tf_op jit(solution)/shard_map/ppermute | solution.py:770
  114.8 3.9 %collective-permute-done.31.refs_2_ = bf16[16,1152]{1,0:T(8,128)(2,1)S(1)} collective-permute-done((bf16[16,1152]{1,0:T(8,128)(2,1)S(1)}, bf16[16,1152]{1,0:T(8,128)(2,1)S(1)}, u32[]{:S(2)}, u32[]{:S(2)}) %collective-permute-start.31) | collective-permute-done | bytes 36896 | tf_op jit(solution)/shard_map/ppermute | solution.py:770
  118.7 1.1 join.1
  (35 shorter events, 0.2 us)
Async XLA Ops:
  1.9 23.1 %collective-permute-start = (bf16[288,1024]{1,0:T(8,128)(2,1)S(1)}, bf16[288,1024]{1,0:T(8,128)(2,1)S(1)}, u32[]{:S(2)}, u32[]{:S(2)}) collective-permute-start(bf16[288,1024]{1,0:T(8,128)(2,1)S(1)} %get-tuple-element.57.refs_0_.refs_1_), channel_id=1, source_target_pairs={{0,4},{1,5},{4,8},{5,9},{8,12},{9,13},{12,14},{13,15},{14,10},{15,... | collective-permute-start | bytes 1769480 | tf_op jit(solution)/shard_map/ppermute | solution.py:680
  5.0 20.0 %collective-permute-start.1 = (bf16[288,1024]{1,0:T(8,128)(2,1)S(1)}, bf16[288,1024]{1,0:T(8,128)(2,1)S(1)}, u32[]{:S(2)}, u32[]{:S(2)}) collective-permute-start(bf16[288,1024]{1,0:T(8,128)(2,1)S(1)} %get-tuple-element.57.refs_0_.refs_1_), channel_id=1, source_target_pairs={{0,2},{1,3},{4,0},{5,1},{8,4},{9,5},{12,8},{13,9},{14,12},{15,13},... | collective-permute-start | bytes 1769480 | tf_op jit(solution)/shard_map/ppermute | solution.py:681
  5.0 1.3 %collective-permute-start.2 = (bf16[2,64,384]{2,1,0:T(8,128)(2,1)S(1)}, bf16[2,64,384]{2,1,0:T(8,128)(2,1)S(1)}, u32[]{:S(2)}, u32[]{:S(2)}) collective-permute-start(bf16[2,64,384]{2,1,0:T(8,128)(2,1)S(1)} %get-tuple-element.59), channel_id=1, source_target_pairs={{0,1},{1,0},{2,3},{3,2},{4,5},{5,4},{6,7},{7,6},{8,9},{9,8},{10,11... | collective-permute-start | bytes 294920 | tf_op jit(solution)/shard_map/ppermute | solution.py:625
  6.4 3.8 %collective-permute-start.3 = (bf16[128,384]{1,0:T(8,128)(2,1)S(1)}, bf16[128,384]{1,0:T(8,128)(2,1)S(1)}, u32[]{:S(2)}, u32[]{:S(2)}) collective-permute-start(bf16[128,384]{1,0:T(8,128)(2,1)S(1)} %get-tuple-element.60.own_ref), channel_id=1, source_target_pairs={{1,3},{3,1},{5,7},{7,5},{9,11},{11,9},{13,15},{15,13},{16,20},{17,... | collective-permute-start | bytes 294920 | tf_op jit(solution)/shard_map/ppermute | solution.py:636
  7.0 18.0 %collective-permute-start.4 = (bf16[128,384]{1,0:T(8,128)(2,1)S(1)}, bf16[128,384]{1,0:T(8,128)(2,1)S(1)}, u32[]{:S(2)}, u32[]{:S(2)}) collective-permute-start(bf16[128,384]{1,0:T(8,128)(2,1)S(1)} %get-tuple-element.61), channel_id=1, source_target_pairs={{0,8},{1,11},{2,10},{3,9},{4,12},{5,15},{6,14},{7,13},{8,0},{9,3},... | collective-permute-start | bytes 294920 | tf_op jit(solution)/shard_map/ppermute | solution.py:636
  25.1 6.2 %collective-permute-start.7 = (bf16[2,128,384]{2,1,0:T(8,128)(2,1)S(1)}, bf16[2,128,384]{2,1,0:T(8,128)(2,1)S(1)}, u32[]{:S(2)}, u32[]{:S(2)}) collective-permute-start(bf16[2,128,384]{2,1,0:T(8,128)(2,1)S(1)} %keep.1.refs_0_.own_ref), channel_id=1, source_target_pairs={{0,16},{16,0},{1,17},{17,1},{2,18},{18,2},{3,19},{19,3},{4,20},{20... | collective-permute-start | bytes 589832 | tf_op jit(solution)/shard_map/ppermute | solution.py:686
  27.6 13.3 %collective-permute-start.5 = (bf16[288,1024]{1,0:T(8,128)(2,1)S(1)}, bf16[288,1024]{1,0:T(8,128)(2,1)S(1)}, u32[]{:S(2)}, u32[]{:S(2)}) collective-permute-start(bf16[288,1024]{1,0:T(8,128)(2,1)S(1)} %collective-permute-done.refs_2_.refs_3_), channel_id=1, source_target_pairs={{0,4},{1,5},{4,8},{5,9},{8,12},{9,13},{12,14},{13,15},{14,10},{15,... | collective-permute-start | bytes 1769480 | tf_op jit(solution)/shard_map/ppermute | solution.py:680
  27.6 13.5 %collective-permute-start.6 = (bf16[288,1024]{1,0:T(8,128)(2,1)S(1)}, bf16[288,1024]{1,0:T(8,128)(2,1)S(1)}, u32[]{:S(2)}, u32[]{:S(2)}) collective-permute-start(bf16[288,1024]{1,0:T(8,128)(2,1)S(1)} %collective-permute-done.1.refs_4_.refs_5_), channel_id=1, source_target_pairs={{0,2},{1,3},{4,0},{5,1},{8,4},{9,5},{12,8},{13,9},{14,12},{15,13},... | collective-permute-start | bytes 1769480 | tf_op jit(solution)/shard_map/ppermute | solution.py:681
  31.3 1.8 %collective-permute-start.8 = (bf16[4,128,384]{2,1,0:T(8,128)(2,1)S(1)}, bf16[4,128,384]{2,1,0:T(8,128)(2,1)S(1)}, u32[]{:S(2)}, u32[]{:S(2)}) collective-permute-start(bf16[4,128,384]{2,1,0:T(8,128)(2,1)S(1)} %gather_blocks.1), channel_id=1, source_target_pairs={{0,1},{1,0},{2,3},{3,2},{4,5},{5,4},{6,7},{7,6},{8,9},{9,8},{10,11... | collective-permute-start | bytes 1179656 | tf_op jit(solution)/shard_map/ppermute | solution.py:690
  33.3 17.1 %copy-start.4 = (f32[1024]{0:T(1024)S(1)}, f32[1024]{0:T(1024)}, u32[]{:S(2)}) copy-start(f32[1024]{0:T(1024)} %param.11) | copy-start | bytes 12292
  41.1 12.7 %collective-permute-start.10 = (bf16[288,1024]{1,0:T(8,128)(2,1)S(1)}, bf16[288,1024]{1,0:T(8,128)(2,1)S(1)}, u32[]{:S(2)}, u32[]{:S(2)}) collective-permute-start(bf16[288,1024]{1,0:T(8,128)(2,1)S(1)} %collective-permute-done.6.refs_8_.refs_9_), channel_id=1, source_target_pairs={{0,2},{1,3},{4,0},{5,1},{8,4},{9,5},{12,8},{13,9},{14,12},{15,13},... | collective-permute-start | bytes 1769480 | tf_op jit(solution)/shard_map/ppermute | solution.py:700
  42.7 13.4 %collective-permute-start.9 = (bf16[288,1024]{1,0:T(8,128)(2,1)S(1)}, bf16[288,1024]{1,0:T(8,128)(2,1)S(1)}, u32[]{:S(2)}, u32[]{:S(2)}) collective-permute-start(bf16[288,1024]{1,0:T(8,128)(2,1)S(1)} %collective-permute-done.5.refs_6_.refs_7_), channel_id=1, source_target_pairs={{0,4},{1,5},{4,8},{5,9},{8,12},{9,13},{12,14},{13,15},{14,10},{15,... | collective-permute-start | bytes 1769480 | tf_op jit(solution)/shard_map/ppermute | solution.py:699
  43.2 7.1 %collective-permute-start.11 = (bf16[5,32,1024]{2,1,0:T(8,128)(2,1)S(1)}, bf16[5,32,1024]{2,1,0:T(8,128)(2,1)S(1)}, u32[]{:S(2)}, u32[]{:S(2)}) collective-permute-start(bf16[5,32,1024]{2,1,0:T(8,128)(2,1)S(1)} %collect.3.refs_0_), channel_id=1, source_target_pairs={{0,16},{16,0},{1,17},{17,1},{2,18},{18,2},{3,19},{19,3},{4,20},{20... | collective-permute-start | bytes 983048 | tf_op jit(solution)/shard_map/ppermute | solution.py:696
  56.1 9.2 %collective-permute-start.13 = (bf16[144,1024]{1,0:T(8,128)(2,1)S(1)}, bf16[144,1024]{1,0:T(8,128)(2,1)S(1)}, u32[]{:S(2)}, u32[]{:S(2)}) collective-permute-start(bf16[144,1024]{1,0:T(8,128)(2,1)S(1)} %slice.6), channel_id=1, source_target_pairs={{0,4},{1,5},{4,8},{5,9},{8,12},{9,13},{12,14},{13,15},{14,10},{15,... | collective-permute-start | bytes 884744 | tf_op jit(solution)/shard_map/ppermute | solution.py:704
  56.5 8.8 %collective-permute-start.14 = (bf16[144,1024]{1,0:T(8,128)(2,1)S(1)}, bf16[144,1024]{1,0:T(8,128)(2,1)S(1)}, u32[]{:S(2)}, u32[]{:S(2)}) collective-permute-start(bf16[144,1024]{1,0:T(8,128)(2,1)S(1)} %slice.7), channel_id=1, source_target_pairs={{0,2},{1,3},{4,0},{5,1},{8,4},{9,5},{12,8},{13,9},{14,12},{15,13},... | collective-permute-start | bytes 884744 | tf_op jit(solution)/shard_map/ppermute | solution.py:705
  58.3 5.0 %collective-permute-start.12 = (bf16[2,32,1024]{2,1,0:T(8,128)(2,1)S(1)}, bf16[2,32,1024]{2,1,0:T(8,128)(2,1)S(1)}, u32[]{:S(2)}, u32[]{:S(2)}) collective-permute-start(bf16[2,32,1024]{2,1,0:T(8,128)(2,1)S(1)} %collect.4.refs_2_), channel_id=1, source_target_pairs={{0,16},{16,0},{1,17},{17,1},{2,18},{18,2},{3,19},{19,3},{4,20},{20... | collective-permute-start | bytes 393224 | tf_op jit(solution)/shard_map/ppermute | solution.py:709
  63.3 2.0 %copy-start.2 = (bf16[2,32,1024]{2,1,0:T(8,128)(2,1)}, bf16[2,32,1024]{2,1,0:T(8,128)(2,1)S(1)}, u32[]{:S(2)}) copy-start(bf16[2,32,1024]{2,1,0:T(8,128)(2,1)S(1)} %collective-permute-done.12.refs_3_) | copy-start | bytes 393220
  65.3 3.7 %collective-permute-start.15 = (bf16[10,2,128,128]{3,2,1,0:T(8,128)(2,1)}, bf16[10,2,128,128]{3,2,1,0:T(8,128)(2,1)}, u32[]{:S(2)}, u32[]{:S(2)}) collective-permute-start(bf16[10,2,128,128]{3,2,1,0:T(8,128)(2,1)} %get-tuple-element.87), channel_id=1, source_target_pairs={{0,1},{1,0},{2,3},{3,2},{4,5},{5,4},{6,7},{7,6},{8,9},{9,8},{10,11... | collective-permute-start | bytes 1966088 | tf_op jit(solution)/shard_map/ppermute | solution.py:676
  65.4 3.6 %collective-permute-start.16 = (bf16[4,2,128,128]{3,2,1,0:T(8,128)(2,1)}, bf16[4,2,128,128]{3,2,1,0:T(8,128)(2,1)}, u32[]{:S(2)}, u32[]{:S(2)}) collective-permute-start(bf16[4,2,128,128]{3,2,1,0:T(8,128)(2,1)} %get-tuple-element.88), channel_id=1, source_target_pairs={{0,1},{1,0},{2,3},{3,2},{4,5},{5,4},{6,7},{7,6},{8,9},{9,8},{10,11... | collective-permute-start | bytes 786440 | tf_op jit(solution)/shard_map/ppermute | solution.py:676
  67.3 1.7 %collective-permute-start.17 = (bf16[2,2,128,128]{3,2,1,0:T(8,128)(2,1)}, bf16[2,2,128,128]{3,2,1,0:T(8,128)(2,1)}, u32[]{:S(2)}, u32[]{:S(2)}) collective-permute-start(bf16[2,2,128,128]{3,2,1,0:T(8,128)(2,1)} %get-tuple-element.89), channel_id=1, source_target_pairs={{0,1},{1,0},{2,3},{3,2},{4,5},{5,4},{6,7},{7,6},{8,9},{9,8},{10,11... | collective-permute-start | bytes 393224 | tf_op jit(solution)/shard_map/ppermute | solution.py:676
  67.4 13.2 %collective-permute-start.18 = (bf16[1,32,1024]{2,1,0:T(8,128)(2,1)S(1)}, bf16[1,32,1024]{2,1,0:T(8,128)(2,1)S(1)}, u32[]{:S(2)}, u32[]{:S(2)}) collective-permute-start(bf16[1,32,1024]{2,1,0:T(8,128)(2,1)S(1)} %collect.5.refs_4_), channel_id=1, source_target_pairs={{0,16},{16,0},{1,17},{17,1},{2,18},{18,2},{3,19},{19,3},{4,20},{20... | collective-permute-start | bytes 196616 | tf_op jit(solution)/shard_map/ppermute | solution.py:723
  68.5 12.1 %copy-start.3 = (bf16[2,32,1024]{2,1,0:T(8,128)(2,1)S(1)}, bf16[2,32,1024]{2,1,0:T(8,128)(2,1)}, u32[]{:S(2)}) copy-start(bf16[2,32,1024]{2,1,0:T(8,128)(2,1)} %copy-done.2) | copy-start | bytes 393220
  69.0 0.7 copy-start.6
  69.7 27.4 %copy-start = (bf16[256,1024]{1,0:T(8,128)(2,1)S(1)}, bf16[256,1024]{1,0:T(8,128)(2,1)}, u32[]{:S(2)}) copy-start(bf16[256,1024]{1,0:T(8,128)(2,1)} %refs_8_.1) | copy-start | bytes 1572868
  69.7 27.4 %copy-start.1 = (bf16[256,1024]{1,0:T(8,128)(2,1)S(1)}, bf16[256,1024]{1,0:T(8,128)(2,1)}, u32[]{:S(2)}) copy-start(bf16[256,1024]{1,0:T(8,128)(2,1)} %refs_10_.1) | copy-start | bytes 1572868
  69.7 27.4 %copy-start.5 = (f32[1024]{0:T(1024)S(1)}, f32[1024]{0:T(1024)}, u32[]{:S(2)}) copy-start(f32[1024]{0:T(1024)} %param.16) | copy-start | bytes 12292
  80.7 16.4 %collective-permute-start.26 = (bf16[8,2,32,1024]{3,2,1,0:T(8,128)(2,1)S(1)}, bf16[8,2,32,1024]{3,2,1,0:T(8,128)(2,1)S(1)}, u32[]{:S(2)}, u32[]{:S(2)}) collective-permute-start(bf16[8,2,32,1024]{3,2,1,0:T(8,128)(2,1)S(1)} %pair_rows.1), channel_id=1, source_target_pairs={{0,1},{1,0},{2,3},{3,2},{4,5},{5,4},{6,7},{7,6},{8,9},{9,8},{10,11... | collective-permute-start | bytes 3145736 | tf_op jit(solution)/shard_map/ppermute | solution.py:743
  80.8 4.5 %collective-permute-start.19 = (bf16[256,128]{1,0:T(8,128)(2,1)S(1)}, bf16[256,128]{1,0:T(8,128)(2,1)S(1)}, u32[]{:S(2)}, u32[]{:S(2)}) collective-permute-start(bf16[256,128]{1,0:T(8,128)(2,1)S(1)} %get-tuple-element.93), channel_id=1, source_target_pairs={{0,2},{1,3},{2,0},{3,1},{4,6},{5,7},{6,4},{7,5},{8,10},{9,11},{10,... | collective-permute-start | bytes 196616 | tf_op jit(solution)/shard_map/ppermute | solution.py:745
  82.4 5.9 %collective-permute-start.20 = (bf16[256,128]{1,0:T(8,128)(2,1)S(1)}, bf16[256,128]{1,0:T(8,128)(2,1)S(1)}, u32[]{:S(2)}, u32[]{:S(2)}) collective-permute-start(bf16[256,128]{1,0:T(8,128)(2,1)S(1)} %get-tuple-element.94), channel_id=1, source_target_pairs={{0,4},{1,5},{2,6},{3,7},{4,0},{5,1},{6,2},{7,3},{8,12},{9,13},{10,... | collective-permute-start | bytes 196616 | tf_op jit(solution)/shard_map/ppermute | solution.py:745
  82.6 6.2 %collective-permute-start.21 = (bf16[256,128]{1,0:T(8,128)(2,1)S(1)}, bf16[256,128]{1,0:T(8,128)(2,1)S(1)}, u32[]{:S(2)}, u32[]{:S(2)}) collective-permute-start(bf16[256,128]{1,0:T(8,128)(2,1)S(1)} %get-tuple-element.95), channel_id=1, source_target_pairs={{0,6},{1,7},{2,4},{3,5},{4,2},{5,3},{6,0},{7,1},{8,14},{9,15},{10,... | collective-permute-start | bytes 196616 | tf_op jit(solution)/shard_map/ppermute | solution.py:745
  84.4 9.2 %collective-permute-start.22 = (bf16[256,128]{1,0:T(8,128)(2,1)S(1)}, bf16[256,128]{1,0:T(8,128)(2,1)S(1)}, u32[]{:S(2)}, u32[]{:S(2)}) collective-permute-start(bf16[256,128]{1,0:T(8,128)(2,1)S(1)} %get-tuple-element.96), channel_id=1, source_target_pairs={{0,8},{1,9},{2,10},{3,11},{4,12},{5,13},{6,14},{7,15},{8,0},{9,1},... | collective-permute-start | bytes 196616 | tf_op jit(solution)/shard_map/ppermute | solution.py:745
  85.3 11.8 %collective-permute-start.23 = (bf16[256,128]{1,0:T(8,128)(2,1)S(1)}, bf16[256,128]{1,0:T(8,128)(2,1)S(1)}, u32[]{:S(2)}, u32[]{:S(2)}) collective-permute-start(bf16[256,128]{1,0:T(8,128)(2,1)S(1)} %get-tuple-element.97), channel_id=1, source_target_pairs={{0,10},{1,11},{2,8},{3,9},{4,14},{5,15},{6,12},{7,13},{8,2},{9,3},... | collective-permute-start | bytes 196616 | tf_op jit(solution)/shard_map/ppermute | solution.py:745
  88.2 8.9 %collective-permute-start.24 = (bf16[256,128]{1,0:T(8,128)(2,1)S(1)}, bf16[256,128]{1,0:T(8,128)(2,1)S(1)}, u32[]{:S(2)}, u32[]{:S(2)}) collective-permute-start(bf16[256,128]{1,0:T(8,128)(2,1)S(1)} %get-tuple-element.98), channel_id=1, source_target_pairs={{0,12},{1,13},{2,14},{3,15},{4,8},{5,9},{6,10},{7,11},{8,4},{9,5},... | collective-permute-start | bytes 196616 | tf_op jit(solution)/shard_map/ppermute | solution.py:745
  88.9 8.2 %collective-permute-start.25 = (bf16[256,128]{1,0:T(8,128)(2,1)S(1)}, bf16[256,128]{1,0:T(8,128)(2,1)S(1)}, u32[]{:S(2)}, u32[]{:S(2)}) collective-permute-start(bf16[256,128]{1,0:T(8,128)(2,1)S(1)} %get-tuple-element.99), channel_id=1, source_target_pairs={{0,14},{1,15},{2,12},{3,13},{4,10},{5,11},{6,8},{7,9},{8,6},{9,7},... | collective-permute-start | bytes 196616 | tf_op jit(solution)/shard_map/ppermute | solution.py:745
  101.2 6.6 %collective-permute-start.27 = (bf16[64,1152]{1,0:T(8,128)(2,1)S(1)}, bf16[64,1152]{1,0:T(8,128)(2,1)S(1)}, u32[]{:S(2)}, u32[]{:S(2)}) collective-permute-start(bf16[64,1152]{1,0:T(8,128)(2,1)S(1)} %get-tuple-element.105), channel_id=1, source_target_pairs={{0,2},{1,3},{2,0},{3,1},{4,6},{5,7},{6,4},{7,5},{8,10},{9,11},{10,... | collective-permute-start | bytes 442376 | tf_op jit(solution)/shard_map/ppermute | solution.py:764
  102.1 6.1 %collective-permute-start.28 = (bf16[64,1152]{1,0:T(8,128)(2,1)S(1)}, bf16[64,1152]{1,0:T(8,128)(2,1)S(1)}, u32[]{:S(2)}, u32[]{:S(2)}) collective-permute-start(bf16[64,1152]{1,0:T(8,128)(2,1)S(1)} %get-tuple-element.106), channel_id=1, source_target_pairs={{0,3},{1,2},{2,1},{3,0},{4,7},{5,6},{6,5},{7,4},{8,11},{9,10},{10,... | collective-permute-start | bytes 442376 | tf_op jit(solution)/shard_map/ppermute | solution.py:765
  102.1 6.1 %collective-permute-start.29 = (bf16[64,1152]{1,0:T(8,128)(2,1)S(1)}, bf16[64,1152]{1,0:T(8,128)(2,1)S(1)}, u32[]{:S(2)}, u32[]{:S(2)}) collective-permute-start(bf16[64,1152]{1,0:T(8,128)(2,1)S(1)} %get-tuple-element.107), channel_id=1, source_target_pairs={{0,1},{1,0},{2,3},{3,2},{4,5},{5,4},{6,7},{7,6},{8,9},{9,8},{10,11... | collective-permute-start | bytes 442376 | tf_op jit(solution)/shard_map/ppermute | solution.py:766
  109.4 5.5 %collective-permute-start.30 = (bf16[16,1152]{1,0:T(8,128)(2,1)S(1)}, bf16[16,1152]{1,0:T(8,128)(2,1)S(1)}, u32[]{:S(2)}, u32[]{:S(2)}) collective-permute-start(bf16[16,1152]{1,0:T(8,128)(2,1)S(1)} %get-tuple-element.109), channel_id=1, source_target_pairs={{0,4},{1,5},{2,6},{3,7},{4,0},{5,1},{6,2},{7,3},{8,12},{9,13},{10,... | collective-permute-start | bytes 110600 | tf_op jit(solution)/shard_map/ppermute | solution.py:770
  112.4 6.3 %collective-permute-start.31 = (bf16[16,1152]{1,0:T(8,128)(2,1)S(1)}, bf16[16,1152]{1,0:T(8,128)(2,1)S(1)}, u32[]{:S(2)}, u32[]{:S(2)}) collective-permute-start(bf16[16,1152]{1,0:T(8,128)(2,1)S(1)} %get-tuple-element.110), channel_id=1, source_target_pairs={{0,8},{1,9},{2,10},{3,11},{4,12},{5,13},{6,14},{7,15},{8,0},{9,1},... | collective-permute-start | bytes 110600 | tf_op jit(solution)/shard_map/ppermute | solution.py:770
  112.4 6.3 %collective-permute-start.32 = (bf16[16,1152]{1,0:T(8,128)(2,1)S(1)}, bf16[16,1152]{1,0:T(8,128)(2,1)S(1)}, u32[]{:S(2)}, u32[]{:S(2)}) collective-permute-start(bf16[16,1152]{1,0:T(8,128)(2,1)S(1)} %get-tuple-element.111), channel_id=1, source_target_pairs={{0,12},{1,13},{2,14},{3,15},{4,8},{5,9},{6,10},{7,11},{8,4},{9,5},... | collective-permute-start | bytes 110600 | tf_op jit(solution)/shard_map/ppermute | solution.py:770

commit v5 on v4

--- a/solution.py
+++ b/solution.py
@@ -353,7 +353,7 @@
     def attend_block(index, used):
         row, block = place_of(index)
         count = counts_ref[block]
-        picked = [lists_ref[block, s] for s in range(used)]
+        picked = [lists_ref[s, block] for s in range(used)]
         stacked = head_masked(q_all[row], heads)
         scores = []
         for s, p in enumerate(picked):
@@ -723,7 +723,7 @@
         late_twin = lax.ppermute(late, "scan", twins)
     q_all, kv_all = state
     attended = attend(
-        key_blocks,
+        key_blocks.T,
         key_counts,
         q_all,
         kv_all,

time: 120 us -> 117 us (0.975)
  Pallas kernels: 25.8 us -> 22.7 us
  local copies, waits for them, and re-layouts: 1.48 us -> 0.07 us
    ppermute x3, waiting for transfers between devices: 0.22 us -> 2.85 us  [per_device(): backward = lax.ppermute(backward, 'seq', around(-1))]
    pallas_call x3, Pallas kernels: 6.9 us -> 4.79 us  [project(): pl.pallas_call(functools.partial(project_kernel, chips, starts, width, sh...]
    ppermute x3, starting transfers between devices: 3.56 us -> 5.47 us  [per_device(): backward = lax.ppermute(backward, 'seq', around(-1))]
    unnamed x15 -> x12, local copies, waits for them, and re-layouts: 1.44 us -> 0.03 us
    ppermute x2, waiting for transfers between devices: 14.9 us -> 13.6 us  [per_device(): lax.ppermute(sent[j], ('scan', 'seq'), serve(4 * j))]
  transfers between devices with their start and end apart: 33 -> 33, of which waited for: 16 -> 18; matrix products, arithmetic and copies ran while one was open for 1% -> 0% of each run, Pallas kernels for 15% -> 13%
where the time goes in v5:
time: 117 us
  waiting for transfers between devices  57.4 us (49%)
  starting transfers between devices  36.2 us (31%)
  Pallas kernels  22.7 us (19%)
    ppermute x2, waiting for transfers between devices, per_device(): lax.ppermute(sent[j], ('scan', 'seq'), serve(4 * j))  13.6 us
    ppermute x7, starting transfers between devices, per_device(): lax.ppermute(attended[k], 'seq', across(k))  10.1 us
    pallas_call x1, Pallas kernels, attend(): pl.pallas_call(functools.partial(attend_kernel, chips, group, heads, step...  9.84 us
    ppermute x3, waiting for transfers between devices, per_device(): forward = lax.ppermute(forward, 'seq', around(1))  8.82 us
    ppermute x1, waiting for transfers between devices, per_device(): early_twin = lax.ppermute(early, 'scan', twins)  7.72 us
    ppermute x3, starting transfers between devices, per_device(): lax.ppermute(lines[k], 'seq', across(2 * k))  5.83 us
    ppermute x3, starting transfers between devices, per_device(): backward = lax.ppermute(backward, 'seq', around(-1))  5.47 us
    ppermute x7, waiting for transfers between devices, per_device(): lax.ppermute(attended[k], 'seq', across(k))  5.34 us
  transfers between devices with their start and end apart: 33, of which 18 were waited for; matrix products, arithmetic and copies ran while one was open for 0% of the time, Pallas kernels for 13%

profile of v5, /device:TPU:0, one launch (start us, length us, event | category | flops | bytes accessed | tf_op | source)
XLA Modules:
  0.0 117.2 jit_solution(17470766665167955511)
XLA Ops:
  0.6 1.3 %prepare.1 = (bf16[288,1024]{1,0:T(8,128)(2,1)S(1)}, bf16[2,64,384]{2,1,0:T(8,128)(2,1)S(1)}, bf16[2,64,384]{2,1,0:T(8,128)(2,1)S(1)}) custom-call(bf16[256,1024]{1,0:T(8,128)(2,1)} %refs_8_.1, bf16[64,1024]{1,0:T(8,128)(2,1)} %query_ref.1, bf16[64,1024]{1,0:T(8,128)(2,1)} %key_ref.1, bf16[64,1024]{1,0:T(8,128)(2,1)} %value_ref.1, bf16[64,1024]{1,0:T(8,128)(2,1)} %out_ref.1), custom_call_target="tpu_custom_call" | custom-call | tf_op jit(solution)/shard_map/prepare/pallas_call | solution.py:111
  1.9 3.0 %collective-permute-start.1 = (bf16[288,1024]{1,0:T(8,128)(2,1)S(1)}, bf16[288,1024]{1,0:T(8,128)(2,1)S(1)}, u32[]{:S(2)}, u32[]{:S(2)}) collective-permute-start(bf16[288,1024]{1,0:T(8,128)(2,1)S(1)} %get-tuple-element.57.refs_0_.refs_1_), channel_id=1, source_target_pairs={{0,2},{1,3},{4,0},{5,1},{8,4},{9,5},{12,8},{13,9},{14,12},{15,13},... | collective-permute-start | bytes 1769480 | tf_op jit(solution)/shard_map/ppermute | solution.py:681
  5.0 0.1 collective-permute-start
  5.1 0.0 collective-permute-start.2
  5.1 1.3 %collective-permute-done.2.got_ref = bf16[2,64,384]{2,1,0:T(8,128)(2,1)S(1)} collective-permute-done((bf16[2,64,384]{2,1,0:T(8,128)(2,1)S(1)}, bf16[2,64,384]{2,1,0:T(8,128)(2,1)S(1)}, u32[]{:S(2)}, u32[]{:S(2)}) %collective-permute-start.2) | collective-permute-done | bytes 98336 | tf_op jit(solution)/shard_map/ppermute | solution.py:625
  6.4 3.0 %collective-permute-start.4 = (bf16[128,384]{1,0:T(8,128)(2,1)S(1)}, bf16[128,384]{1,0:T(8,128)(2,1)S(1)}, u32[]{:S(2)}, u32[]{:S(2)}) collective-permute-start(bf16[128,384]{1,0:T(8,128)(2,1)S(1)} %get-tuple-element.61), channel_id=1, source_target_pairs={{0,8},{1,11},{2,10},{3,9},{4,12},{5,15},{6,14},{7,13},{8,0},{9,3},... | collective-permute-start | bytes 294920 | tf_op jit(solution)/shard_map/ppermute | solution.py:636
  9.4 0.7 collective-permute-start.3
  10.1 13.6 %collective-permute-done.4.far_ref = bf16[128,384]{1,0:T(8,128)(2,1)S(1)} collective-permute-done((bf16[128,384]{1,0:T(8,128)(2,1)S(1)}, bf16[128,384]{1,0:T(8,128)(2,1)S(1)}, u32[]{:S(2)}, u32[]{:S(2)}) %collective-permute-start.4) | collective-permute-done | bytes 98336 | tf_op jit(solution)/shard_map/ppermute | solution.py:636
  23.8 1.6 %collective-permute-start.7 = (bf16[2,128,384]{2,1,0:T(8,128)(2,1)S(1)}, bf16[2,128,384]{2,1,0:T(8,128)(2,1)S(1)}, u32[]{:S(2)}, u32[]{:S(2)}) collective-permute-start(bf16[2,128,384]{2,1,0:T(8,128)(2,1)S(1)} %keep.1.refs_0_.own_ref), channel_id=1, source_target_pairs={{0,16},{16,0},{1,17},{17,1},{2,18},{18,2},{3,19},{19,3},{4,20},{20... | collective-permute-start | bytes 589832 | tf_op jit(solution)/shard_map/ppermute | solution.py:686
  25.3 0.7 collective-permute-start.5
  26.1 2.2 %collective-permute-start.6 = (bf16[288,1024]{1,0:T(8,128)(2,1)S(1)}, bf16[288,1024]{1,0:T(8,128)(2,1)S(1)}, u32[]{:S(2)}, u32[]{:S(2)}) collective-permute-start(bf16[288,1024]{1,0:T(8,128)(2,1)S(1)} %collective-permute-done.1.refs_4_.refs_5_), channel_id=1, source_target_pairs={{0,2},{1,3},{4,0},{5,1},{8,4},{9,5},{12,8},{13,9},{14,12},{15,13},... | collective-permute-start | bytes 1769480 | tf_op jit(solution)/shard_map/ppermute | solution.py:681
  28.2 2.0 %collective-permute-done.7.refs_1_.twin_ref = bf16[2,128,384]{2,1,0:T(8,128)(2,1)S(1)} collective-permute-done((bf16[2,128,384]{2,1,0:T(8,128)(2,1)S(1)}, bf16[2,128,384]{2,1,0:T(8,128)(2,1)S(1)}, u32[]{:S(2)}, u32[]{:S(2)}) %collective-permute-start.7) | collective-permute-done | bytes 196640 | tf_op jit(solution)/shard_map/ppermute | solution.py:686
  30.2 0.1 collective-permute-start.8
  30.3 1.7 %collective-permute-done.8.other_ref = bf16[4,128,384]{2,1,0:T(8,128)(2,1)S(1)} collective-permute-done((bf16[4,128,384]{2,1,0:T(8,128)(2,1)S(1)}, bf16[4,128,384]{2,1,0:T(8,128)(2,1)S(1)}, u32[]{:S(2)}, u32[]{:S(2)}) %collective-permute-start.8) | collective-permute-done | bytes 393248 | tf_op jit(solution)/shard_map/ppermute | solution.py:690
  32.0 0.2 assemble.1.refs_11_.refs_5_.refs_3_
  32.2 0.0 copy-start.2
  32.2 7.6 %collective-permute-done.5.refs_6_.refs_7_ = bf16[288,1024]{1,0:T(8,128)(2,1)S(1)} collective-permute-done((bf16[288,1024]{1,0:T(8,128)(2,1)S(1)}, bf16[288,1024]{1,0:T(8,128)(2,1)S(1)}, u32[]{:S(2)}, u32[]{:S(2)}) %collective-permute-start.5) | collective-permute-done | bytes 589856 | tf_op jit(solution)/shard_map/ppermute | solution.py:680
  39.8 1.2 %collective-permute-done.6.refs_8_.refs_9_ = bf16[288,1024]{1,0:T(8,128)(2,1)S(1)} collective-permute-done((bf16[288,1024]{1,0:T(8,128)(2,1)S(1)}, bf16[288,1024]{1,0:T(8,128)(2,1)S(1)}, u32[]{:S(2)}, u32[]{:S(2)}) %collective-permute-start.6) | collective-permute-done | bytes 589856 | tf_op jit(solution)/shard_map/ppermute | solution.py:681
  41.0 1.7 %collective-permute-start.9 = (bf16[288,1024]{1,0:T(8,128)(2,1)S(1)}, bf16[288,1024]{1,0:T(8,128)(2,1)S(1)}, u32[]{:S(2)}, u32[]{:S(2)}) collective-permute-start(bf16[288,1024]{1,0:T(8,128)(2,1)S(1)} %collective-permute-done.5.refs_6_.refs_7_), channel_id=1, source_target_pairs={{0,4},{1,5},{4,8},{5,9},{8,12},{9,13},{12,14},{13,15},{14,10},{15,... | collective-permute-start | bytes 1769480 | tf_op jit(solution)/shard_map/ppermute | solution.py:699
  42.8 0.3 collective-permute-start.10
  43.1 0.4 collective-permute-start.11
  43.5 7.7 %collective-permute-done.11.refs_1_ = bf16[5,32,1024]{2,1,0:T(8,128)(2,1)S(1)} collective-permute-done((bf16[5,32,1024]{2,1,0:T(8,128)(2,1)S(1)}, bf16[5,32,1024]{2,1,0:T(8,128)(2,1)S(1)}, u32[]{:S(2)}, u32[]{:S(2)}) %collective-permute-start.11) | collective-permute-done | bytes 327712 | tf_op jit(solution)/shard_map/ppermute | solution.py:696
  51.2 2.7 %project.3 = (bf16[16,128,128]{2,1,0:T(8,128)(2,1)S(1)}, bf16[32,2,128,128]{3,2,1,0:T(8,128)(2,1)S(1)}, bf16[10,2,128,128]{3,2,1,0:T(8,128)(2,1)S(1)}) custom-call(bf16[288,1024]{1,0:T(8,128)(2,1)S(1)} %get-tuple-element.57.refs_0_.refs_1_, bf16[288,1024]{1,0:T(8,128)(2,1)S(1)} %get-tuple-element.57.refs_0_.refs_1_, ...), custom_call_target="tpu_custom_call" | custom-call | tf_op jit(solution)/shard_map/project/pallas_call | solution.py:319
  53.9 1.2 %collective-permute-done.9.refs_0_.refs_1_ = bf16[288,1024]{1,0:T(8,128)(2,1)S(1)} collective-permute-done((bf16[288,1024]{1,0:T(8,128)(2,1)S(1)}, bf16[288,1024]{1,0:T(8,128)(2,1)S(1)}, u32[]{:S(2)}, u32[]{:S(2)}) %collective-permute-start.9) | collective-permute-done | bytes 589856 | tf_op jit(solution)/shard_map/ppermute | solution.py:699
  55.1 1.6 %collective-permute-done.10.refs_2_.refs_3_ = bf16[288,1024]{1,0:T(8,128)(2,1)S(1)} collective-permute-done((bf16[288,1024]{1,0:T(8,128)(2,1)S(1)}, bf16[288,1024]{1,0:T(8,128)(2,1)S(1)}, u32[]{:S(2)}, u32[]{:S(2)}) %collective-permute-start.10) | collective-permute-done | bytes 589856 | tf_op jit(solution)/shard_map/ppermute | solution.py:700
  56.8 0.7 collective-permute-start.13
  57.4 1.4 %collective-permute-start.14 = (bf16[144,1024]{1,0:T(8,128)(2,1)S(1)}, bf16[144,1024]{1,0:T(8,128)(2,1)S(1)}, u32[]{:S(2)}, u32[]{:S(2)}) collective-permute-start(bf16[144,1024]{1,0:T(8,128)(2,1)S(1)} %slice.7), channel_id=1, source_target_pairs={{0,2},{1,3},{4,0},{5,1},{8,4},{9,5},{12,8},{13,9},{14,12},{15,13},... | collective-permute-start | bytes 884744 | tf_op jit(solution)/shard_map/ppermute | solution.py:705
  58.9 0.7 collective-permute-start.12
  59.6 4.3 %collective-permute-done.12.refs_3_ = bf16[2,32,1024]{2,1,0:T(8,128)(2,1)S(1)} collective-permute-done((bf16[2,32,1024]{2,1,0:T(8,128)(2,1)S(1)}, bf16[2,32,1024]{2,1,0:T(8,128)(2,1)S(1)}, u32[]{:S(2)}, u32[]{:S(2)}) %collective-permute-start.12) | collective-permute-done | bytes 131104 | tf_op jit(solution)/shard_map/ppermute | solution.py:709
  63.9 1.3 %project.4 = (bf16[16,128,128]{2,1,0:T(8,128)(2,1)S(1)}, bf16[32,2,128,128]{3,2,1,0:T(8,128)(2,1)S(1)}, bf16[4,2,128,128]{3,2,1,0:T(8,128)(2,1)S(1)}) custom-call(bf16[288,1024]{1,0:T(8,128)(2,1)S(1)} %collective-permute-done.9.refs_0_.refs_1_, ...), custom_call_target="tpu_custom_call", output_to_operand_aliasing={{0}: (6, {}), {1}: (7, {})} | custom-call | tf_op jit(solution)/shard_map/project/pallas_call | solution.py:319
  65.2 0.1 collective-permute-start.15
  65.3 0.5 collective-permute-start.16
  65.8 0.8 project.5
  66.6 0.1 collective-permute-start.17
  66.8 0.7 collective-permute-start.18
  67.4 0.6 collective-permute-done.17.refs_3_
  68.1 0.0 copy-start
  68.1 0.0 copy-start.1
  68.1 0.0 copy-start.4
  68.1 9.8 %attend.1 = (bf16[32,2,128,128]{3,2,1,0:T(8,128)(2,1)S(1)}, bf16[256,128]{1,0:T(8,128)(2,1)S(1)}, bf16[256,128]{1,0:T(8,128)(2,1)S(1)}, bf16[256,128]{1,0:T(8,12...) custom-call(s32[8,32]{1,0:T(8,128)S(1)} %bitcast.10, ...), custom_call_target="tpu_custom_call", output_to_operand_aliasing={{0}: (3, {})} | custom-call | tf_op jit(solution)/shard_map/attend/pallas_call | solution.py:405
  78.0 0.1 pair_rows.1
  78.1 0.1 collective-permute-start.26
  78.2 0.4 collective-permute-start.19
  78.5 0.4 collective-permute-start.20
  78.9 2.8 %collective-permute-start.21 = (bf16[256,128]{1,0:T(8,128)(2,1)S(1)}, bf16[256,128]{1,0:T(8,128)(2,1)S(1)}, u32[]{:S(2)}, u32[]{:S(2)}) collective-permute-start(bf16[256,128]{1,0:T(8,128)(2,1)S(1)} %get-tuple-element.95), channel_id=1, source_target_pairs={{0,6},{1,7},{2,4},{3,5},{4,2},{5,3},{6,0},{7,1},{8,14},{9,15},{10,... | collective-permute-start | bytes 196616 | tf_op jit(solution)/shard_map/ppermute | solution.py:745
  81.7 0.3 collective-permute-start.22
  82.0 0.6 collective-permute-done.19.refs_1_
  82.7 1.7 %collective-permute-start.23 = (bf16[256,128]{1,0:T(8,128)(2,1)S(1)}, bf16[256,128]{1,0:T(8,128)(2,1)S(1)}, u32[]{:S(2)}, u32[]{:S(2)}) collective-permute-start(bf16[256,128]{1,0:T(8,128)(2,1)S(1)} %get-tuple-element.97), channel_id=1, source_target_pairs={{0,10},{1,11},{2,8},{3,9},{4,14},{5,15},{6,12},{7,13},{8,2},{9,3},... | collective-permute-start | bytes 196616 | tf_op jit(solution)/shard_map/ppermute | solution.py:745
  84.4 1.0 collective-permute-start.24
  85.3 0.5 collective-permute-done.21.refs_3_
  85.8 3.6 %collective-permute-start.25 = (bf16[256,128]{1,0:T(8,128)(2,1)S(1)}, bf16[256,128]{1,0:T(8,128)(2,1)S(1)}, u32[]{:S(2)}, u32[]{:S(2)}) collective-permute-start(bf16[256,128]{1,0:T(8,128)(2,1)S(1)} %get-tuple-element.99), channel_id=1, source_target_pairs={{0,14},{1,15},{2,12},{3,13},{4,10},{5,11},{6,8},{7,9},{8,6},{9,7},... | collective-permute-start | bytes 196616 | tf_op jit(solution)/shard_map/ppermute | solution.py:745
  89.4 2.0 %collective-permute-done.22.refs_4_ = bf16[256,128]{1,0:T(8,128)(2,1)S(1)} collective-permute-done((bf16[256,128]{1,0:T(8,128)(2,1)S(1)}, bf16[256,128]{1,0:T(8,128)(2,1)S(1)}, u32[]{:S(2)}, u32[]{:S(2)}) %collective-permute-start.22) | collective-permute-done | bytes 65568 | tf_op jit(solution)/shard_map/ppermute | solution.py:745
  91.4 2.2 %collective-permute-done.23.refs_5_ = bf16[256,128]{1,0:T(8,128)(2,1)S(1)} collective-permute-done((bf16[256,128]{1,0:T(8,128)(2,1)S(1)}, bf16[256,128]{1,0:T(8,128)(2,1)S(1)}, u32[]{:S(2)}, u32[]{:S(2)}) %collective-permute-start.23) | collective-permute-done | bytes 65568 | tf_op jit(solution)/shard_map/ppermute | solution.py:745
  93.6 4.1 %tail.1 = (bf16[256,1024]{1,0:T(8,128)(2,1)}, bf16[64,1152]{1,0:T(8,128)(2,1)S(1)}, bf16[64,1152]{1,0:T(8,128)(2,1)S(1)}, bf16[64,1152]{1,0:T(8,128)(2,1)S(1)}, bf16[64,1152]{1,0:T(8,128)(2,1)S(1)}) custom-call(bf16[256,128]{1,0:T(8,128)(2,1)S(1)} %get-tuple-element.92.refs_0_, bf16[256,128]{1,0:T(8,128)(2,1)S(1)} %collective-permute-done.19.refs_1_, ...), custom_call_target="tpu_custom_call" | custom-call | tf_op jit(solution)/shard_map/tail/pallas_call | solution.py:495
  97.7 1.4 %collective-permute-start.27 = (bf16[64,1152]{1,0:T(8,128)(2,1)S(1)}, bf16[64,1152]{1,0:T(8,128)(2,1)S(1)}, u32[]{:S(2)}, u32[]{:S(2)}) collective-permute-start(bf16[64,1152]{1,0:T(8,128)(2,1)S(1)} %get-tuple-element.105), channel_id=1, source_target_pairs={{0,2},{1,3},{2,0},{3,1},{4,6},{5,7},{6,4},{7,5},{8,10},{9,11},{10,... | collective-permute-start | bytes 442376 | tf_op jit(solution)/shard_map/ppermute | solution.py:764
  99.1 0.8 collective-permute-start.29
  99.9 3.8 %collective-permute-done.27.refs_1_ = bf16[64,1152]{1,0:T(8,128)(2,1)S(1)} collective-permute-done((bf16[64,1152]{1,0:T(8,128)(2,1)S(1)}, bf16[64,1152]{1,0:T(8,128)(2,1)S(1)}, u32[]{:S(2)}, u32[]{:S(2)}) %collective-permute-start.27) | collective-permute-done | bytes 147488 | tf_op jit(solution)/shard_map/ppermute | solution.py:764
  103.7 1.5 %collective-permute-done.28.refs_2_ = bf16[64,1152]{1,0:T(8,128)(2,1)S(1)} collective-permute-done((bf16[64,1152]{1,0:T(8,128)(2,1)S(1)}, bf16[64,1152]{1,0:T(8,128)(2,1)S(1)}, u32[]{:S(2)}, u32[]{:S(2)}) %collective-permute-start.28) | collective-permute-done | bytes 147488 | tf_op jit(solution)/shard_map/ppermute | solution.py:765
  105.2 1.2 deal.1
  106.4 3.4 %collective-permute-start.30 = (bf16[16,1152]{1,0:T(8,128)(2,1)S(1)}, bf16[16,1152]{1,0:T(8,128)(2,1)S(1)}, u32[]{:S(2)}, u32[]{:S(2)}) collective-permute-start(bf16[16,1152]{1,0:T(8,128)(2,1)S(1)} %get-tuple-element.109), channel_id=1, source_target_pairs={{0,4},{1,5},{2,6},{3,7},{4,0},{5,1},{6,2},{7,3},{8,12},{9,13},{10,... | collective-permute-start | bytes 110600 | tf_op jit(solution)/shard_map/ppermute | solution.py:770
  109.8 0.2 collective-permute-start.31
  110.0 2.3 %collective-permute-start.32 = (bf16[16,1152]{1,0:T(8,128)(2,1)S(1)}, bf16[16,1152]{1,0:T(8,128)(2,1)S(1)}, u32[]{:S(2)}, u32[]{:S(2)}) collective-permute-start(bf16[16,1152]{1,0:T(8,128)(2,1)S(1)} %get-tuple-element.111), channel_id=1, source_target_pairs={{0,12},{1,13},{2,14},{3,15},{4,8},{5,9},{6,10},{7,11},{8,4},{9,5},... | collective-permute-start | bytes 110600 | tf_op jit(solution)/shard_map/ppermute | solution.py:770
  112.2 3.8 %collective-permute-done.31.refs_2_ = bf16[16,1152]{1,0:T(8,128)(2,1)S(1)} collective-permute-done((bf16[16,1152]{1,0:T(8,128)(2,1)S(1)}, bf16[16,1152]{1,0:T(8,128)(2,1)S(1)}, u32[]{:S(2)}, u32[]{:S(2)}) %collective-permute-start.31) | collective-permute-done | bytes 36896 | tf_op jit(solution)/shard_map/ppermute | solution.py:770
  116.0 1.1 join.1
  (32 shorter events, 0.2 us)
Async XLA Ops:
  1.9 21.8 %collective-permute-start.1 = (bf16[288,1024]{1,0:T(8,128)(2,1)S(1)}, bf16[288,1024]{1,0:T(8,128)(2,1)S(1)}, u32[]{:S(2)}, u32[]{:S(2)}) collective-permute-start(bf16[288,1024]{1,0:T(8,128)(2,1)S(1)} %get-tuple-element.57.refs_0_.refs_1_), channel_id=1, source_target_pairs={{0,2},{1,3},{4,0},{5,1},{8,4},{9,5},{12,8},{13,9},{14,12},{15,13},... | collective-permute-start | bytes 1769480 | tf_op jit(solution)/shard_map/ppermute | solution.py:681
  5.0 18.8 %collective-permute-start = (bf16[288,1024]{1,0:T(8,128)(2,1)S(1)}, bf16[288,1024]{1,0:T(8,128)(2,1)S(1)}, u32[]{:S(2)}, u32[]{:S(2)}) collective-permute-start(bf16[288,1024]{1,0:T(8,128)(2,1)S(1)} %get-tuple-element.57.refs_0_.refs_1_), channel_id=1, source_target_pairs={{0,4},{1,5},{4,8},{5,9},{8,12},{9,13},{12,14},{13,15},{14,10},{15,... | collective-permute-start | bytes 1769480 | tf_op jit(solution)/shard_map/ppermute | solution.py:680
  5.1 1.3 %collective-permute-start.2 = (bf16[2,64,384]{2,1,0:T(8,128)(2,1)S(1)}, bf16[2,64,384]{2,1,0:T(8,128)(2,1)S(1)}, u32[]{:S(2)}, u32[]{:S(2)}) collective-permute-start(bf16[2,64,384]{2,1,0:T(8,128)(2,1)S(1)} %get-tuple-element.59), channel_id=1, source_target_pairs={{0,1},{1,0},{2,3},{3,2},{4,5},{5,4},{6,7},{7,6},{8,9},{9,8},{10,11... | collective-permute-start | bytes 294920 | tf_op jit(solution)/shard_map/ppermute | solution.py:625
  6.4 17.3 %collective-permute-start.4 = (bf16[128,384]{1,0:T(8,128)(2,1)S(1)}, bf16[128,384]{1,0:T(8,128)(2,1)S(1)}, u32[]{:S(2)}, u32[]{:S(2)}) collective-permute-start(bf16[128,384]{1,0:T(8,128)(2,1)S(1)} %get-tuple-element.61), channel_id=1, source_target_pairs={{0,8},{1,11},{2,10},{3,9},{4,12},{5,15},{6,14},{7,13},{8,0},{9,3},... | collective-permute-start | bytes 294920 | tf_op jit(solution)/shard_map/ppermute | solution.py:636
  9.4 14.3 %collective-permute-start.3 = (bf16[128,384]{1,0:T(8,128)(2,1)S(1)}, bf16[128,384]{1,0:T(8,128)(2,1)S(1)}, u32[]{:S(2)}, u32[]{:S(2)}) collective-permute-start(bf16[128,384]{1,0:T(8,128)(2,1)S(1)} %get-tuple-element.60.own_ref), channel_id=1, source_target_pairs={{1,3},{3,1},{5,7},{7,5},{9,11},{11,9},{13,15},{15,13},{16,20},{17,... | collective-permute-start | bytes 294920 | tf_op jit(solution)/shard_map/ppermute | solution.py:636
  23.8 6.4 %collective-permute-start.7 = (bf16[2,128,384]{2,1,0:T(8,128)(2,1)S(1)}, bf16[2,128,384]{2,1,0:T(8,128)(2,1)S(1)}, u32[]{:S(2)}, u32[]{:S(2)}) collective-permute-start(bf16[2,128,384]{2,1,0:T(8,128)(2,1)S(1)} %keep.1.refs_0_.own_ref), channel_id=1, source_target_pairs={{0,16},{16,0},{1,17},{17,1},{2,18},{18,2},{3,19},{19,3},{4,20},{20... | collective-permute-start | bytes 589832 | tf_op jit(solution)/shard_map/ppermute | solution.py:686
  25.3 14.5 %collective-permute-start.5 = (bf16[288,1024]{1,0:T(8,128)(2,1)S(1)}, bf16[288,1024]{1,0:T(8,128)(2,1)S(1)}, u32[]{:S(2)}, u32[]{:S(2)}) collective-permute-start(bf16[288,1024]{1,0:T(8,128)(2,1)S(1)} %collective-permute-done.refs_2_.refs_3_), channel_id=1, source_target_pairs={{0,4},{1,5},{4,8},{5,9},{8,12},{9,13},{12,14},{13,15},{14,10},{15,... | collective-permute-start | bytes 1769480 | tf_op jit(solution)/shard_map/ppermute | solution.py:680
  26.1 15.0 %collective-permute-start.6 = (bf16[288,1024]{1,0:T(8,128)(2,1)S(1)}, bf16[288,1024]{1,0:T(8,128)(2,1)S(1)}, u32[]{:S(2)}, u32[]{:S(2)}) collective-permute-start(bf16[288,1024]{1,0:T(8,128)(2,1)S(1)} %collective-permute-done.1.refs_4_.refs_5_), channel_id=1, source_target_pairs={{0,2},{1,3},{4,0},{5,1},{8,4},{9,5},{12,8},{13,9},{14,12},{15,13},... | collective-permute-start | bytes 1769480 | tf_op jit(solution)/shard_map/ppermute | solution.py:681
  30.2 1.8 %collective-permute-start.8 = (bf16[4,128,384]{2,1,0:T(8,128)(2,1)S(1)}, bf16[4,128,384]{2,1,0:T(8,128)(2,1)S(1)}, u32[]{:S(2)}, u32[]{:S(2)}) collective-permute-start(bf16[4,128,384]{2,1,0:T(8,128)(2,1)S(1)} %gather_blocks.1), channel_id=1, source_target_pairs={{0,1},{1,0},{2,3},{3,2},{4,5},{5,4},{6,7},{7,6},{8,9},{9,8},{10,11... | collective-permute-start | bytes 1179656 | tf_op jit(solution)/shard_map/ppermute | solution.py:690
  32.2 19.0 %copy-start.2 = (f32[1024]{0:T(1024)S(1)}, f32[1024]{0:T(1024)}, u32[]{:S(2)}) copy-start(f32[1024]{0:T(1024)} %param.11) | copy-start | bytes 12292
  41.0 14.1 %collective-permute-start.9 = (bf16[288,1024]{1,0:T(8,128)(2,1)S(1)}, bf16[288,1024]{1,0:T(8,128)(2,1)S(1)}, u32[]{:S(2)}, u32[]{:S(2)}) collective-permute-start(bf16[288,1024]{1,0:T(8,128)(2,1)S(1)} %collective-permute-done.5.refs_6_.refs_7_), channel_id=1, source_target_pairs={{0,4},{1,5},{4,8},{5,9},{8,12},{9,13},{12,14},{13,15},{14,10},{15,... | collective-permute-start | bytes 1769480 | tf_op jit(solution)/shard_map/ppermute | solution.py:699
  42.8 14.0 %collective-permute-start.10 = (bf16[288,1024]{1,0:T(8,128)(2,1)S(1)}, bf16[288,1024]{1,0:T(8,128)(2,1)S(1)}, u32[]{:S(2)}, u32[]{:S(2)}) collective-permute-start(bf16[288,1024]{1,0:T(8,128)(2,1)S(1)} %collective-permute-done.6.refs_8_.refs_9_), channel_id=1, source_target_pairs={{0,2},{1,3},{4,0},{5,1},{8,4},{9,5},{12,8},{13,9},{14,12},{15,13},... | collective-permute-start | bytes 1769480 | tf_op jit(solution)/shard_map/ppermute | solution.py:700
  43.1 8.1 %collective-permute-start.11 = (bf16[5,32,1024]{2,1,0:T(8,128)(2,1)S(1)}, bf16[5,32,1024]{2,1,0:T(8,128)(2,1)S(1)}, u32[]{:S(2)}, u32[]{:S(2)}) collective-permute-start(bf16[5,32,1024]{2,1,0:T(8,128)(2,1)S(1)} %collect.3.refs_0_), channel_id=1, source_target_pairs={{0,16},{16,0},{1,17},{17,1},{2,18},{18,2},{3,19},{19,3},{4,20},{20... | collective-permute-start | bytes 983048 | tf_op jit(solution)/shard_map/ppermute | solution.py:696
  56.8 8.4 %collective-permute-start.13 = (bf16[144,1024]{1,0:T(8,128)(2,1)S(1)}, bf16[144,1024]{1,0:T(8,128)(2,1)S(1)}, u32[]{:S(2)}, u32[]{:S(2)}) collective-permute-start(bf16[144,1024]{1,0:T(8,128)(2,1)S(1)} %slice.6), channel_id=1, source_target_pairs={{0,4},{1,5},{4,8},{5,9},{8,12},{9,13},{12,14},{13,15},{14,10},{15,... | collective-permute-start | bytes 884744 | tf_op jit(solution)/shard_map/ppermute | solution.py:704
  57.4 7.8 %collective-permute-start.14 = (bf16[144,1024]{1,0:T(8,128)(2,1)S(1)}, bf16[144,1024]{1,0:T(8,128)(2,1)S(1)}, u32[]{:S(2)}, u32[]{:S(2)}) collective-permute-start(bf16[144,1024]{1,0:T(8,128)(2,1)S(1)} %slice.7), channel_id=1, source_target_pairs={{0,2},{1,3},{4,0},{5,1},{8,4},{9,5},{12,8},{13,9},{14,12},{15,13},... | collective-permute-start | bytes 884744 | tf_op jit(solution)/shard_map/ppermute | solution.py:705
  58.9 5.0 %collective-permute-start.12 = (bf16[2,32,1024]{2,1,0:T(8,128)(2,1)S(1)}, bf16[2,32,1024]{2,1,0:T(8,128)(2,1)S(1)}, u32[]{:S(2)}, u32[]{:S(2)}) collective-permute-start(bf16[2,32,1024]{2,1,0:T(8,128)(2,1)S(1)} %collect.4.refs_2_), channel_id=1, source_target_pairs={{0,16},{16,0},{1,17},{17,1},{2,18},{18,2},{3,19},{19,3},{4,20},{20... | collective-permute-start | bytes 393224 | tf_op jit(solution)/shard_map/ppermute | solution.py:709
  65.2 2.8 %collective-permute-start.15 = (bf16[10,2,128,128]{3,2,1,0:T(8,128)(2,1)S(1)}, bf16[10,2,128,128]{3,2,1,0:T(8,128)(2,1)S(1)}, u32[]{:S(2)}, u32[]{:S(2)}) collective-permute-start(bf16[10,2,128,128]{3,2,1,0:T(8,128)(2,1)S(1)} %get-tuple-element.87), channel_id=1, source_target_pairs={{0,1},{1,0},{2,3},{3,2},{4,5},{5,4},{6,7},{7,6},{8,9},{9,8},{10,11... | collective-permute-start | bytes 1966088 | tf_op jit(solution)/shard_map/ppermute | solution.py:676
  65.3 2.7 %collective-permute-start.16 = (bf16[4,2,128,128]{3,2,1,0:T(8,128)(2,1)S(1)}, bf16[4,2,128,128]{3,2,1,0:T(8,128)(2,1)S(1)}, u32[]{:S(2)}, u32[]{:S(2)}) collective-permute-start(bf16[4,2,128,128]{3,2,1,0:T(8,128)(2,1)S(1)} %get-tuple-element.88), channel_id=1, source_target_pairs={{0,1},{1,0},{2,3},{3,2},{4,5},{5,4},{6,7},{7,6},{8,9},{9,8},{10,11... | collective-permute-start | bytes 786440 | tf_op jit(solution)/shard_map/ppermute | solution.py:676
  65.8 2.2 %copy-start.3 = (s32[32,8]{0,1:T(8,128)S(1)}, s32[32,8]{0,1:T(8,128)}, u32[]{:S(2)}) copy-start(s32[32,8]{0,1:T(8,128)} %param.18) | copy-start | bytes 3076
  65.8 2.2 %copy-start.5 = (s32[32]{0:T(128)S(1)}, s32[32]{0:T(128)}, u32[]{:S(2)}) copy-start(s32[32]{0:T(128)} %counts_ref.1) | copy-start | bytes 388
  66.6 1.4 %collective-permute-start.17 = (bf16[2,2,128,128]{3,2,1,0:T(8,128)(2,1)S(1)}, bf16[2,2,128,128]{3,2,1,0:T(8,128)(2,1)S(1)}, u32[]{:S(2)}, u32[]{:S(2)}) collective-permute-start(bf16[2,2,128,128]{3,2,1,0:T(8,128)(2,1)S(1)} %get-tuple-element.89), channel_id=1, source_target_pairs={{0,1},{1,0},{2,3},{3,2},{4,5},{5,4},{6,7},{7,6},{8,9},{9,8},{10,11... | collective-permute-start | bytes 393224 | tf_op jit(solution)/shard_map/ppermute | solution.py:676
  66.8 11.2 %collective-permute-start.18 = (bf16[1,32,1024]{2,1,0:T(8,128)(2,1)S(1)}, bf16[1,32,1024]{2,1,0:T(8,128)(2,1)S(1)}, u32[]{:S(2)}, u32[]{:S(2)}) collective-permute-start(bf16[1,32,1024]{2,1,0:T(8,128)(2,1)S(1)} %collect.5.refs_4_), channel_id=1, source_target_pairs={{0,16},{16,0},{1,17},{17,1},{2,18},{18,2},{3,19},{19,3},{4,20},{20... | collective-permute-start | bytes 196616 | tf_op jit(solution)/shard_map/ppermute | solution.py:723
  68.1 25.5 %copy-start = (bf16[256,1024]{1,0:T(8,128)(2,1)S(1)}, bf16[256,1024]{1,0:T(8,128)(2,1)}, u32[]{:S(2)}) copy-start(bf16[256,1024]{1,0:T(8,128)(2,1)} %refs_8_.1) | copy-start | bytes 1572868
  68.1 25.5 %copy-start.1 = (bf16[256,1024]{1,0:T(8,128)(2,1)S(1)}, bf16[256,1024]{1,0:T(8,128)(2,1)}, u32[]{:S(2)}) copy-start(bf16[256,1024]{1,0:T(8,128)(2,1)} %refs_10_.1) | copy-start | bytes 1572868
  68.1 25.5 %copy-start.4 = (f32[1024]{0:T(1024)S(1)}, f32[1024]{0:T(1024)}, u32[]{:S(2)}) copy-start(f32[1024]{0:T(1024)} %param.16) | copy-start | bytes 12292
  78.1 15.5 %collective-permute-start.26 = (bf16[8,2,32,1024]{3,2,1,0:T(8,128)(2,1)S(1)}, bf16[8,2,32,1024]{3,2,1,0:T(8,128)(2,1)S(1)}, u32[]{:S(2)}, u32[]{:S(2)}) collective-permute-start(bf16[8,2,32,1024]{3,2,1,0:T(8,128)(2,1)S(1)} %pair_rows.1), channel_id=1, source_target_pairs={{0,1},{1,0},{2,3},{3,2},{4,5},{5,4},{6,7},{7,6},{8,9},{9,8},{10,11... | collective-permute-start | bytes 3145736 | tf_op jit(solution)/shard_map/ppermute | solution.py:743
  78.2 4.5 %collective-permute-start.19 = (bf16[256,128]{1,0:T(8,128)(2,1)S(1)}, bf16[256,128]{1,0:T(8,128)(2,1)S(1)}, u32[]{:S(2)}, u32[]{:S(2)}) collective-permute-start(bf16[256,128]{1,0:T(8,128)(2,1)S(1)} %get-tuple-element.93), channel_id=1, source_target_pairs={{0,2},{1,3},{2,0},{3,1},{4,6},{5,7},{6,4},{7,5},{8,10},{9,11},{10,... | collective-permute-start | bytes 196616 | tf_op jit(solution)/shard_map/ppermute | solution.py:745
  78.5 5.9 %collective-permute-start.20 = (bf16[256,128]{1,0:T(8,128)(2,1)S(1)}, bf16[256,128]{1,0:T(8,128)(2,1)S(1)}, u32[]{:S(2)}, u32[]{:S(2)}) collective-permute-start(bf16[256,128]{1,0:T(8,128)(2,1)S(1)} %get-tuple-element.94), channel_id=1, source_target_pairs={{0,4},{1,5},{2,6},{3,7},{4,0},{5,1},{6,2},{7,3},{8,12},{9,13},{10,... | collective-permute-start | bytes 196616 | tf_op jit(solution)/shard_map/ppermute | solution.py:745
  78.9 6.9 %collective-permute-start.21 = (bf16[256,128]{1,0:T(8,128)(2,1)S(1)}, bf16[256,128]{1,0:T(8,128)(2,1)S(1)}, u32[]{:S(2)}, u32[]{:S(2)}) collective-permute-start(bf16[256,128]{1,0:T(8,128)(2,1)S(1)} %get-tuple-element.95), channel_id=1, source_target_pairs={{0,6},{1,7},{2,4},{3,5},{4,2},{5,3},{6,0},{7,1},{8,14},{9,15},{10,... | collective-permute-start | bytes 196616 | tf_op jit(solution)/shard_map/ppermute | solution.py:745
  81.7 9.6 %collective-permute-start.22 = (bf16[256,128]{1,0:T(8,128)(2,1)S(1)}, bf16[256,128]{1,0:T(8,128)(2,1)S(1)}, u32[]{:S(2)}, u32[]{:S(2)}) collective-permute-start(bf16[256,128]{1,0:T(8,128)(2,1)S(1)} %get-tuple-element.96), channel_id=1, source_target_pairs={{0,8},{1,9},{2,10},{3,11},{4,12},{5,13},{6,14},{7,15},{8,0},{9,1},... | collective-permute-start | bytes 196616 | tf_op jit(solution)/shard_map/ppermute | solution.py:745
  82.7 10.9 %collective-permute-start.23 = (bf16[256,128]{1,0:T(8,128)(2,1)S(1)}, bf16[256,128]{1,0:T(8,128)(2,1)S(1)}, u32[]{:S(2)}, u32[]{:S(2)}) collective-permute-start(bf16[256,128]{1,0:T(8,128)(2,1)S(1)} %get-tuple-element.97), channel_id=1, source_target_pairs={{0,10},{1,11},{2,8},{3,9},{4,14},{5,15},{6,12},{7,13},{8,2},{9,3},... | collective-permute-start | bytes 196616 | tf_op jit(solution)/shard_map/ppermute | solution.py:745
  84.4 9.2 %collective-permute-start.24 = (bf16[256,128]{1,0:T(8,128)(2,1)S(1)}, bf16[256,128]{1,0:T(8,128)(2,1)S(1)}, u32[]{:S(2)}, u32[]{:S(2)}) collective-permute-start(bf16[256,128]{1,0:T(8,128)(2,1)S(1)} %get-tuple-element.98), channel_id=1, source_target_pairs={{0,12},{1,13},{2,14},{3,15},{4,8},{5,9},{6,10},{7,11},{8,4},{9,5},... | collective-permute-start | bytes 196616 | tf_op jit(solution)/shard_map/ppermute | solution.py:745
  85.8 7.8 %collective-permute-start.25 = (bf16[256,128]{1,0:T(8,128)(2,1)S(1)}, bf16[256,128]{1,0:T(8,128)(2,1)S(1)}, u32[]{:S(2)}, u32[]{:S(2)}) collective-permute-start(bf16[256,128]{1,0:T(8,128)(2,1)S(1)} %get-tuple-element.99), channel_id=1, source_target_pairs={{0,14},{1,15},{2,12},{3,13},{4,10},{5,11},{6,8},{7,9},{8,6},{9,7},... | collective-permute-start | bytes 196616 | tf_op jit(solution)/shard_map/ppermute | solution.py:745
  97.7 6.0 %collective-permute-start.27 = (bf16[64,1152]{1,0:T(8,128)(2,1)S(1)}, bf16[64,1152]{1,0:T(8,128)(2,1)S(1)}, u32[]{:S(2)}, u32[]{:S(2)}) collective-permute-start(bf16[64,1152]{1,0:T(8,128)(2,1)S(1)} %get-tuple-element.105), channel_id=1, source_target_pairs={{0,2},{1,3},{2,0},{3,1},{4,6},{5,7},{6,4},{7,5},{8,10},{9,11},{10,... | collective-permute-start | bytes 442376 | tf_op jit(solution)/shard_map/ppermute | solution.py:764
  99.1 6.1 %collective-permute-start.28 = (bf16[64,1152]{1,0:T(8,128)(2,1)S(1)}, bf16[64,1152]{1,0:T(8,128)(2,1)S(1)}, u32[]{:S(2)}, u32[]{:S(2)}) collective-permute-start(bf16[64,1152]{1,0:T(8,128)(2,1)S(1)} %get-tuple-element.106), channel_id=1, source_target_pairs={{0,3},{1,2},{2,1},{3,0},{4,7},{5,6},{6,5},{7,4},{8,11},{9,10},{10,... | collective-permute-start | bytes 442376 | tf_op jit(solution)/shard_map/ppermute | solution.py:765
  99.1 6.1 %collective-permute-start.29 = (bf16[64,1152]{1,0:T(8,128)(2,1)S(1)}, bf16[64,1152]{1,0:T(8,128)(2,1)S(1)}, u32[]{:S(2)}, u32[]{:S(2)}) collective-permute-start(bf16[64,1152]{1,0:T(8,128)(2,1)S(1)} %get-tuple-element.107), channel_id=1, source_target_pairs={{0,1},{1,0},{2,3},{3,2},{4,5},{5,4},{6,7},{7,6},{8,9},{9,8},{10,11... | collective-permute-start | bytes 442376 | tf_op jit(solution)/shard_map/ppermute | solution.py:766
  106.4 5.8 %collective-permute-start.30 = (bf16[16,1152]{1,0:T(8,128)(2,1)S(1)}, bf16[16,1152]{1,0:T(8,128)(2,1)S(1)}, u32[]{:S(2)}, u32[]{:S(2)}) collective-permute-start(bf16[16,1152]{1,0:T(8,128)(2,1)S(1)} %get-tuple-element.109), channel_id=1, source_target_pairs={{0,4},{1,5},{2,6},{3,7},{4,0},{5,1},{6,2},{7,3},{8,12},{9,13},{10,... | collective-permute-start | bytes 110600 | tf_op jit(solution)/shard_map/ppermute | solution.py:770
  109.8 6.2 %collective-permute-start.31 = (bf16[16,1152]{1,0:T(8,128)(2,1)S(1)}, bf16[16,1152]{1,0:T(8,128)(2,1)S(1)}, u32[]{:S(2)}, u32[]{:S(2)}) collective-permute-start(bf16[16,1152]{1,0:T(8,128)(2,1)S(1)} %get-tuple-element.110), channel_id=1, source_target_pairs={{0,8},{1,9},{2,10},{3,11},{4,12},{5,13},{6,14},{7,15},{8,0},{9,1},... | collective-permute-start | bytes 110600 | tf_op jit(solution)/shard_map/ppermute | solution.py:770
  110.0 6.1 %collective-permute-start.32 = (bf16[16,1152]{1,0:T(8,128)(2,1)S(1)}, bf16[16,1152]{1,0:T(8,128)(2,1)S(1)}, u32[]{:S(2)}, u32[]{:S(2)}) collective-permute-start(bf16[16,1152]{1,0:T(8,128)(2,1)S(1)} %get-tuple-element.111), channel_id=1, source_target_pairs={{0,12},{1,13},{2,14},{3,15},{4,8},{5,9},{6,10},{7,11},{8,4},{9,5},... | collective-permute-start | bytes 110600 | tf_op jit(solution)/shard_map/ppermute | solution.py:770

commit v6 on v5

--- a/solution.py
+++ b/solution.py
@@ -366,10 +366,10 @@
         scores = jnp.concatenate(scores, axis=0)
         top = jnp.max(scores, axis=0, keepdims=True)
         weights = jnp.exp2((scores - top) * EXP2_SCALE)
-        total = jnp.sum(weights, axis=0, keepdims=True)
         values = jnp.concatenate([kv_all[p, 1] for p in picked], axis=1)[:width]
+        values = jnp.concatenate([values, jnp.ones((16, used * BLOCK), BF16)], axis=0)
         full = jnp.dot(values, weights.astype(BF16), preferred_element_type=F32)
-        full = full * (1.0 / total)
+        full = full[:width] * (1.0 / full[width : width + 1])
         result = jnp.concatenate(
             [
                 full[h * HEAD_DIM : (h + 1) * HEAD_DIM, h * BLOCK : (h + 1) * BLOCK]
@@ -474,9 +474,11 @@
         scores = lax.dot_general(own, stacked, NT, preferred_element_type=F32)
         top = jnp.max(scores, axis=0, keepdims=True)
         weights = jnp.exp2((scores - top) * EXP2_SCALE)
-        total = jnp.sum(weights, axis=0, keepdims=True)
         flipped = jnp.transpose(own.astype(F32)).astype(BF16)
-        full = jnp.dot(flipped, weights.astype(BF16), preferred_element_type=F32) / total
+        flipped = jnp.concatenate([flipped, jnp.ones((16, TOK_DEV), BF16)], axis=0)
+        full = jnp.dot(flipped, weights.astype(BF16), preferred_element_type=F32)
+        total = full[2 * HEAD_DIM : 2 * HEAD_DIM + 1]
+        full = full[: 2 * HEAD_DIM] * (1.0 / total)
         result = jnp.concatenate([full[:HEAD_DIM, :PROBES], full[HEAD_DIM:, PROBES:]], axis=0)
         emit(lo, jnp.transpose(result))
         logs = top * SCALE + jnp.log(total)
@@ -707,8 +709,6 @@
     if packed:
         middle = collect(spread(forward, backward), depth // 2)
         middle_twin = lax.ppermute(middle, "scan", twins)
-        q_all, kv_all, middle_twin = barrier((*state, middle_twin))
-        state = (q_all, kv_all)
     near_shards = (chips - 3, chips - 2)
     near = advance(spread(forward, backward), near_shards)
     pair, near, *final = barrier((pair, near, *final))

time: 117 us -> 117 us (level)
  waiting for transfers between devices: 57.4 us -> 55.6 us
  starting transfers between devices: 36.2 us -> 37.5 us
    ppermute x1, waiting for transfers between devices: 4.3 us -> 0.01 us  [per_device(): middle_twin = lax.ppermute(middle, 'scan', twins)]
    ppermute x1, waiting for transfers between devices: 0.01 us -> 3.33 us  [per_device(): lax.ppermute(forward[:length], 'seq', around(1))]
    ppermute x3, waiting for transfers between devices: 2.85 us -> 0.77 us  [per_device(): backward = lax.ppermute(backward, 'seq', around(-1))]
    ppermute x3, starting transfers between devices: 5.47 us -> 3.56 us  [per_device(): backward = lax.ppermute(backward, 'seq', around(-1))]
    ppermute x1, waiting for transfers between devices: 1.49 us -> 0.01 us  [per_device(): lax.ppermute(both_part, 'seq', [(i, i ^ 3) for i in range(ranks)])]
    ppermute x3, waiting for transfers between devices: 8.82 us -> 10.2 us  [per_device(): forward = lax.ppermute(forward, 'seq', around(1))]
    ppermute x2, waiting for transfers between devices: 13.6 us -> 14.9 us  [per_device(): lax.ppermute(sent[j], ('scan', 'seq'), serve(4 * j))]
  transfers between devices with their start and end apart: 33 -> 33, of which waited for: 18 -> 15; matrix products, arithmetic and copies ran while one was open for 0% -> 0% of each run, Pallas kernels for 13% -> 13%
where the time goes in v6:
time: 117 us
  waiting for transfers between devices  55.6 us (48%)
  starting transfers between devices  37.5 us (32%)
  Pallas kernels  22.7 us (19%)
    ppermute x2, waiting for transfers between devices, per_device(): lax.ppermute(sent[j], ('scan', 'seq'), serve(4 * j))  14.9 us
    ppermute x7, starting transfers between devices, per_device(): lax.ppermute(attended[k], 'seq', across(k))  11.2 us
    ppermute x3, waiting for transfers between devices, per_device(): forward = lax.ppermute(forward, 'seq', around(1))  10.2 us
    pallas_call x1, Pallas kernels, attend(): pl.pallas_call(functools.partial(attend_kernel, chips, group, heads, step...  10 us
    ppermute x1, waiting for transfers between devices, per_device(): early_twin = lax.ppermute(early, 'scan', twins)  6.88 us
    ppermute x7, waiting for transfers between devices, per_device(): lax.ppermute(attended[k], 'seq', across(k))  6.01 us
    ppermute x3, starting transfers between devices, per_device(): lax.ppermute(lines[k], 'seq', across(2 * k))  5.45 us
    pallas_call x3, Pallas kernels, project(): pl.pallas_call(functools.partial(project_kernel, chips, starts, width, sh...  4.8 us
  transfers between devices with their start and end apart: 33, of which 15 were waited for; matrix products, arithmetic and copies ran while one was open for 0% of the time, Pallas kernels for 13%

profile of v6, /device:TPU:0, one launch (start us, length us, event | category | flops | bytes accessed | tf_op | source)
XLA Modules:
  0.0 116.8 jit_solution(8121759054470615782)
XLA Ops:
  0.6 1.3 %prepare.1 = (bf16[288,1024]{1,0:T(8,128)(2,1)S(1)}, bf16[2,64,384]{2,1,0:T(8,128)(2,1)S(1)}, bf16[2,64,384]{2,1,0:T(8,128)(2,1)S(1)}) custom-call(bf16[256,1024]{1,0:T(8,128)(2,1)} %refs_8_.1, bf16[64,1024]{1,0:T(8,128)(2,1)} %query_ref.1, bf16[64,1024]{1,0:T(8,128)(2,1)} %key_ref.1, bf16[64,1024]{1,0:T(8,128)(2,1)} %value_ref.1, bf16[64,1024]{1,0:T(8,128)(2,1)} %out_ref.1), custom_call_target="tpu_custom_call" | custom-call | tf_op jit(solution)/shard_map/prepare/pallas_call | solution.py:111
  1.9 3.1 %collective-permute-start = (bf16[288,1024]{1,0:T(8,128)(2,1)S(1)}, bf16[288,1024]{1,0:T(8,128)(2,1)S(1)}, u32[]{:S(2)}, u32[]{:S(2)}) collective-permute-start(bf16[288,1024]{1,0:T(8,128)(2,1)S(1)} %get-tuple-element.54.refs_0_.refs_1_), channel_id=1, source_target_pairs={{0,4},{1,5},{4,8},{5,9},{8,12},{9,13},{12,14},{13,15},{14,10},{15,... | collective-permute-start | bytes 1769480 | tf_op jit(solution)/shard_map/ppermute | solution.py:682
  5.0 0.0 collective-permute-start.1
  5.0 1.3 %collective-permute-done.2.got_ref = bf16[2,64,384]{2,1,0:T(8,128)(2,1)S(1)} collective-permute-done((bf16[2,64,384]{2,1,0:T(8,128)(2,1)S(1)}, bf16[2,64,384]{2,1,0:T(8,128)(2,1)S(1)}, u32[]{:S(2)}, u32[]{:S(2)}) %collective-permute-start.2) | collective-permute-done | bytes 98336 | tf_op jit(solution)/shard_map/ppermute | solution.py:627
  6.4 0.7 collective-permute-start.3
  7.0 3.1 %collective-permute-start.4 = (bf16[128,384]{1,0:T(8,128)(2,1)S(1)}, bf16[128,384]{1,0:T(8,128)(2,1)S(1)}, u32[]{:S(2)}, u32[]{:S(2)}) collective-permute-start(bf16[128,384]{1,0:T(8,128)(2,1)S(1)} %get-tuple-element.58), channel_id=1, source_target_pairs={{0,8},{1,11},{2,10},{3,9},{4,12},{5,15},{6,14},{7,13},{8,0},{9,3},... | collective-permute-start | bytes 294920 | tf_op jit(solution)/shard_map/ppermute | solution.py:638
  10.1 0.0 collective-permute-done.3.near_ref
  10.1 14.9 %collective-permute-done.4.far_ref = bf16[128,384]{1,0:T(8,128)(2,1)S(1)} collective-permute-done((bf16[128,384]{1,0:T(8,128)(2,1)S(1)}, bf16[128,384]{1,0:T(8,128)(2,1)S(1)}, u32[]{:S(2)}, u32[]{:S(2)}) %collective-permute-start.4) | collective-permute-done | bytes 98336 | tf_op jit(solution)/shard_map/ppermute | solution.py:638
  25.0 0.0 collective-permute-done.refs_2_.refs_3_
  25.0 0.0 collective-permute-done.1.refs_4_.refs_5_
  25.1 2.6 %collective-permute-start.7 = (bf16[2,128,384]{2,1,0:T(8,128)(2,1)S(1)}, bf16[2,128,384]{2,1,0:T(8,128)(2,1)S(1)}, u32[]{:S(2)}, u32[]{:S(2)}) collective-permute-start(bf16[2,128,384]{2,1,0:T(8,128)(2,1)S(1)} %keep.1.refs_0_.own_ref), channel_id=1, source_target_pairs={{0,16},{16,0},{1,17},{17,1},{2,18},{18,2},{3,19},{19,3},{4,20},{20... | collective-permute-start | bytes 589832 | tf_op jit(solution)/shard_map/ppermute | solution.py:688
  27.6 0.0 collective-permute-start.5
  27.6 2.0 %collective-permute-start.6 = (bf16[288,1024]{1,0:T(8,128)(2,1)S(1)}, bf16[288,1024]{1,0:T(8,128)(2,1)S(1)}, u32[]{:S(2)}, u32[]{:S(2)}) collective-permute-start(bf16[288,1024]{1,0:T(8,128)(2,1)S(1)} %collective-permute-done.1.refs_4_.refs_5_), channel_id=1, source_target_pairs={{0,2},{1,3},{4,0},{5,1},{8,4},{9,5},{12,8},{13,9},{14,12},{15,13},... | collective-permute-start | bytes 1769480 | tf_op jit(solution)/shard_map/ppermute | solution.py:683
  29.7 1.6 %collective-permute-done.7.refs_1_.twin_ref = bf16[2,128,384]{2,1,0:T(8,128)(2,1)S(1)} collective-permute-done((bf16[2,128,384]{2,1,0:T(8,128)(2,1)S(1)}, bf16[2,128,384]{2,1,0:T(8,128)(2,1)S(1)}, u32[]{:S(2)}, u32[]{:S(2)}) %collective-permute-start.7) | collective-permute-done | bytes 196640 | tf_op jit(solution)/shard_map/ppermute | solution.py:688
  31.3 0.1 collective-permute-start.8
  31.4 1.7 %collective-permute-done.8.other_ref = bf16[4,128,384]{2,1,0:T(8,128)(2,1)S(1)} collective-permute-done((bf16[4,128,384]{2,1,0:T(8,128)(2,1)S(1)}, bf16[4,128,384]{2,1,0:T(8,128)(2,1)S(1)}, u32[]{:S(2)}, u32[]{:S(2)}) %collective-permute-start.8) | collective-permute-done | bytes 393248 | tf_op jit(solution)/shard_map/ppermute | solution.py:692
  33.1 0.2 assemble.1.refs_11_.refs_5_.refs_3_
  33.3 0.0 copy-start.2
  33.3 7.6 %collective-permute-done.5.refs_6_.refs_7_ = bf16[288,1024]{1,0:T(8,128)(2,1)S(1)} collective-permute-done((bf16[288,1024]{1,0:T(8,128)(2,1)S(1)}, bf16[288,1024]{1,0:T(8,128)(2,1)S(1)}, u32[]{:S(2)}, u32[]{:S(2)}) %collective-permute-start.5) | collective-permute-done | bytes 589856 | tf_op jit(solution)/shard_map/ppermute | solution.py:682
  40.9 0.2 collective-permute-done.6.refs_8_.refs_9_
  41.1 1.5 %collective-permute-start.10 = (bf16[288,1024]{1,0:T(8,128)(2,1)S(1)}, bf16[288,1024]{1,0:T(8,128)(2,1)S(1)}, u32[]{:S(2)}, u32[]{:S(2)}) collective-permute-start(bf16[288,1024]{1,0:T(8,128)(2,1)S(1)} %collective-permute-done.6.refs_8_.refs_9_), channel_id=1, source_target_pairs={{0,2},{1,3},{4,0},{5,1},{8,4},{9,5},{12,8},{13,9},{14,12},{15,13},... | collective-permute-start | bytes 1769480 | tf_op jit(solution)/shard_map/ppermute | solution.py:702
  42.7 0.5 collective-permute-start.9
  43.2 0.3 collective-permute-start.11
  43.4 6.9 %collective-permute-done.11.refs_1_ = bf16[5,32,1024]{2,1,0:T(8,128)(2,1)S(1)} collective-permute-done((bf16[5,32,1024]{2,1,0:T(8,128)(2,1)S(1)}, bf16[5,32,1024]{2,1,0:T(8,128)(2,1)S(1)}, u32[]{:S(2)}, u32[]{:S(2)}) %collective-permute-start.11) | collective-permute-done | bytes 327712 | tf_op jit(solution)/shard_map/ppermute | solution.py:698
  50.3 2.7 %project.3 = (bf16[16,128,128]{2,1,0:T(8,128)(2,1)S(1)}, bf16[32,2,128,128]{3,2,1,0:T(8,128)(2,1)S(1)}, bf16[10,2,128,128]{3,2,1,0:T(8,128)(2,1)S(1)}) custom-call(bf16[288,1024]{1,0:T(8,128)(2,1)S(1)} %get-tuple-element.54.refs_0_.refs_1_, bf16[288,1024]{1,0:T(8,128)(2,1)S(1)} %get-tuple-element.54.refs_0_.refs_1_, ...), custom_call_target="tpu_custom_call" | custom-call | tf_op jit(solution)/shard_map/project/pallas_call | solution.py:319
  53.0 0.5 collective-permute-done.10.refs_2_.refs_3_
  53.6 2.5 %collective-permute-done.9.refs_0_.refs_1_ = bf16[288,1024]{1,0:T(8,128)(2,1)S(1)} collective-permute-done((bf16[288,1024]{1,0:T(8,128)(2,1)S(1)}, bf16[288,1024]{1,0:T(8,128)(2,1)S(1)}, u32[]{:S(2)}, u32[]{:S(2)}) %collective-permute-start.9) | collective-permute-done | bytes 589856 | tf_op jit(solution)/shard_map/ppermute | solution.py:701
  56.1 0.3 collective-permute-start.12
  56.5 1.8 %collective-permute-start.13 = (bf16[144,1024]{1,0:T(8,128)(2,1)S(1)}, bf16[144,1024]{1,0:T(8,128)(2,1)S(1)}, u32[]{:S(2)}, u32[]{:S(2)}) collective-permute-start(bf16[144,1024]{1,0:T(8,128)(2,1)S(1)} %slice.7), channel_id=1, source_target_pairs={{0,2},{1,3},{4,0},{5,1},{8,4},{9,5},{12,8},{13,9},{14,12},{15,13},... | collective-permute-start | bytes 884744 | tf_op jit(solution)/shard_map/ppermute | solution.py:707
  58.3 1.3 %project.4 = (bf16[16,128,128]{2,1,0:T(8,128)(2,1)S(1)}, bf16[32,2,128,128]{3,2,1,0:T(8,128)(2,1)S(1)}, bf16[4,2,128,128]{3,2,1,0:T(8,128)(2,1)S(1)}) custom-call(bf16[288,1024]{1,0:T(8,128)(2,1)S(1)} %collective-permute-done.9.refs_0_.refs_1_, ...), custom_call_target="tpu_custom_call", output_to_operand_aliasing={{0}: (6, {}), {1}: (7, {})} | custom-call | tf_op jit(solution)/shard_map/project/pallas_call | solution.py:319
  59.6 3.3 %collective-permute-done.12.refs_0_ = bf16[144,1024]{1,0:T(8,128)(2,1)S(1)} collective-permute-done((bf16[144,1024]{1,0:T(8,128)(2,1)S(1)}, bf16[144,1024]{1,0:T(8,128)(2,1)S(1)}, u32[]{:S(2)}, u32[]{:S(2)}) %collective-permute-start.12) | collective-permute-done | bytes 294944 | tf_op jit(solution)/shard_map/ppermute | solution.py:706
  62.9 0.4 collective-permute-done.13.refs_1_
  63.2 0.5 collective-permute-start.15
  63.7 0.8 project.5
  64.6 0.0 copy-start.3
  64.6 0.0 copy-start.5
  64.6 0.1 collective-permute-start.16
  64.7 0.4 collective-permute-start.17
  65.1 1.7 %collective-permute-start.18 = (bf16[1,32,1024]{2,1,0:T(8,128)(2,1)S(1)}, bf16[1,32,1024]{2,1,0:T(8,128)(2,1)S(1)}, u32[]{:S(2)}, u32[]{:S(2)}) collective-permute-start(bf16[1,32,1024]{2,1,0:T(8,128)(2,1)S(1)} %collect.5.refs_4_), channel_id=1, source_target_pairs={{0,16},{16,0},{1,17},{17,1},{2,18},{18,2},{3,19},{19,3},{4,20},{20... | collective-permute-start | bytes 196616 | tf_op jit(solution)/shard_map/ppermute | solution.py:723
  66.8 0.0 copy-start
  66.8 0.0 copy-start.1
  66.9 0.0 copy-start.4
  66.9 10.0 %attend.1 = (bf16[32,2,128,128]{3,2,1,0:T(8,128)(2,1)S(1)}, bf16[256,128]{1,0:T(8,128)(2,1)S(1)}, bf16[256,128]{1,0:T(8,128)(2,1)S(1)}, bf16[256,128]{1,0:T(8,12...) custom-call(s32[8,32]{1,0:T(8,128)S(1)} %bitcast.10, ...), custom_call_target="tpu_custom_call", output_to_operand_aliasing={{0}: (3, {})} | custom-call | tf_op jit(solution)/shard_map/attend/pallas_call | solution.py:405
  76.9 0.1 pair_rows.1
  77.0 0.1 collective-permute-start.26
  77.1 1.8 %collective-permute-start.19 = (bf16[256,128]{1,0:T(8,128)(2,1)S(1)}, bf16[256,128]{1,0:T(8,128)(2,1)S(1)}, u32[]{:S(2)}, u32[]{:S(2)}) collective-permute-start(bf16[256,128]{1,0:T(8,128)(2,1)S(1)} %get-tuple-element.87), channel_id=1, source_target_pairs={{0,2},{1,3},{2,0},{3,1},{4,6},{5,7},{6,4},{7,5},{8,10},{9,11},{10,... | collective-permute-start | bytes 196616 | tf_op jit(solution)/shard_map/ppermute | solution.py:745
  78.9 1.5 %collective-permute-start.20 = (bf16[256,128]{1,0:T(8,128)(2,1)S(1)}, bf16[256,128]{1,0:T(8,128)(2,1)S(1)}, u32[]{:S(2)}, u32[]{:S(2)}) collective-permute-start(bf16[256,128]{1,0:T(8,128)(2,1)S(1)} %get-tuple-element.88), channel_id=1, source_target_pairs={{0,4},{1,5},{2,6},{3,7},{4,0},{5,1},{6,2},{7,3},{8,12},{9,13},{10,... | collective-permute-start | bytes 196616 | tf_op jit(solution)/shard_map/ppermute | solution.py:745
  80.4 0.3 collective-permute-start.21
  80.6 1.5 %collective-permute-start.22 = (bf16[256,128]{1,0:T(8,128)(2,1)S(1)}, bf16[256,128]{1,0:T(8,128)(2,1)S(1)}, u32[]{:S(2)}, u32[]{:S(2)}) collective-permute-start(bf16[256,128]{1,0:T(8,128)(2,1)S(1)} %get-tuple-element.90), channel_id=1, source_target_pairs={{0,8},{1,9},{2,10},{3,11},{4,12},{5,13},{6,14},{7,15},{8,0},{9,1},... | collective-permute-start | bytes 196616 | tf_op jit(solution)/shard_map/ppermute | solution.py:745
  82.1 2.6 %collective-permute-start.23 = (bf16[256,128]{1,0:T(8,128)(2,1)S(1)}, bf16[256,128]{1,0:T(8,128)(2,1)S(1)}, u32[]{:S(2)}, u32[]{:S(2)}) collective-permute-start(bf16[256,128]{1,0:T(8,128)(2,1)S(1)} %get-tuple-element.91), channel_id=1, source_target_pairs={{0,10},{1,11},{2,8},{3,9},{4,14},{5,15},{6,12},{7,13},{8,2},{9,3},... | collective-permute-start | bytes 196616 | tf_op jit(solution)/shard_map/ppermute | solution.py:745
  84.8 1.9 %collective-permute-start.24 = (bf16[256,128]{1,0:T(8,128)(2,1)S(1)}, bf16[256,128]{1,0:T(8,128)(2,1)S(1)}, u32[]{:S(2)}, u32[]{:S(2)}) collective-permute-start(bf16[256,128]{1,0:T(8,128)(2,1)S(1)} %get-tuple-element.92), channel_id=1, source_target_pairs={{0,12},{1,13},{2,14},{3,15},{4,8},{5,9},{6,10},{7,11},{8,4},{9,5},... | collective-permute-start | bytes 196616 | tf_op jit(solution)/shard_map/ppermute | solution.py:745
  86.6 1.7 %collective-permute-start.25 = (bf16[256,128]{1,0:T(8,128)(2,1)S(1)}, bf16[256,128]{1,0:T(8,128)(2,1)S(1)}, u32[]{:S(2)}, u32[]{:S(2)}) collective-permute-start(bf16[256,128]{1,0:T(8,128)(2,1)S(1)} %get-tuple-element.93), channel_id=1, source_target_pairs={{0,14},{1,15},{2,12},{3,13},{4,10},{5,11},{6,8},{7,9},{8,6},{9,7},... | collective-permute-start | bytes 196616 | tf_op jit(solution)/shard_map/ppermute | solution.py:745
  88.3 6.0 %collective-permute-done.23.refs_5_ = bf16[256,128]{1,0:T(8,128)(2,1)S(1)} collective-permute-done((bf16[256,128]{1,0:T(8,128)(2,1)S(1)}, bf16[256,128]{1,0:T(8,128)(2,1)S(1)}, u32[]{:S(2)}, u32[]{:S(2)}) %collective-permute-start.23) | collective-permute-done | bytes 65568 | tf_op jit(solution)/shard_map/ppermute | solution.py:745
  94.3 4.0 %tail.1 = (bf16[256,1024]{1,0:T(8,128)(2,1)}, bf16[64,1152]{1,0:T(8,128)(2,1)S(1)}, bf16[64,1152]{1,0:T(8,128)(2,1)S(1)}, bf16[64,1152]{1,0:T(8,128)(2,1)S(1)}, bf16[64,1152]{1,0:T(8,128)(2,1)S(1)}) custom-call(bf16[256,128]{1,0:T(8,128)(2,1)S(1)} %get-tuple-element.86.refs_0_, bf16[256,128]{1,0:T(8,128)(2,1)S(1)} %collective-permute-done.19.refs_1_, ...), custom_call_target="tpu_custom_call" | custom-call | tf_op jit(solution)/shard_map/tail/pallas_call | solution.py:497
  98.3 0.3 collective-permute-start.27
  98.6 1.9 %collective-permute-start.29 = (bf16[64,1152]{1,0:T(8,128)(2,1)S(1)}, bf16[64,1152]{1,0:T(8,128)(2,1)S(1)}, u32[]{:S(2)}, u32[]{:S(2)}) collective-permute-start(bf16[64,1152]{1,0:T(8,128)(2,1)S(1)} %get-tuple-element.101), channel_id=1, source_target_pairs={{0,1},{1,0},{2,3},{3,2},{4,5},{5,4},{6,7},{7,6},{8,9},{9,8},{10,11... | collective-permute-start | bytes 442376 | tf_op jit(solution)/shard_map/ppermute | solution.py:766
  100.5 4.2 %collective-permute-done.27.refs_1_ = bf16[64,1152]{1,0:T(8,128)(2,1)S(1)} collective-permute-done((bf16[64,1152]{1,0:T(8,128)(2,1)S(1)}, bf16[64,1152]{1,0:T(8,128)(2,1)S(1)}, u32[]{:S(2)}, u32[]{:S(2)}) %collective-permute-start.27) | collective-permute-done | bytes 147488 | tf_op jit(solution)/shard_map/ppermute | solution.py:764
  104.7 1.2 deal.1
  105.9 3.0 %collective-permute-start.30 = (bf16[16,1152]{1,0:T(8,128)(2,1)S(1)}, bf16[16,1152]{1,0:T(8,128)(2,1)S(1)}, u32[]{:S(2)}, u32[]{:S(2)}) collective-permute-start(bf16[16,1152]{1,0:T(8,128)(2,1)S(1)} %get-tuple-element.103), channel_id=1, source_target_pairs={{0,4},{1,5},{2,6},{3,7},{4,0},{5,1},{6,2},{7,3},{8,12},{9,13},{10,... | collective-permute-start | bytes 110600 | tf_op jit(solution)/shard_map/ppermute | solution.py:770
  108.9 0.9 collective-permute-start.31
  109.8 1.6 %collective-permute-start.32 = (bf16[16,1152]{1,0:T(8,128)(2,1)S(1)}, bf16[16,1152]{1,0:T(8,128)(2,1)S(1)}, u32[]{:S(2)}, u32[]{:S(2)}) collective-permute-start(bf16[16,1152]{1,0:T(8,128)(2,1)S(1)} %get-tuple-element.105), channel_id=1, source_target_pairs={{0,12},{1,13},{2,14},{3,15},{4,8},{5,9},{6,10},{7,11},{8,4},{9,5},... | collective-permute-start | bytes 110600 | tf_op jit(solution)/shard_map/ppermute | solution.py:770
  111.4 3.5 %collective-permute-done.31.refs_2_ = bf16[16,1152]{1,0:T(8,128)(2,1)S(1)} collective-permute-done((bf16[16,1152]{1,0:T(8,128)(2,1)S(1)}, bf16[16,1152]{1,0:T(8,128)(2,1)S(1)}, u32[]{:S(2)}, u32[]{:S(2)}) %collective-permute-start.31) | collective-permute-done | bytes 36896 | tf_op jit(solution)/shard_map/ppermute | solution.py:770
  114.9 0.8 collective-permute-done.32.refs_3_
  115.7 1.1 join.1
  (32 shorter events, 0.2 us)
Async XLA Ops:
  1.9 23.1 %collective-permute-start = (bf16[288,1024]{1,0:T(8,128)(2,1)S(1)}, bf16[288,1024]{1,0:T(8,128)(2,1)S(1)}, u32[]{:S(2)}, u32[]{:S(2)}) collective-permute-start(bf16[288,1024]{1,0:T(8,128)(2,1)S(1)} %get-tuple-element.54.refs_0_.refs_1_), channel_id=1, source_target_pairs={{0,4},{1,5},{4,8},{5,9},{8,12},{9,13},{12,14},{13,15},{14,10},{15,... | collective-permute-start | bytes 1769480 | tf_op jit(solution)/shard_map/ppermute | solution.py:682
  5.0 20.0 %collective-permute-start.1 = (bf16[288,1024]{1,0:T(8,128)(2,1)S(1)}, bf16[288,1024]{1,0:T(8,128)(2,1)S(1)}, u32[]{:S(2)}, u32[]{:S(2)}) collective-permute-start(bf16[288,1024]{1,0:T(8,128)(2,1)S(1)} %get-tuple-element.54.refs_0_.refs_1_), channel_id=1, source_target_pairs={{0,2},{1,3},{4,0},{5,1},{8,4},{9,5},{12,8},{13,9},{14,12},{15,13},... | collective-permute-start | bytes 1769480 | tf_op jit(solution)/shard_map/ppermute | solution.py:683
  5.0 1.3 %collective-permute-start.2 = (bf16[2,64,384]{2,1,0:T(8,128)(2,1)S(1)}, bf16[2,64,384]{2,1,0:T(8,128)(2,1)S(1)}, u32[]{:S(2)}, u32[]{:S(2)}) collective-permute-start(bf16[2,64,384]{2,1,0:T(8,128)(2,1)S(1)} %get-tuple-element.56), channel_id=1, source_target_pairs={{0,1},{1,0},{2,3},{3,2},{4,5},{5,4},{6,7},{7,6},{8,9},{9,8},{10,11... | collective-permute-start | bytes 294920 | tf_op jit(solution)/shard_map/ppermute | solution.py:627
  6.4 3.8 %collective-permute-start.3 = (bf16[128,384]{1,0:T(8,128)(2,1)S(1)}, bf16[128,384]{1,0:T(8,128)(2,1)S(1)}, u32[]{:S(2)}, u32[]{:S(2)}) collective-permute-start(bf16[128,384]{1,0:T(8,128)(2,1)S(1)} %get-tuple-element.57.own_ref), channel_id=1, source_target_pairs={{1,3},{3,1},{5,7},{7,5},{9,11},{11,9},{13,15},{15,13},{16,20},{17,... | collective-permute-start | bytes 294920 | tf_op jit(solution)/shard_map/ppermute | solution.py:638
  7.0 18.0 %collective-permute-start.4 = (bf16[128,384]{1,0:T(8,128)(2,1)S(1)}, bf16[128,384]{1,0:T(8,128)(2,1)S(1)}, u32[]{:S(2)}, u32[]{:S(2)}) collective-permute-start(bf16[128,384]{1,0:T(8,128)(2,1)S(1)} %get-tuple-element.58), channel_id=1, source_target_pairs={{0,8},{1,11},{2,10},{3,9},{4,12},{5,15},{6,14},{7,13},{8,0},{9,3},... | collective-permute-start | bytes 294920 | tf_op jit(solution)/shard_map/ppermute | solution.py:638
  25.1 6.2 %collective-permute-start.7 = (bf16[2,128,384]{2,1,0:T(8,128)(2,1)S(1)}, bf16[2,128,384]{2,1,0:T(8,128)(2,1)S(1)}, u32[]{:S(2)}, u32[]{:S(2)}) collective-permute-start(bf16[2,128,384]{2,1,0:T(8,128)(2,1)S(1)} %keep.1.refs_0_.own_ref), channel_id=1, source_target_pairs={{0,16},{16,0},{1,17},{17,1},{2,18},{18,2},{3,19},{19,3},{4,20},{20... | collective-permute-start | bytes 589832 | tf_op jit(solution)/shard_map/ppermute | solution.py:688
  27.6 13.3 %collective-permute-start.5 = (bf16[288,1024]{1,0:T(8,128)(2,1)S(1)}, bf16[288,1024]{1,0:T(8,128)(2,1)S(1)}, u32[]{:S(2)}, u32[]{:S(2)}) collective-permute-start(bf16[288,1024]{1,0:T(8,128)(2,1)S(1)} %collective-permute-done.refs_2_.refs_3_), channel_id=1, source_target_pairs={{0,4},{1,5},{4,8},{5,9},{8,12},{9,13},{12,14},{13,15},{14,10},{15,... | collective-permute-start | bytes 1769480 | tf_op jit(solution)/shard_map/ppermute | solution.py:682
  27.6 13.5 %collective-permute-start.6 = (bf16[288,1024]{1,0:T(8,128)(2,1)S(1)}, bf16[288,1024]{1,0:T(8,128)(2,1)S(1)}, u32[]{:S(2)}, u32[]{:S(2)}) collective-permute-start(bf16[288,1024]{1,0:T(8,128)(2,1)S(1)} %collective-permute-done.1.refs_4_.refs_5_), channel_id=1, source_target_pairs={{0,2},{1,3},{4,0},{5,1},{8,4},{9,5},{12,8},{13,9},{14,12},{15,13},... | collective-permute-start | bytes 1769480 | tf_op jit(solution)/shard_map/ppermute | solution.py:683
  31.3 1.8 %collective-permute-start.8 = (bf16[4,128,384]{2,1,0:T(8,128)(2,1)S(1)}, bf16[4,128,384]{2,1,0:T(8,128)(2,1)S(1)}, u32[]{:S(2)}, u32[]{:S(2)}) collective-permute-start(bf16[4,128,384]{2,1,0:T(8,128)(2,1)S(1)} %gather_blocks.1), channel_id=1, source_target_pairs={{0,1},{1,0},{2,3},{3,2},{4,5},{5,4},{6,7},{7,6},{8,9},{9,8},{10,11... | collective-permute-start | bytes 1179656 | tf_op jit(solution)/shard_map/ppermute | solution.py:692
  33.3 17.1 %copy-start.2 = (f32[1024]{0:T(1024)S(1)}, f32[1024]{0:T(1024)}, u32[]{:S(2)}) copy-start(f32[1024]{0:T(1024)} %param.11) | copy-start | bytes 12292
  41.1 12.4 %collective-permute-start.10 = (bf16[288,1024]{1,0:T(8,128)(2,1)S(1)}, bf16[288,1024]{1,0:T(8,128)(2,1)S(1)}, u32[]{:S(2)}, u32[]{:S(2)}) collective-permute-start(bf16[288,1024]{1,0:T(8,128)(2,1)S(1)} %collective-permute-done.6.refs_8_.refs_9_), channel_id=1, source_target_pairs={{0,2},{1,3},{4,0},{5,1},{8,4},{9,5},{12,8},{13,9},{14,12},{15,13},... | collective-permute-start | bytes 1769480 | tf_op jit(solution)/shard_map/ppermute | solution.py:702
  42.7 13.4 %collective-permute-start.9 = (bf16[288,1024]{1,0:T(8,128)(2,1)S(1)}, bf16[288,1024]{1,0:T(8,128)(2,1)S(1)}, u32[]{:S(2)}, u32[]{:S(2)}) collective-permute-start(bf16[288,1024]{1,0:T(8,128)(2,1)S(1)} %collective-permute-done.5.refs_6_.refs_7_), channel_id=1, source_target_pairs={{0,4},{1,5},{4,8},{5,9},{8,12},{9,13},{12,14},{13,15},{14,10},{15,... | collective-permute-start | bytes 1769480 | tf_op jit(solution)/shard_map/ppermute | solution.py:701
  43.2 7.1 %collective-permute-start.11 = (bf16[5,32,1024]{2,1,0:T(8,128)(2,1)S(1)}, bf16[5,32,1024]{2,1,0:T(8,128)(2,1)S(1)}, u32[]{:S(2)}, u32[]{:S(2)}) collective-permute-start(bf16[5,32,1024]{2,1,0:T(8,128)(2,1)S(1)} %collect.3.refs_0_), channel_id=1, source_target_pairs={{0,16},{16,0},{1,17},{17,1},{2,18},{18,2},{3,19},{19,3},{4,20},{20... | collective-permute-start | bytes 983048 | tf_op jit(solution)/shard_map/ppermute | solution.py:698
  56.1 6.8 %collective-permute-start.12 = (bf16[144,1024]{1,0:T(8,128)(2,1)S(1)}, bf16[144,1024]{1,0:T(8,128)(2,1)S(1)}, u32[]{:S(2)}, u32[]{:S(2)}) collective-permute-start(bf16[144,1024]{1,0:T(8,128)(2,1)S(1)} %slice.6), channel_id=1, source_target_pairs={{0,4},{1,5},{4,8},{5,9},{8,12},{9,13},{12,14},{13,15},{14,10},{15,... | collective-permute-start | bytes 884744 | tf_op jit(solution)/shard_map/ppermute | solution.py:706
  56.5 6.8 %collective-permute-start.13 = (bf16[144,1024]{1,0:T(8,128)(2,1)S(1)}, bf16[144,1024]{1,0:T(8,128)(2,1)S(1)}, u32[]{:S(2)}, u32[]{:S(2)}) collective-permute-start(bf16[144,1024]{1,0:T(8,128)(2,1)S(1)} %slice.7), channel_id=1, source_target_pairs={{0,2},{1,3},{4,0},{5,1},{8,4},{9,5},{12,8},{13,9},{14,12},{15,13},... | collective-permute-start | bytes 884744 | tf_op jit(solution)/shard_map/ppermute | solution.py:707
  63.2 3.6 %collective-permute-start.14 = (bf16[10,2,128,128]{3,2,1,0:T(8,128)(2,1)S(1)}, bf16[10,2,128,128]{3,2,1,0:T(8,128)(2,1)S(1)}, u32[]{:S(2)}, u32[]{:S(2)}) collective-permute-start(bf16[10,2,128,128]{3,2,1,0:T(8,128)(2,1)S(1)} %get-tuple-element.82), channel_id=1, source_target_pairs={{0,1},{1,0},{2,3},{3,2},{4,5},{5,4},{6,7},{7,6},{8,9},{9,8},{10,11... | collective-permute-start | bytes 1966088 | tf_op jit(solution)/shard_map/ppermute | solution.py:678
  63.2 3.6 %collective-permute-start.15 = (bf16[4,2,128,128]{3,2,1,0:T(8,128)(2,1)S(1)}, bf16[4,2,128,128]{3,2,1,0:T(8,128)(2,1)S(1)}, u32[]{:S(2)}, u32[]{:S(2)}) collective-permute-start(bf16[4,2,128,128]{3,2,1,0:T(8,128)(2,1)S(1)} %get-tuple-element.83), channel_id=1, source_target_pairs={{0,1},{1,0},{2,3},{3,2},{4,5},{5,4},{6,7},{7,6},{8,9},{9,8},{10,11... | collective-permute-start | bytes 786440 | tf_op jit(solution)/shard_map/ppermute | solution.py:678
  64.6 2.2 %copy-start.3 = (s32[32,8]{0,1:T(8,128)S(1)}, s32[32,8]{0,1:T(8,128)}, u32[]{:S(2)}) copy-start(s32[32,8]{0,1:T(8,128)} %param.18) | copy-start | bytes 3076
  64.6 2.2 %copy-start.5 = (s32[32]{0:T(128)S(1)}, s32[32]{0:T(128)}, u32[]{:S(2)}) copy-start(s32[32]{0:T(128)} %counts_ref.1) | copy-start | bytes 388
  64.6 2.2 %collective-permute-start.16 = (bf16[2,2,128,128]{3,2,1,0:T(8,128)(2,1)S(1)}, bf16[2,2,128,128]{3,2,1,0:T(8,128)(2,1)S(1)}, u32[]{:S(2)}, u32[]{:S(2)}) collective-permute-start(bf16[2,2,128,128]{3,2,1,0:T(8,128)(2,1)S(1)} %get-tuple-element.84), channel_id=1, source_target_pairs={{0,1},{1,0},{2,3},{3,2},{4,5},{5,4},{6,7},{7,6},{8,9},{9,8},{10,11... | collective-permute-start | bytes 393224 | tf_op jit(solution)/shard_map/ppermute | solution.py:678
  64.7 12.2 %collective-permute-start.17 = (bf16[2,32,1024]{2,1,0:T(8,128)(2,1)S(1)}, bf16[2,32,1024]{2,1,0:T(8,128)(2,1)S(1)}, u32[]{:S(2)}, u32[]{:S(2)}) collective-permute-start(bf16[2,32,1024]{2,1,0:T(8,128)(2,1)S(1)} %collect.4.refs_2_), channel_id=1, source_target_pairs={{0,16},{16,0},{1,17},{17,1},{2,18},{18,2},{3,19},{19,3},{4,20},{20... | collective-permute-start | bytes 393224 | tf_op jit(solution)/shard_map/ppermute | solution.py:711
  65.1 11.8 %collective-permute-start.18 = (bf16[1,32,1024]{2,1,0:T(8,128)(2,1)S(1)}, bf16[1,32,1024]{2,1,0:T(8,128)(2,1)S(1)}, u32[]{:S(2)}, u32[]{:S(2)}) collective-permute-start(bf16[1,32,1024]{2,1,0:T(8,128)(2,1)S(1)} %collect.5.refs_4_), channel_id=1, source_target_pairs={{0,16},{16,0},{1,17},{17,1},{2,18},{18,2},{3,19},{19,3},{4,20},{20... | collective-permute-start | bytes 196616 | tf_op jit(solution)/shard_map/ppermute | solution.py:723
  66.8 27.5 %copy-start = (bf16[256,1024]{1,0:T(8,128)(2,1)S(1)}, bf16[256,1024]{1,0:T(8,128)(2,1)}, u32[]{:S(2)}) copy-start(bf16[256,1024]{1,0:T(8,128)(2,1)} %refs_8_.1) | copy-start | bytes 1572868
  66.8 27.5 %copy-start.1 = (bf16[256,1024]{1,0:T(8,128)(2,1)S(1)}, bf16[256,1024]{1,0:T(8,128)(2,1)}, u32[]{:S(2)}) copy-start(bf16[256,1024]{1,0:T(8,128)(2,1)} %refs_10_.1) | copy-start | bytes 1572868
  66.9 27.5 %copy-start.4 = (f32[1024]{0:T(1024)S(1)}, f32[1024]{0:T(1024)}, u32[]{:S(2)}) copy-start(f32[1024]{0:T(1024)} %param.16) | copy-start | bytes 12292
  77.0 17.3 %collective-permute-start.26 = (bf16[8,2,32,1024]{3,2,1,0:T(8,128)(2,1)S(1)}, bf16[8,2,32,1024]{3,2,1,0:T(8,128)(2,1)S(1)}, u32[]{:S(2)}, u32[]{:S(2)}) collective-permute-start(bf16[8,2,32,1024]{3,2,1,0:T(8,128)(2,1)S(1)} %pair_rows.1), channel_id=1, source_target_pairs={{0,1},{1,0},{2,3},{3,2},{4,5},{5,4},{6,7},{7,6},{8,9},{9,8},{10,11... | collective-permute-start | bytes 3145736 | tf_op jit(solution)/shard_map/ppermute | solution.py:743
  77.1 5.1 %collective-permute-start.19 = (bf16[256,128]{1,0:T(8,128)(2,1)S(1)}, bf16[256,128]{1,0:T(8,128)(2,1)S(1)}, u32[]{:S(2)}, u32[]{:S(2)}) collective-permute-start(bf16[256,128]{1,0:T(8,128)(2,1)S(1)} %get-tuple-element.87), channel_id=1, source_target_pairs={{0,2},{1,3},{2,0},{3,1},{4,6},{5,7},{6,4},{7,5},{8,10},{9,11},{10,... | collective-permute-start | bytes 196616 | tf_op jit(solution)/shard_map/ppermute | solution.py:745
  78.9 5.9 %collective-permute-start.20 = (bf16[256,128]{1,0:T(8,128)(2,1)S(1)}, bf16[256,128]{1,0:T(8,128)(2,1)S(1)}, u32[]{:S(2)}, u32[]{:S(2)}) collective-permute-start(bf16[256,128]{1,0:T(8,128)(2,1)S(1)} %get-tuple-element.88), channel_id=1, source_target_pairs={{0,4},{1,5},{2,6},{3,7},{4,0},{5,1},{6,2},{7,3},{8,12},{9,13},{10,... | collective-permute-start | bytes 196616 | tf_op jit(solution)/shard_map/ppermute | solution.py:745
  80.4 6.2 %collective-permute-start.21 = (bf16[256,128]{1,0:T(8,128)(2,1)S(1)}, bf16[256,128]{1,0:T(8,128)(2,1)S(1)}, u32[]{:S(2)}, u32[]{:S(2)}) collective-permute-start(bf16[256,128]{1,0:T(8,128)(2,1)S(1)} %get-tuple-element.89), channel_id=1, source_target_pairs={{0,6},{1,7},{2,4},{3,5},{4,2},{5,3},{6,0},{7,1},{8,14},{9,15},{10,... | collective-permute-start | bytes 196616 | tf_op jit(solution)/shard_map/ppermute | solution.py:745
  80.6 7.7 %collective-permute-start.22 = (bf16[256,128]{1,0:T(8,128)(2,1)S(1)}, bf16[256,128]{1,0:T(8,128)(2,1)S(1)}, u32[]{:S(2)}, u32[]{:S(2)}) collective-permute-start(bf16[256,128]{1,0:T(8,128)(2,1)S(1)} %get-tuple-element.90), channel_id=1, source_target_pairs={{0,8},{1,9},{2,10},{3,11},{4,12},{5,13},{6,14},{7,15},{8,0},{9,1},... | collective-permute-start | bytes 196616 | tf_op jit(solution)/shard_map/ppermute | solution.py:745
  82.1 12.2 %collective-permute-start.23 = (bf16[256,128]{1,0:T(8,128)(2,1)S(1)}, bf16[256,128]{1,0:T(8,128)(2,1)S(1)}, u32[]{:S(2)}, u32[]{:S(2)}) collective-permute-start(bf16[256,128]{1,0:T(8,128)(2,1)S(1)} %get-tuple-element.91), channel_id=1, source_target_pairs={{0,10},{1,11},{2,8},{3,9},{4,14},{5,15},{6,12},{7,13},{8,2},{9,3},... | collective-permute-start | bytes 196616 | tf_op jit(solution)/shard_map/ppermute | solution.py:745
  84.8 9.5 %collective-permute-start.24 = (bf16[256,128]{1,0:T(8,128)(2,1)S(1)}, bf16[256,128]{1,0:T(8,128)(2,1)S(1)}, u32[]{:S(2)}, u32[]{:S(2)}) collective-permute-start(bf16[256,128]{1,0:T(8,128)(2,1)S(1)} %get-tuple-element.92), channel_id=1, source_target_pairs={{0,12},{1,13},{2,14},{3,15},{4,8},{5,9},{6,10},{7,11},{8,4},{9,5},... | collective-permute-start | bytes 196616 | tf_op jit(solution)/shard_map/ppermute | solution.py:745
  86.6 7.7 %collective-permute-start.25 = (bf16[256,128]{1,0:T(8,128)(2,1)S(1)}, bf16[256,128]{1,0:T(8,128)(2,1)S(1)}, u32[]{:S(2)}, u32[]{:S(2)}) collective-permute-start(bf16[256,128]{1,0:T(8,128)(2,1)S(1)} %get-tuple-element.93), channel_id=1, source_target_pairs={{0,14},{1,15},{2,12},{3,13},{4,10},{5,11},{6,8},{7,9},{8,6},{9,7},... | collective-permute-start | bytes 196616 | tf_op jit(solution)/shard_map/ppermute | solution.py:745
  98.3 6.4 %collective-permute-start.27 = (bf16[64,1152]{1,0:T(8,128)(2,1)S(1)}, bf16[64,1152]{1,0:T(8,128)(2,1)S(1)}, u32[]{:S(2)}, u32[]{:S(2)}) collective-permute-start(bf16[64,1152]{1,0:T(8,128)(2,1)S(1)} %get-tuple-element.99), channel_id=1, source_target_pairs={{0,2},{1,3},{2,0},{3,1},{4,6},{5,7},{6,4},{7,5},{8,10},{9,11},{10,... | collective-permute-start | bytes 442376 | tf_op jit(solution)/shard_map/ppermute | solution.py:764
  98.6 6.2 %collective-permute-start.28 = (bf16[64,1152]{1,0:T(8,128)(2,1)S(1)}, bf16[64,1152]{1,0:T(8,128)(2,1)S(1)}, u32[]{:S(2)}, u32[]{:S(2)}) collective-permute-start(bf16[64,1152]{1,0:T(8,128)(2,1)S(1)} %get-tuple-element.100), channel_id=1, source_target_pairs={{0,3},{1,2},{2,1},{3,0},{4,7},{5,6},{6,5},{7,4},{8,11},{9,10},{10,... | collective-permute-start | bytes 442376 | tf_op jit(solution)/shard_map/ppermute | solution.py:765
  98.6 6.2 %collective-permute-start.29 = (bf16[64,1152]{1,0:T(8,128)(2,1)S(1)}, bf16[64,1152]{1,0:T(8,128)(2,1)S(1)}, u32[]{:S(2)}, u32[]{:S(2)}) collective-permute-start(bf16[64,1152]{1,0:T(8,128)(2,1)S(1)} %get-tuple-element.101), channel_id=1, source_target_pairs={{0,1},{1,0},{2,3},{3,2},{4,5},{5,4},{6,7},{7,6},{8,9},{9,8},{10,11... | collective-permute-start | bytes 442376 | tf_op jit(solution)/shard_map/ppermute | solution.py:766
  105.9 5.5 %collective-permute-start.30 = (bf16[16,1152]{1,0:T(8,128)(2,1)S(1)}, bf16[16,1152]{1,0:T(8,128)(2,1)S(1)}, u32[]{:S(2)}, u32[]{:S(2)}) collective-permute-start(bf16[16,1152]{1,0:T(8,128)(2,1)S(1)} %get-tuple-element.103), channel_id=1, source_target_pairs={{0,4},{1,5},{2,6},{3,7},{4,0},{5,1},{6,2},{7,3},{8,12},{9,13},{10,... | collective-permute-start | bytes 110600 | tf_op jit(solution)/shard_map/ppermute | solution.py:770
  108.9 5.9 %collective-permute-start.31 = (bf16[16,1152]{1,0:T(8,128)(2,1)S(1)}, bf16[16,1152]{1,0:T(8,128)(2,1)S(1)}, u32[]{:S(2)}, u32[]{:S(2)}) collective-permute-start(bf16[16,1152]{1,0:T(8,128)(2,1)S(1)} %get-tuple-element.104), channel_id=1, source_target_pairs={{0,8},{1,9},{2,10},{3,11},{4,12},{5,13},{6,14},{7,15},{8,0},{9,1},... | collective-permute-start | bytes 110600 | tf_op jit(solution)/shard_map/ppermute | solution.py:770
  109.8 5.9 %collective-permute-start.32 = (bf16[16,1152]{1,0:T(8,128)(2,1)S(1)}, bf16[16,1152]{1,0:T(8,128)(2,1)S(1)}, u32[]{:S(2)}, u32[]{:S(2)}) collective-permute-start(bf16[16,1152]{1,0:T(8,128)(2,1)S(1)} %get-tuple-element.105), channel_id=1, source_target_pairs={{0,12},{1,13},{2,14},{3,15},{4,8},{5,9},{6,10},{7,11},{8,4},{9,5},... | collective-permute-start | bytes 110600 | tf_op jit(solution)/shard_map/ppermute | solution.py:770
